TPU v7x, 512 devices: a whole 4x8x8 slice. The times are simulated.
512 devices in a mesh: tensor: 64 (over x, y, core), replica: 8 (over z).
Axes of the slice: x: 4, y: 8, z: 8, core: 2. Of those that a mesh axis runs over, the one named last changes fastest.
Arguments:
- amplitudes: bfloat16 [1024, 64, 128], P('tensor'), may hold values from -6 to 6
- block_slot: int32 [1024], replicated, may hold values from 0 to 1023, each once
- integrals: bfloat16 [1024, 64, 64, 64], P('tensor', 'replica'), may hold values from -0.09375 to 0.09375
- tile_cols: int32 [1024, 64], P('tensor'), may hold values from 0 to 1023, as said below
- irreps: int32 [1024], replicated, may hold values from 0 to 7, as said below
Outputs:
- ladder: float32 [1024, 64, 128], P('tensor', None, 'replica')
Inputs may be any that keep to these rules, and one draw needn't show every extreme that they name: `block_slot`: each block has one slot and each slot one block. `tile_cols`: the tiles of a row that name blocks of the row's own irrep name distinct blocks; other tiles may name any block of another irrep. `irreps`: each irrep labels exactly 128 blocks.
All inputs are finite; a program needn't handle non-finite values.
Results may differ from a plain program's by a relative error of at most 0.0003.
Values may be sent and summed in bfloat16 or wider, within the bound.
No kernel may reach another device: no remote copies, remote signals or barrier semaphores. Data moves between devices by JAX's collectives and lax.ppermute only.
A program may use at most 128 MiB of HBM per device.

v0:
```python
import jax
import jax.numpy as jnp
from jax import lax
from jax.sharding import PartitionSpec as P


def local(amplitudes, block_slot, integrals, tile_cols, irreps):
    blocks = tile_cols.shape[0]
    rep_id = lax.axis_index("replica")
    rows_glob = lax.axis_index("tensor") * blocks + jnp.arange(blocks, dtype=jnp.int32)
    row_irrep = irreps[rows_glob]
    per_rep = integrals.shape[1]
    my_cols = lax.dynamic_slice_in_dim(tile_cols, rep_id * per_rep, per_rep, 1)
    whole = lax.all_gather(amplitudes, "tensor", axis=0, tiled=True)
    picked = whole[block_slot[my_cols]]
    allowed = (irreps[my_cols] == row_irrep[:, None]).astype(jnp.bfloat16)
    tiles = integrals * allowed[:, :, None, None]
    partial_sum = jnp.einsum("bnxy,bnyp->bxp", tiles, picked, preferred_element_type=jnp.float32)
    return lax.psum_scatter(partial_sum, "replica", scatter_dimension=2, tiled=True)


def solution(mesh):
    in_specs = (
        P("tensor", None, None),
        P(),
        P("tensor", "replica", None, None),
        P("tensor", None),
        P(),
    )
    out_specs = P("tensor", None, "replica")
    return jax.shard_map(local, mesh=mesh, in_specs=in_specs, out_specs=out_specs, check_vma=False)
```

profile of v0, /device:TPU:2, one launch (start us, length us, event | category | flops | bytes accessed | tf_op | source)
XLA Modules:
  0.0 177.6 jit_solution(1262501762788884398)
XLA Ops:
  6.5 0.0 copy-start
  6.5 0.0 all-gather.2.cloned.1.call-start
  6.5 0.7 all-gather.2.cloned.1.call-update
  7.3 0.0 reduce-scatter.2.cloned.1.call-start
  7.3 0.8 compare_select_fusion.1
  8.1 0.1 reshape.50
  8.2 0.0 copy-done
  8.2 0.6 gather_fusion.1
  8.9 0.0 copy-start.1
  8.9 1.0 gather_fusion
  9.9 0.0 copy-done.1
  9.9 1.0 gather_fusion.2
  10.8 0.1 reshape.49
  10.9 0.1 gather.17
  11.0 0.1 reshape.74
  11.1 0.1 compare_convert_fusion
  11.2 107.2 %all-gather.2.cloned.1.call-done = bf16[1024,64,128]{2,1,0:T(8,128)(2,1)} async-done(((bf16[16,64,128]{2,1,0:T(8,128)(2,1)}), bf16[1024,64,128]{2,1,0:T(8,128)(2,1)}) %all-gather.2.cloned.1.call-update) | async-done | bytes 16777232 | tf_op jit(solution)/shard_map/all_gather | solution.py:14
  118.4 6.7 %gather_fusion.3 = bf16[128,64,128]{2,1,0:T(8,128)(2,1)S(1)} fusion(bf16[1024,64,128]{2,1,0:T(8,128)(2,1)} %all-gather.2.cloned.1.call-done, s32[1024]{0:T(1024)S(1)} %pad_clamp_fusion), kind=kCustom, calls=%fused_computation.3 | custom fusion | bytes 4194816 | tf_op jit(solution)/shard_map/gather | solution.py:15
  125.2 4.1 %fusion.2 = f32[16,64,128]{1,2,0:T(8,128)} fusion(bf16[16,8,64,128]{3,2,1,0:T(8,128)(2,1)S(1)} %bitcast.9, bf16[16,8,64,64]{3,2,1,0:T(8,128)(2,1)} %param.7, bf16[16,8]{1,0:T(8,128)(2,1)S(1)} %compare_convert_fusion), kind=kOutput, calls=%fused_computation.6 | convolution fusion | flops 134742016 | bytes 3670272 | tf_op jit(solution)/shard_map/bnxy,bnyp->bxp/dot_general | solution.py:18
  129.3 0.0 reduce-scatter.2.cloned.1.call-update
  129.3 41.4 %reduce-scatter.2.cloned.1.call-done = f32[16,64,16]{1,2,0:T(8,128)} async-done(((f32[16,64,128]{1,2,0:T(8,128)}), f32[16,64,16]{1,2,0:T(8,128)}) %reduce-scatter.2.cloned.1.call-update) | async-done | bytes 65552 | tf_op jit(solution)/shard_map/reduce_scatter | solution.py:19
  (5 shorter events, 0.0 us)
Async XLA Ops:
  6.5 1.7 copy-start
  6.5 111.9 %all-gather.2.cloned.1.call-start = ((), (), s32[]{:S(2)}) async-start(), calls=%async_computation.1 | async-start | bytes 17039360 | tf_op jit(solution)/shard_map/all_gather | solution.py:14
  7.3 163.5 %reduce-scatter.2.cloned.1.call-start = ((), (), s32[]{:S(2)}) async-start(), calls=%async_computation.2 | async-start | bytes 1179648 | tf_op jit(solution)/shard_map/reduce_scatter | solution.py:19
  8.9 1.0 copy-start.1
Sparse Core Ops, SparseCore 0:
  10.7 107.6 all-gather.1
  129.4 41.2 reduce-scatter.1
where the time goes:
time: 178 us
  waiting for transfers between devices  149 us (84%)
  between operations  13.5 us (8%)
  local copies, waits for them, and re-layouts  9.65 us (5%)
  matrix products  4.12 us (2%)
    all_gather x1, waiting for transfers between devices, local(): whole = lax.all_gather(amplitudes, 'tensor', axis=0, tiled=True)  107 us
    reduce_scatter x1, waiting for transfers between devices, local(): lax.psum_scatter(partial_sum, 'replica', scatter_dimension=2, tiled=True)  41.4 us
    gather x3, local copies, waits for them, and re-layouts, local(): picked = whole[block_slot[my_cols]]  7.77 us
    dot_general x1, matrix products, local(): jnp.einsum('bnxy,bnyp->bxp', tiles, picked, preferred_element_type=jnp.fl...  4.12 us
  transfers between devices with their start and end apart: 2, of which 2 were waited for; matrix products, arithmetic and copies ran while one was open for 2% of the time, Pallas kernels for 0%

commit v1 on v0

v1 whole, which is shorter than its diff:
```python
import jax
import jax.numpy as jnp
from jax import lax
from jax.experimental import pallas as pl
from jax.experimental.pallas import tpu as pltpu
from jax.sharding import Mesh, PartitionSpec as P

NX, NY, NC, NZ = 4, 8, 2, 8
BLK = 1024
ROWS = 16
PAIRS = ROWS // 2
TILE = 64
SUB = TILE // NZ
PER_Z = 8
OCC = 128
CONTR = NZ * PER_Z * SUB

bf16 = jnp.bfloat16
f32 = jnp.float32


def split_tiles(tiles_ref, out_ref):
    eye = (
        lax.broadcasted_iota(jnp.int32, (TILE, TILE), 0)
        == lax.broadcasted_iota(jnp.int32, (TILE, TILE), 1)
    ).astype(bf16)

    def step(pair, carry):
        for n in range(PER_Z):
            both = jnp.concatenate(
                [tiles_ref[2 * pair, n], tiles_ref[2 * pair + 1, n]], axis=0
            )
            turned = lax.dot_general(
                eye, both, (((1,), (1,)), ((), ())), preferred_element_type=f32
            ).astype(bf16)
            for z in range(NZ):
                out_ref[z, pair, n * SUB : (n + 1) * SUB, :] = turned[
                    z * SUB : (z + 1) * SUB, :
                ]
        return carry

    lax.fori_loop(0, PAIRS, step, 0)


def contract(where_ref, own_hbm, other_hbm, tiles_ref, out_ref, amp, picked, sem):
    half = BLK // NC
    first = pltpu.make_async_copy(own_hbm, amp.at[pl.ds(0, half)], sem.at[0])
    second = pltpu.make_async_copy(other_hbm, amp.at[pl.ds(half, half)], sem.at[1])
    first.start()
    second.start()
    amp[BLK] = jnp.zeros((SUB, OCC), bf16)
    low = lax.broadcasted_iota(jnp.int32, (OCC, OCC), 1) < TILE
    first.wait()
    second.wait()

    def step(pair, carry):
        for parity in range(2):
            for n in range(NZ * PER_Z):
                at = where_ref[2 * pair + parity, n]
                picked[n * SUB : (n + 1) * SUB, parity * OCC : (parity + 1) * OCC] = (
                    amp[at]
                )
        tiles = tiles_ref[:, pair].reshape(CONTR, OCC)
        both = lax.dot_general(
            picked[...], tiles, (((0,), (0,)), ((), ())), preferred_element_type=f32
        )
        out_ref[:, pair] = jnp.where(low, both[:OCC], both[OCC:]).reshape(
            NZ, OCC // NZ, OCC
        )
        return carry

    lax.fori_loop(0, PAIRS, step, 0)


def add_up(parts_ref, out_ref):
    total = parts_ref[0]
    for z in range(1, NZ):
        total = total + parts_ref[z]
    for pair in range(PAIRS):
        out_ref[2 * pair] = total[pair, :, :TILE]
        out_ref[2 * pair + 1] = total[pair, :, TILE:]


def in_vmem(n):
    return [pl.BlockSpec(memory_space=pltpu.VMEM)] * n


def local(amplitudes, block_slot, integrals, tile_cols, irreps):
    x, y = lax.axis_index("x"), lax.axis_index("y")
    core, z = lax.axis_index("core"), lax.axis_index("z")

    part = lax.dynamic_slice_in_dim(amplitudes, z * SUB, SUB, 1)
    along_y = lax.all_to_all(
        jnp.broadcast_to(part, (NY, ROWS, SUB, OCC)), "y", 0, 0, tiled=False
    )
    along_x = lax.all_to_all(
        jnp.broadcast_to(along_y, (NX, NY, ROWS, SUB, OCC)), "x", 0, 0, tiled=False
    )
    own = along_x.reshape(BLK // NC, SUB, OCC)
    other = lax.ppermute(own, "core", [(0, 1), (1, 0)])

    split = pl.pallas_call(
        split_tiles,
        out_shape=jax.ShapeDtypeStruct((NZ, PAIRS, PER_Z * SUB, OCC), bf16),
        in_specs=in_vmem(1),
        out_specs=in_vmem(1)[0],
        cost_estimate=pl.CostEstimate(
            flops=1 << 28, bytes_accessed=3 << 20, transcendentals=0
        ),
        name="split_tiles",
    )(integrals)
    tiles = lax.all_to_all(split, "z", 0, 0, tiled=False)

    first_row = ((x * NY + y) * NC + core) * ROWS
    row_irrep = lax.dynamic_slice_in_dim(irreps, first_row, ROWS, 0)
    slot = block_slot[tile_cols]
    allowed = irreps[tile_cols] == row_irrep[:, None]
    holder = slot // ROWS
    place = (holder // NC) * ROWS + slot % ROWS
    place = place + jnp.where(holder % NC == core, 0, BLK // NC)
    where = jnp.where(allowed, place, BLK)

    sums = pl.pallas_call(
        contract,
        out_shape=jax.ShapeDtypeStruct((NZ, PAIRS, OCC // NZ, OCC), f32),
        in_specs=[
            pl.BlockSpec(memory_space=pltpu.SMEM),
            pl.BlockSpec(memory_space=pl.ANY),
            pl.BlockSpec(memory_space=pl.ANY),
            pl.BlockSpec(memory_space=pltpu.VMEM),
        ],
        out_specs=in_vmem(1)[0],
        scratch_shapes=[
            pltpu.VMEM((BLK + 8, SUB, OCC), bf16),
            pltpu.VMEM((CONTR, 2 * OCC), bf16),
            pltpu.SemaphoreType.DMA((2,)),
        ],
        cost_estimate=pl.CostEstimate(
            flops=1 << 28, bytes_accessed=4 << 20, transcendentals=0
        ),
        name="contract",
    )(where, own, other, tiles)
    parts = lax.all_to_all(sums, "z", 0, 0, tiled=False)

    total = pl.pallas_call(
        add_up,
        out_shape=jax.ShapeDtypeStruct((ROWS, OCC // NZ, TILE), f32),
        in_specs=in_vmem(1),
        out_specs=in_vmem(1)[0],
        name="add_up",
    )(parts)
    return jnp.swapaxes(total, 1, 2)


def solution(mesh):
    fine = Mesh(mesh.devices.reshape(NX, NY, NC, NZ), ("x", "y", "core", "z"))
    tensor = ("x", "y", "core")
    in_specs = (
        P(tensor, None, None),
        P(),
        P(tensor, "z", None, None),
        P(tensor, None),
        P(),
    )
    return jax.shard_map(
        local, mesh=fine, in_specs=in_specs, out_specs=P(tensor, None, "z"), check_vma=False
    )
```

time: 178 us -> 105 us (0.59)
  the two profiles are of different devices: /device:TPU:2 before, /device:TPU:48 now
where the time goes in v1:
time: 105 us
  blocking collectives  35.2 us (34%)
  waiting for transfers between devices  25.1 us (24%)
  starting transfers between devices  16.5 us (16%)
  Pallas kernels  13.6 us (13%)
  local copies, waits for them, and re-layouts  13.5 us (13%)
    all_to_all x1, blocking collectives, local(): parts = lax.all_to_all(sums, 'z', 0, 0, tiled=False)  20.4 us
    all_to_all x1, waiting for transfers between devices, local(): tiles = lax.all_to_all(split, 'z', 0, 0, tiled=False)  15.2 us
    all_to_all x1, blocking collectives, local(): lax.all_to_all(jnp.broadcast_to(part, (NY, ROWS, SUB, OCC)), 'y', 0, 0, t...  14.8 us
    all_to_all x1, starting transfers between devices, local(): tiles = lax.all_to_all(split, 'z', 0, 0, tiled=False)  10.3 us
    all_to_all x1, waiting for transfers between devices, local(): lax.all_to_all(jnp.broadcast_to(along_y, (NX, NY, ROWS, SUB, OCC)), 'x',...  9.83 us
    pallas_call x1, Pallas kernels, local(): pl.pallas_call(contract, out_shape=jax.ShapeDtypeStruct((NZ, PAIRS, OCC /...  6.9 us
    pallas_call x1, Pallas kernels, local(): pl.pallas_call(split_tiles, out_shape=jax.ShapeDtypeStruct((NZ, PAIRS, PE...  4.89 us
    gather x2, local copies, waits for them, and re-layouts, local(): slot = block_slot[tile_cols]  4.6 us
  transfers between devices with their start and end apart: 3, of which 2 were waited for; matrix products, arithmetic and copies ran while one was open for 10% of the time, Pallas kernels for 5%

profile of v1, /device:TPU:48, one launch (start us, length us, event | category | flops | bytes accessed | tf_op | source)
XLA Modules:
  0.0 104.7 jit_solution(15514034798780347266)
XLA Ops:
  0.0 0.0 copy-start
  0.0 0.9 copy-done
  1.0 14.8 %all_to_all.20 = bf16[8,16,8,128]{3,2,1,0:T(8,128)(2,1)S(1)} all-to-all(bf16[8,16,8,128]{3,2,1,0:T(8,128)(2,1)S(1)} %broadcast_in_dim.21), channel_id=1, replica_groups=mesh['x'=4,'y'=8,'core'=2,'z'=8] {'y'}, dimensions={0} | all-to-all | bytes 524288 | tf_op jit(solution)/shard_map/all_to_all | solution.py:93
  15.8 1.2 %broadcast_in_dim.22 = bf16[4,8,16,8,128]{4,3,2,1,0:T(8,128)(2,1)} broadcast(bf16[8,16,8,128]{3,2,1,0:T(8,128)(2,1)S(1)} %all_to_all.20), dimensions={1,2,3,4} | broadcast | bytes 1310720 | tf_op jit(solution)/shard_map/broadcast_in_dim | solution.py:97
  17.1 4.3 %all-to-all-start.1 = ((bf16[4,8,16,8,128]{4,3,2,1,0:T(8,128)(2,1)}), bf16[4,8,16,8,128]{4,3,2,1,0:T(8,128)(2,1)S(1)}, u32[]{:S(2)}, u32[]{:S(2)}) async-start(bf16[4,8,16,8,128]{4,3,2,1,0:T(8,128)(2,1)} %broadcast_in_dim.22), calls=%async_computation.1 | async-start | bytes 2097152 | tf_op jit(solution)/shard_map/all_to_all | solution.py:96
  21.3 4.9 %split_tiles.1 = bf16[8,8,64,128]{3,2,1,0:T(8,128)(2,1)} custom-call(bf16[16,8,64,64]{3,2,1,0:T(8,128)(2,1)} %tiles_ref.1), custom_call_target="tpu_custom_call" | custom-call | flops 268435456 | bytes 3145728 | tf_op jit(solution)/shard_map/split_tiles/pallas_call | solution.py:102
  26.2 9.8 %all-to-all-done.1 = bf16[4,8,16,8,128]{4,3,2,1,0:T(8,128)(2,1)S(1)} async-done(((bf16[4,8,16,8,128]{4,3,2,1,0:T(8,128)(2,1)}), bf16[4,8,16,8,128]{4,3,2,1,0:T(8,128)(2,1)S(1)}, u32[]{:S(2)}, u32[]{:S(2)}) %all-to-all-start.1) | async-done | bytes 1048608 | tf_op jit(solution)/shard_map/all_to_all | solution.py:96
  36.1 10.3 %all-to-all-start.2 = ((bf16[8,8,64,128]{3,2,1,0:T(8,128)(2,1)}), bf16[8,8,64,128]{3,2,1,0:T(8,128)(2,1)S(1)}, u32[]{:S(2)}, u32[]{:S(2)}) async-start(bf16[8,8,64,128]{3,2,1,0:T(8,128)(2,1)} %split_tiles.1), calls=%async_computation.2 | async-start | bytes 2097152 | tf_op jit(solution)/shard_map/all_to_all | solution.py:112
  46.4 1.9 %collective-permute-start = (bf16[512,8,128]{2,1,0:T(8,128)(2,1)S(1)}, bf16[512,8,128]{2,1,0:T(8,128)(2,1)S(1)}, u32[]{:S(2)}, u32[]{:S(2)}) collective-permute-start(bf16[512,8,128]{2,1,0:T(8,128)(2,1)S(1)} %bitcast.2), channel_id=1, source_target_pairs={{0,8},{8,0},{1,9},{9,1},{2,10},{10,2},{3,11},{11,3},{4,12},{12,4},... | collective-permute-start | bytes 3145736 | tf_op jit(solution)/shard_map/ppermute | solution.py:100
  48.3 0.0 copy-done.6
  48.3 0.1 reshape.7
  48.4 0.1 dynamic_slice.6
  48.5 4.5 %gather_fusion = s32[1024]{0:T(1024)S(1)} fusion(s32[1024]{0:T(1024)S(1)} %copy-done.1, s32[1024]{0:T(1024)S(1)} %broadcast_clamp_fusion), kind=kCustom, calls=%fused_computation | custom fusion | bytes 12288 | tf_op jit(solution)/shard_map/gather | solution.py:117
  53.0 4.5 %gather_fusion.1 = s32[1024]{0:T(1024)S(1)} fusion(s32[1024]{0:T(1024)S(1)} %copy-done.2, s32[1024]{0:T(1024)S(1)} %broadcast_clamp_fusion), kind=kCustom, calls=%fused_computation.1 | custom fusion | bytes 12288 | tf_op jit(solution)/shard_map/gather | solution.py:116
  57.6 0.1 reshape.6
  57.6 0.1 reshape.14
  57.7 0.7 fusion.3.where_ref
  58.4 15.2 %all-to-all-done.2.tiles_ref = bf16[8,8,64,128]{3,2,1,0:T(8,128)(2,1)S(1)} async-done(((bf16[8,8,64,128]{3,2,1,0:T(8,128)(2,1)}), bf16[8,8,64,128]{3,2,1,0:T(8,128)(2,1)S(1)}, u32[]{:S(2)}, u32[]{:S(2)}) %all-to-all-start.2) | async-done | bytes 1048608 | tf_op jit(solution)/shard_map/all_to_all | solution.py:112
  73.6 0.0 collective-permute-done.other_hbm
  73.6 1.0 copy-done.4
  74.6 1.0 copy-done.5
  75.6 6.9 %contract.1 = f32[8,8,16,128]{3,2,1,0:T(8,128)} custom-call(s32[16,64]{1,0:T(8,128)} %fusion.3.where_ref, bf16[512,8,128]{2,1,0:T(8,128)(2,1)} %bitcast.3, bf16[512,8,128]{2,1,0:T(8,128)(2,1)} %copy-done.5, bf16[8,8,64,128]{3,2,1,0:T(8,128)(2,1)} %copy-done.4), custom_call_target="tpu_custom_call" | custom-call | flops 268435456 | bytes 4194304 | tf_op jit(solution)/shard_map/contract/pallas_call | solution.py:123
  82.5 20.4 %all_to_all.21.parts_ref = f32[8,8,16,128]{3,2,1,0:T(8,128)} all-to-all(f32[8,8,16,128]{3,2,1,0:T(8,128)} %contract.1), channel_id=1, replica_groups=mesh['x'=4,'y'=8,'core'=2,'z'=8] {'z'}, dimensions={0} | all-to-all | bytes 1048576 | tf_op jit(solution)/shard_map/all_to_all | solution.py:143
  102.9 1.8 %add_up.1 = f32[16,16,64]{2,1,0:T(8,128)} custom-call(f32[8,8,16,128]{3,2,1,0:T(8,128)} %all_to_all.21.parts_ref), custom_call_target="tpu_custom_call" | custom-call | tf_op jit(solution)/shard_map/add_up/pallas_call | solution.py:145
  (13 shorter events, 0.1 us)
Async XLA Ops:
  0.0 1.0 copy-start
  17.1 19.0 %all-to-all-start.1 = ((bf16[4,8,16,8,128]{4,3,2,1,0:T(8,128)(2,1)}), bf16[4,8,16,8,128]{4,3,2,1,0:T(8,128)(2,1)S(1)}, u32[]{:S(2)}, u32[]{:S(2)}) async-start(bf16[4,8,16,8,128]{4,3,2,1,0:T(8,128)(2,1)} %broadcast_in_dim.22), calls=%async_computation.1 | async-start | bytes 2097152 | tf_op jit(solution)/shard_map/all_to_all | solution.py:96
  21.3 27.0 %copy-start.6 = (s32[16,64]{1,0:T(8,128)S(1)}, s32[16,64]{1,0:T(8,128)}, u32[]{:S(2)}) copy-start(s32[16,64]{1,0:T(8,128)} %param.8) | copy-start | bytes 12292
  21.3 27.1 %copy-start.1 = (s32[1024]{0:T(1024)S(1)}, s32[1024]{0:T(1024)}, u32[]{:S(2)}) copy-start(s32[1024]{0:T(1024)} %param.9) | copy-start | bytes 12292
  36.1 17.0 %copy-start.3 = (bf16[4,8,16,8,128]{4,3,2,1,0:T(8,128)(2,1)}, bf16[4,8,16,8,128]{4,3,2,1,0:T(8,128)(2,1)S(1)}, u32[]{:S(2)}) copy-start(bf16[4,8,16,8,128]{4,3,2,1,0:T(8,128)(2,1)S(1)} %all-to-all-done.1) | copy-start | bytes 3145732
  36.1 37.5 %all-to-all-start.2 = ((bf16[8,8,64,128]{3,2,1,0:T(8,128)(2,1)}), bf16[8,8,64,128]{3,2,1,0:T(8,128)(2,1)S(1)}, u32[]{:S(2)}, u32[]{:S(2)}) async-start(bf16[8,8,64,128]{3,2,1,0:T(8,128)(2,1)} %split_tiles.1), calls=%async_computation.2 | async-start | bytes 2097152 | tf_op jit(solution)/shard_map/all_to_all | solution.py:112
  46.4 27.2 %collective-permute-start = (bf16[512,8,128]{2,1,0:T(8,128)(2,1)S(1)}, bf16[512,8,128]{2,1,0:T(8,128)(2,1)S(1)}, u32[]{:S(2)}, u32[]{:S(2)}) collective-permute-start(bf16[512,8,128]{2,1,0:T(8,128)(2,1)S(1)} %bitcast.2), channel_id=1, source_target_pairs={{0,8},{8,0},{1,9},{9,1},{2,10},{10,2},{3,11},{11,3},{4,12},{12,4},... | collective-permute-start | bytes 3145736 | tf_op jit(solution)/shard_map/ppermute | solution.py:100
  48.5 4.5 %copy-start.2 = (s32[1024]{0:T(1024)S(1)}, s32[1024]{0:T(1024)}, u32[]{:S(2)}) copy-start(s32[1024]{0:T(1024)} %param.6) | copy-start | bytes 12292
  73.6 1.0 copy-start.4
  74.6 1.0 copy-start.5

commit v2 on v1

v2 whole, which is shorter than its diff:
```python
import jax
import jax.numpy as jnp
from jax import lax
from jax.experimental import pallas as pl
from jax.experimental.pallas import tpu as pltpu
from jax.sharding import Mesh, PartitionSpec as P


NX, NY, NC, NZ = 4, 8, 2, 8
BLK = 1024
ROWS = 16
PAIRS = ROWS // 2
TILE = 64
SUB = TILE // NZ
PER_Z = 8
OCC = 128
VMEM = 16 << 20
CONTR = NZ * PER_Z * SUB

bf16 = jnp.bfloat16
f32 = jnp.float32


def split_tiles(tiles_ref, out_ref):
    eye = (
        lax.broadcasted_iota(jnp.int32, (TILE, TILE), 0)
        == lax.broadcasted_iota(jnp.int32, (TILE, TILE), 1)
    ).astype(bf16)

    def step(pair, carry):
        for n in range(PER_Z):
            both = jnp.concatenate(
                [tiles_ref[2 * pair, n], tiles_ref[2 * pair + 1, n]], axis=0
            )
            turned = lax.dot_general(
                eye, both, (((1,), (1,)), ((), ())), preferred_element_type=f32
            ).astype(bf16)
            for z in range(NZ):
                out_ref[z, pair, n * SUB : (n + 1) * SUB, :] = turned[
                    z * SUB : (z + 1) * SUB, :
                ]
        return carry

    lax.fori_loop(0, PAIRS, step, 0)


def pick(where_ref, *refs):
    pieces, out_ref, amp, sem = refs[:-3], *refs[-3:]
    size = BLK // len(pieces)
    copies = [
        pltpu.make_async_copy(piece, amp.at[pl.ds(k * size, size)], sem.at[k])
        for k, piece in enumerate(pieces)
    ]
    for copy in copies:
        copy.start()
    amp[BLK] = jnp.zeros((SUB, OCC), bf16)
    for copy in copies:
        copy.wait()

    def step(pair, carry):
        for parity in range(2):
            for n in range(NZ * PER_Z):
                at = where_ref[2 * pair + parity, n]
                out_ref[
                    pair, n * SUB : (n + 1) * SUB, parity * OCC : (parity + 1) * OCC
                ] = amp[at]
        return carry

    lax.fori_loop(0, PAIRS, step, 0)


def contract(picked_ref, tiles_ref, out_ref):
    low = lax.broadcasted_iota(jnp.int32, (OCC, OCC), 1) < TILE
    for pair in range(PAIRS):
        tiles = tiles_ref[:, pair].reshape(CONTR, OCC)
        both = lax.dot_general(
            picked_ref[pair], tiles, (((0,), (0,)), ((), ())), preferred_element_type=f32
        )
        out_ref[:, pair] = jnp.where(low, both[:OCC], both[OCC:]).reshape(
            NZ, OCC // NZ, OCC
        )


def add_up(parts_ref, out_ref):
    total = parts_ref[0]
    for z in range(1, NZ):
        total = total + parts_ref[z]
    for pair in range(PAIRS):
        out_ref[2 * pair] = total[pair, :, :TILE]
        out_ref[2 * pair + 1] = total[pair, :, TILE:]


def in_vmem(n):
    return [pl.BlockSpec(memory_space=pltpu.VMEM)] * n


def cost(mib):
    return pl.CostEstimate(
        flops=1 << 28, bytes_accessed=mib << 20, transcendentals=0
    )


def local(amplitudes, block_slot, integrals, tile_cols, irreps):
    x, y = lax.axis_index("x"), lax.axis_index("y")
    core, z = lax.axis_index("core"), lax.axis_index("z")

    part = lax.dynamic_slice_in_dim(amplitudes, z * SUB, SUB, 1)
    to_y = jnp.broadcast_to(part, (NY, ROWS, SUB, OCC))
    along_y = lax.all_to_all(to_y, "y", 0, 0, tiled=False)
    own = [along_y.reshape(NY * ROWS, SUB, OCC)]
    for k in (1, 2, 3):
        shift = [((i + k) % NX, i) for i in range(NX)]
        own.append(lax.ppermute(own[0], "x", shift))
    other = []
    for piece in own:
        other.append(lax.ppermute(piece, "core", [(0, 1), (1, 0)]))

    split = pl.pallas_call(
        split_tiles,
        out_shape=jax.ShapeDtypeStruct((NZ, PAIRS, PER_Z * SUB, OCC), bf16),
        in_specs=in_vmem(1),
        out_specs=in_vmem(1)[0],
        compiler_params=pltpu.CompilerParams(vmem_limit_bytes=VMEM),
        cost_estimate=cost(3),
        name="split_tiles",
    )(integrals)
    tiles = lax.all_to_all(split, "z", 0, 0, tiled=False)

    table = block_slot * 8 + irreps
    first_row = ((x * NY + y) * NC + core) * ROWS
    row_irrep = lax.dynamic_slice_in_dim(irreps, first_row, ROWS, 0)
    found = table[tile_cols]
    slot, labels = found // 8, found % 8
    allowed = labels == row_irrep[:, None]
    holder = slot // ROWS
    holder_x, holder_y = holder // (NY * NC), (holder // NC) % NY
    place = ((holder_x - x) % NX) * NY + holder_y + (holder + core) % NC * (NX * NY)
    where = jnp.where(allowed, place * ROWS + slot % ROWS, BLK)

    picked = pl.pallas_call(
        pick,
        out_shape=jax.ShapeDtypeStruct((PAIRS, CONTR, 2 * OCC), bf16),
        in_specs=[pl.BlockSpec(memory_space=pltpu.SMEM)]
        + [pl.BlockSpec(memory_space=pl.ANY)] * (NX * NC),
        out_specs=in_vmem(1)[0],
        scratch_shapes=[
            pltpu.VMEM((BLK + 8, SUB, OCC), bf16),
            pltpu.SemaphoreType.DMA((NX * NC,)),
        ],
        compiler_params=pltpu.CompilerParams(vmem_limit_bytes=VMEM),
        cost_estimate=cost(6),
        name="pick",
    )(where, *own, *other)
    sums = pl.pallas_call(
        contract,
        out_shape=jax.ShapeDtypeStruct((NZ, PAIRS, OCC // NZ, OCC), f32),
        in_specs=in_vmem(2),
        out_specs=in_vmem(1)[0],
        compiler_params=pltpu.CompilerParams(vmem_limit_bytes=VMEM),
        cost_estimate=cost(4),
        name="contract",
    )(picked, tiles)
    parts = lax.all_to_all(sums, "z", 0, 0, tiled=False)

    total = pl.pallas_call(
        add_up,
        out_shape=jax.ShapeDtypeStruct((ROWS, OCC // NZ, TILE), f32),
        in_specs=in_vmem(1),
        out_specs=in_vmem(1)[0],
        compiler_params=pltpu.CompilerParams(vmem_limit_bytes=VMEM),
        cost_estimate=cost(1),
        name="add_up",
    )(parts)
    return jnp.swapaxes(total, 1, 2)


def solution(mesh):
    fine = Mesh(mesh.devices.reshape(NX, NY, NC, NZ), ("x", "y", "core", "z"))
    tensor = ("x", "y", "core")
    in_specs = (
        P(tensor, None, None),
        P(),
        P(tensor, "z", None, None),
        P(tensor, None),
        P(),
    )

    return jax.shard_map(
        local,
        mesh=fine,
        in_specs=in_specs,
        out_specs=P(tensor, None, "z"),
        check_vma=False,
    )
```

time: 105 us -> 95.9 us (0.913)
  the two profiles are of different devices: /device:TPU:48 before, /device:TPU:2 now
where the time goes in v2:
time: 95.9 us; the launch traced here: 94.9 us
  starting transfers between devices  36 us (38%)
  blocking collectives  24.9 us (26%)
  local copies, waits for them, and re-layouts  18.5 us (19%)
  waiting for transfers between devices  8.42 us (9%)
  Pallas kernels  6.77 us (7%)
    all_to_all x1, blocking collectives, local(): parts = lax.all_to_all(sums, 'z', 0, 0, tiled=False)  24.9 us
    unnamed x42, local copies, waits for them, and re-layouts  13 us
    ppermute x3, starting transfers between devices, local(): own.append(lax.ppermute(own[0], 'x', shift))  10.5 us
    all_to_all x1, starting transfers between devices, local(): tiles = lax.all_to_all(split, 'z', 0, 0, tiled=False)  10.3 us
    ppermute x4, starting transfers between devices, local(): other.append(lax.ppermute(piece, 'core', [(0, 1), (1, 0)]))  8.13 us
    all_to_all x1, starting transfers between devices, local(): along_y = lax.all_to_all(to_y, 'y', 0, 0, tiled=False)  7.1 us
    all_to_all x1, waiting for transfers between devices, local(): along_y = lax.all_to_all(to_y, 'y', 0, 0, tiled=False)  7.03 us
    gather x2, local copies, waits for them, and re-layouts, local(): found = table[tile_cols]  4.59 us
  transfers between devices with their start and end apart: 9, of which 3 were waited for; matrix products, arithmetic and copies ran while one was open for 5% of the time, Pallas kernels for 6%

profile of v2, /device:TPU:2, one launch (start us, length us, event | category | flops | bytes accessed | tf_op | source)
XLA Modules:
  0.0 94.9 jit_solution(1627560297126434834)
XLA Ops:
  0.0 0.9 copy-done
  1.7 7.1 %all-to-all-start = ((bf16[8,16,8,128]{3,2,1,0:T(8,128)(2,1)}), bf16[8,16,8,128]{3,2,1,0:T(8,128)(2,1)S(1)}, u32[]{:S(2)}, u32[]{:S(2)}) async-start(bf16[8,16,8,128]{3,2,1,0:T(8,128)(2,1)} %broadcast_in_dim.10), calls=%async_computation | async-start | bytes 524288 | tf_op jit(solution)/shard_map/all_to_all | solution.py:109
  8.8 1.6 %copy-done.1 = bf16[16,8,64,64]{3,2,1,0:T(8,128)(2,1)S(1)} copy-done((bf16[16,8,64,64]{3,2,1,0:T(8,128)(2,1)S(1)}, bf16[16,8,64,64]{3,2,1,0:T(8,128)(2,1)}, u32[]{:S(2)}) %copy-start.1) | copy-done | bytes 1048600
  10.4 3.3 %split_tiles.1 = bf16[8,8,64,128]{3,2,1,0:T(8,128)(2,1)} custom-call(bf16[16,8,64,64]{3,2,1,0:T(8,128)(2,1)S(1)} %copy-done.1), custom_call_target="tpu_custom_call" | custom-call | flops 268435456 | bytes 3145728 | tf_op jit(solution)/shard_map/split_tiles/pallas_call | solution.py:118
  13.7 7.0 %all-to-all-done = bf16[8,16,8,128]{3,2,1,0:T(8,128)(2,1)S(1)} async-done(((bf16[8,16,8,128]{3,2,1,0:T(8,128)(2,1)}), bf16[8,16,8,128]{3,2,1,0:T(8,128)(2,1)S(1)}, u32[]{:S(2)}, u32[]{:S(2)}) %all-to-all-start) | async-done | bytes 262176 | tf_op jit(solution)/shard_map/all_to_all | solution.py:109
  20.7 10.3 %all-to-all-start.1 = ((bf16[8,8,64,128]{3,2,1,0:T(8,128)(2,1)}), bf16[8,8,64,128]{3,2,1,0:T(8,128)(2,1)S(1)}, u32[]{:S(2)}, u32[]{:S(2)}) async-start(bf16[8,8,64,128]{3,2,1,0:T(8,128)(2,1)} %split_tiles.1), calls=%async_computation.1 | async-start | bytes 2097152 | tf_op jit(solution)/shard_map/all_to_all | solution.py:127
  31.0 3.4 %collective-permute-start.2 = (bf16[128,8,128]{2,1,0:T(8,128)(2,1)S(1)}, bf16[128,8,128]{2,1,0:T(8,128)(2,1)S(1)}, u32[]{:S(2)}, u32[]{:S(2)}) collective-permute-start(bf16[128,8,128]{2,1,0:T(8,128)(2,1)S(1)} %bitcast.2), channel_id=1, source_target_pairs={{384,0},{0,128},{128,256},{256,384},{385,1},{1,129},{129,257},{257... | collective-permute-start | bytes 786440 | tf_op jit(solution)/shard_map/ppermute | solution.py:113
  34.4 3.0 %collective-permute-start.1 = (bf16[128,8,128]{2,1,0:T(8,128)(2,1)S(1)}, bf16[128,8,128]{2,1,0:T(8,128)(2,1)S(1)}, u32[]{:S(2)}, u32[]{:S(2)}) collective-permute-start(bf16[128,8,128]{2,1,0:T(8,128)(2,1)S(1)} %bitcast.3), channel_id=1, source_target_pairs={{256,0},{384,128},{0,256},{128,384},{257,1},{385,129},{1,257},{129... | collective-permute-start | bytes 786440 | tf_op jit(solution)/shard_map/ppermute | solution.py:113
  37.4 4.1 %collective-permute-start = (bf16[128,8,128]{2,1,0:T(8,128)(2,1)S(1)}, bf16[128,8,128]{2,1,0:T(8,128)(2,1)S(1)}, u32[]{:S(2)}, u32[]{:S(2)}) collective-permute-start(bf16[128,8,128]{2,1,0:T(8,128)(2,1)S(1)} %bitcast.4), channel_id=1, source_target_pairs={{128,0},{256,128},{384,256},{0,384},{129,1},{257,129},{385,257},{1... | collective-permute-start | bytes 786440 | tf_op jit(solution)/shard_map/ppermute | solution.py:113
  41.6 1.9 %collective-permute-start.3 = (bf16[128,8,128]{2,1,0:T(8,128)(2,1)S(1)}, bf16[128,8,128]{2,1,0:T(8,128)(2,1)S(1)}, u32[]{:S(2)}, u32[]{:S(2)}) collective-permute-start(bf16[128,8,128]{2,1,0:T(8,128)(2,1)S(1)} %bitcast.5), channel_id=1, source_target_pairs={{0,8},{8,0},{1,9},{9,1},{2,10},{10,2},{3,11},{11,3},{4,12},{12,4},... | collective-permute-start | bytes 786440 | tf_op jit(solution)/shard_map/ppermute | solution.py:116
  43.5 2.4 %collective-permute-start.6 = (bf16[128,8,128]{2,1,0:T(8,128)(2,1)S(1)}, bf16[128,8,128]{2,1,0:T(8,128)(2,1)S(1)}, u32[]{:S(2)}, u32[]{:S(2)}) collective-permute-start(bf16[128,8,128]{2,1,0:T(8,128)(2,1)S(1)} %collective-permute-done.2.refs_3_), channel_id=1, source_target_pairs={{0,8},{8,0},{1,9},{9,1},{2,10},{10,2},{3,11},{11,3},{4,12},{12,4},... | collective-permute-start | bytes 786440 | tf_op jit(solution)/shard_map/ppermute | solution.py:116
  46.5 1.9 %collective-permute-start.5 = (bf16[128,8,128]{2,1,0:T(8,128)(2,1)S(1)}, bf16[128,8,128]{2,1,0:T(8,128)(2,1)S(1)}, u32[]{:S(2)}, u32[]{:S(2)}) collective-permute-start(bf16[128,8,128]{2,1,0:T(8,128)(2,1)S(1)} %collective-permute-done.1.refs_2_), channel_id=1, source_target_pairs={{0,8},{8,0},{1,9},{9,1},{2,10},{10,2},{3,11},{11,3},{4,12},{12,4},... | collective-permute-start | bytes 786440 | tf_op jit(solution)/shard_map/ppermute | solution.py:116
  49.2 1.9 %collective-permute-start.4 = (bf16[128,8,128]{2,1,0:T(8,128)(2,1)S(1)}, bf16[128,8,128]{2,1,0:T(8,128)(2,1)S(1)}, u32[]{:S(2)}, u32[]{:S(2)}) collective-permute-start(bf16[128,8,128]{2,1,0:T(8,128)(2,1)S(1)} %collective-permute-done.refs_1_), channel_id=1, source_target_pairs={{0,8},{8,0},{1,9},{9,1},{2,10},{10,2},{3,11},{11,3},{4,12},{12,4},... | collective-permute-start | bytes 786440 | tf_op jit(solution)/shard_map/ppermute | solution.py:116
  51.3 4.5 %gather_fusion = s32[1024]{0:T(1024)S(1)} fusion(s32[1024]{0:T(1024)S(1)} %get-tuple-element.5, s32[1024]{0:T(1024)S(1)} %get-tuple-element.6), kind=kCustom, calls=%fused_computation | custom fusion | bytes 12288 | tf_op jit(solution)/shard_map/gather | solution.py:132
  58.9 0.9 copy-done.3
  59.8 0.9 copy-done.5
  60.8 0.9 copy-done.7
  61.7 0.9 copy-done.9
  62.7 0.9 copy-done.11
  63.6 0.9 copy-done.13
  64.6 0.9 copy-done.15
  65.5 0.9 copy-done.17
  66.5 2.0 %pick.1.picked_ref = bf16[8,512,256]{2,1,0:T(8,128)(2,1)S(1)} custom-call(s32[16,64]{1,0:T(8,128)S(1)} %fusion.9.where_ref, bf16[128,8,128]{2,1,0:T(8,128)(2,1)S(1)} %bitcast.6, bf16[128,8,128]{2,1,0:T(8,128)(2,1)S(1)} %copy-done.9, bf16[128,8,128]{2,1,0:T(8,128)(2,1)S(1)} %copy-done.7, bf16[128,8,128]{2,1,0:T(8,128)(2,1)S(1)} %copy-done.5, ...), custom_call_target="tpu_custom_call" | custom-call | flops 268435456 | bytes 6291456 | tf_op jit(solution)/shard_map/pick/pallas_call | solution.py:140
  69.3 24.9 %all_to_all.15.parts_ref = f32[8,8,16,128]{3,2,1,0:T(8,128)S(1)} all-to-all(f32[8,8,16,128]{3,2,1,0:T(8,128)S(1)} %contract.1), channel_id=1, replica_groups=mesh['x'=4,'y'=8,'core'=2,'z'=8] {'z'}, dimensions={0} | all-to-all | bytes 1048576 | tf_op jit(solution)/shard_map/all_to_all | solution.py:163
  (50 shorter events, 6.9 us)
Async XLA Ops:
  0.0 1.0 %copy-start = (bf16[16,64,128]{2,1,0:T(8,128)(2,1)S(1)}, bf16[16,64,128]{2,1,0:T(8,128)(2,1)}, u32[]{:S(2)}) copy-start(bf16[16,64,128]{2,1,0:T(8,128)(2,1)} %param.5) | copy-start | bytes 786436
  1.7 19.0 %all-to-all-start = ((bf16[8,16,8,128]{3,2,1,0:T(8,128)(2,1)}), bf16[8,16,8,128]{3,2,1,0:T(8,128)(2,1)S(1)}, u32[]{:S(2)}, u32[]{:S(2)}) async-start(bf16[8,16,8,128]{3,2,1,0:T(8,128)(2,1)} %broadcast_in_dim.10), calls=%async_computation | async-start | bytes 524288 | tf_op jit(solution)/shard_map/all_to_all | solution.py:109
  8.8 1.6 %copy-start.1 = (bf16[16,8,64,64]{3,2,1,0:T(8,128)(2,1)S(1)}, bf16[16,8,64,64]{3,2,1,0:T(8,128)(2,1)}, u32[]{:S(2)}) copy-start(bf16[16,8,64,64]{3,2,1,0:T(8,128)(2,1)} %tiles_ref.1) | copy-start | bytes 3145732
  10.4 31.1 %copy-start.18 = (s32[16,64]{1,0:T(8,128)S(1)}, s32[16,64]{1,0:T(8,128)}, u32[]{:S(2)}) copy-start(s32[16,64]{1,0:T(8,128)} %param.8) | copy-start | bytes 12292
  10.4 40.8 %copy-start.19 = (s32[1024]{0:T(1024)S(1)}, s32[1024]{0:T(1024)}, u32[]{:S(2)}) copy-start(s32[1024]{0:T(1024)} %param.6) | copy-start | bytes 12292
  10.4 40.8 %copy-start.20 = (s32[1024]{0:T(1024)S(1)}, s32[1024]{0:T(1024)}, u32[]{:S(2)}) copy-start(s32[1024]{0:T(1024)} %param.9) | copy-start | bytes 12292
  20.7 35.1 %copy-start.2 = (bf16[8,16,8,128]{3,2,1,0:T(8,128)(2,1)}, bf16[8,16,8,128]{3,2,1,0:T(8,128)(2,1)S(1)}, u32[]{:S(2)}) copy-start(bf16[8,16,8,128]{3,2,1,0:T(8,128)(2,1)S(1)} %all-to-all-done) | copy-start | bytes 786436
  20.7 47.8 %all-to-all-start.1 = ((bf16[8,8,64,128]{3,2,1,0:T(8,128)(2,1)}), bf16[8,8,64,128]{3,2,1,0:T(8,128)(2,1)S(1)}, u32[]{:S(2)}, u32[]{:S(2)}) async-start(bf16[8,8,64,128]{3,2,1,0:T(8,128)(2,1)} %split_tiles.1), calls=%async_computation.1 | async-start | bytes 2097152 | tf_op jit(solution)/shard_map/all_to_all | solution.py:127
  31.0 12.5 %collective-permute-start.2 = (bf16[128,8,128]{2,1,0:T(8,128)(2,1)S(1)}, bf16[128,8,128]{2,1,0:T(8,128)(2,1)S(1)}, u32[]{:S(2)}, u32[]{:S(2)}) collective-permute-start(bf16[128,8,128]{2,1,0:T(8,128)(2,1)S(1)} %bitcast.2), channel_id=1, source_target_pairs={{384,0},{0,128},{128,256},{256,384},{385,1},{1,129},{129,257},{257... | collective-permute-start | bytes 786440 | tf_op jit(solution)/shard_map/ppermute | solution.py:113
  34.4 12.1 %collective-permute-start.1 = (bf16[128,8,128]{2,1,0:T(8,128)(2,1)S(1)}, bf16[128,8,128]{2,1,0:T(8,128)(2,1)S(1)}, u32[]{:S(2)}, u32[]{:S(2)}) collective-permute-start(bf16[128,8,128]{2,1,0:T(8,128)(2,1)S(1)} %bitcast.3), channel_id=1, source_target_pairs={{256,0},{384,128},{0,256},{128,384},{257,1},{385,129},{1,257},{129... | collective-permute-start | bytes 786440 | tf_op jit(solution)/shard_map/ppermute | solution.py:113
  37.4 11.8 %collective-permute-start = (bf16[128,8,128]{2,1,0:T(8,128)(2,1)S(1)}, bf16[128,8,128]{2,1,0:T(8,128)(2,1)S(1)}, u32[]{:S(2)}, u32[]{:S(2)}) collective-permute-start(bf16[128,8,128]{2,1,0:T(8,128)(2,1)S(1)} %bitcast.4), channel_id=1, source_target_pairs={{128,0},{256,128},{384,256},{0,384},{129,1},{257,129},{385,257},{1... | collective-permute-start | bytes 786440 | tf_op jit(solution)/shard_map/ppermute | solution.py:113
  41.6 14.4 %collective-permute-start.3 = (bf16[128,8,128]{2,1,0:T(8,128)(2,1)S(1)}, bf16[128,8,128]{2,1,0:T(8,128)(2,1)S(1)}, u32[]{:S(2)}, u32[]{:S(2)}) collective-permute-start(bf16[128,8,128]{2,1,0:T(8,128)(2,1)S(1)} %bitcast.5), channel_id=1, source_target_pairs={{0,8},{8,0},{1,9},{9,1},{2,10},{10,2},{3,11},{11,3},{4,12},{12,4},... | collective-permute-start | bytes 786440 | tf_op jit(solution)/shard_map/ppermute | solution.py:116
  43.5 12.3 %copy-start.4 = (bf16[128,8,128]{2,1,0:T(8,128)(2,1)}, bf16[128,8,128]{2,1,0:T(8,128)(2,1)S(1)}, u32[]{:S(2)}) copy-start(bf16[128,8,128]{2,1,0:T(8,128)(2,1)S(1)} %collective-permute-done.2.refs_3_) | copy-start | bytes 786436
  43.5 13.2 %collective-permute-start.6 = (bf16[128,8,128]{2,1,0:T(8,128)(2,1)S(1)}, bf16[128,8,128]{2,1,0:T(8,128)(2,1)S(1)}, u32[]{:S(2)}, u32[]{:S(2)}) collective-permute-start(bf16[128,8,128]{2,1,0:T(8,128)(2,1)S(1)} %collective-permute-done.2.refs_3_), channel_id=1, source_target_pairs={{0,8},{8,0},{1,9},{9,1},{2,10},{10,2},{3,11},{11,3},{4,12},{12,4},... | collective-permute-start | bytes 786440 | tf_op jit(solution)/shard_map/ppermute | solution.py:116
  46.5 9.3 %copy-start.6 = (bf16[128,8,128]{2,1,0:T(8,128)(2,1)}, bf16[128,8,128]{2,1,0:T(8,128)(2,1)S(1)}, u32[]{:S(2)}) copy-start(bf16[128,8,128]{2,1,0:T(8,128)(2,1)S(1)} %collective-permute-done.1.refs_2_) | copy-start | bytes 786436
  46.5 10.9 %collective-permute-start.5 = (bf16[128,8,128]{2,1,0:T(8,128)(2,1)S(1)}, bf16[128,8,128]{2,1,0:T(8,128)(2,1)S(1)}, u32[]{:S(2)}, u32[]{:S(2)}) collective-permute-start(bf16[128,8,128]{2,1,0:T(8,128)(2,1)S(1)} %collective-permute-done.1.refs_2_), channel_id=1, source_target_pairs={{0,8},{8,0},{1,9},{9,1},{2,10},{10,2},{3,11},{11,3},{4,12},{12,4},... | collective-permute-start | bytes 786440 | tf_op jit(solution)/shard_map/ppermute | solution.py:116
  49.2 6.6 %copy-start.8 = (bf16[128,8,128]{2,1,0:T(8,128)(2,1)}, bf16[128,8,128]{2,1,0:T(8,128)(2,1)S(1)}, u32[]{:S(2)}) copy-start(bf16[128,8,128]{2,1,0:T(8,128)(2,1)S(1)} %collective-permute-done.refs_1_) | copy-start | bytes 786436
  49.2 8.9 %collective-permute-start.4 = (bf16[128,8,128]{2,1,0:T(8,128)(2,1)S(1)}, bf16[128,8,128]{2,1,0:T(8,128)(2,1)S(1)}, u32[]{:S(2)}, u32[]{:S(2)}) collective-permute-start(bf16[128,8,128]{2,1,0:T(8,128)(2,1)S(1)} %collective-permute-done.refs_1_), channel_id=1, source_target_pairs={{0,8},{8,0},{1,9},{9,1},{2,10},{10,2},{3,11},{11,3},{4,12},{12,4},... | collective-permute-start | bytes 786440 | tf_op jit(solution)/shard_map/ppermute | solution.py:116
  58.9 0.9 %copy-start.3 = (bf16[8,16,8,128]{3,2,1,0:T(8,128)(2,1)S(1)}, bf16[8,16,8,128]{3,2,1,0:T(8,128)(2,1)}, u32[]{:S(2)}) copy-start(bf16[8,16,8,128]{3,2,1,0:T(8,128)(2,1)} %copy-done.2) | copy-start | bytes 786436
  59.8 0.9 %copy-start.5 = (bf16[128,8,128]{2,1,0:T(8,128)(2,1)S(1)}, bf16[128,8,128]{2,1,0:T(8,128)(2,1)}, u32[]{:S(2)}) copy-start(bf16[128,8,128]{2,1,0:T(8,128)(2,1)} %copy-done.4) | copy-start | bytes 786436
  60.8 0.9 %copy-start.7 = (bf16[128,8,128]{2,1,0:T(8,128)(2,1)S(1)}, bf16[128,8,128]{2,1,0:T(8,128)(2,1)}, u32[]{:S(2)}) copy-start(bf16[128,8,128]{2,1,0:T(8,128)(2,1)} %copy-done.6) | copy-start | bytes 786436
  61.7 0.9 %copy-start.9 = (bf16[128,8,128]{2,1,0:T(8,128)(2,1)S(1)}, bf16[128,8,128]{2,1,0:T(8,128)(2,1)}, u32[]{:S(2)}) copy-start(bf16[128,8,128]{2,1,0:T(8,128)(2,1)} %copy-done.8) | copy-start | bytes 786436
  62.7 0.9 %copy-start.11 = (bf16[128,8,128]{2,1,0:T(8,128)(2,1)S(1)}, bf16[128,8,128]{2,1,0:T(8,128)(2,1)}, u32[]{:S(2)}) copy-start(bf16[128,8,128]{2,1,0:T(8,128)(2,1)} %copy-done.10) | copy-start | bytes 786436
  63.6 0.9 %copy-start.13 = (bf16[128,8,128]{2,1,0:T(8,128)(2,1)S(1)}, bf16[128,8,128]{2,1,0:T(8,128)(2,1)}, u32[]{:S(2)}) copy-start(bf16[128,8,128]{2,1,0:T(8,128)(2,1)} %copy-done.12) | copy-start | bytes 786436
  (6 other events, 4.8 us)

commit v3 on v2

--- a/solution.py
+++ b/solution.py
@@ -11,6 +11,7 @@
 ROWS = 16
 PAIRS = ROWS // 2
 TILE = 64
+NIRR = 8
 SUB = TILE // NZ
 PER_Z = 8
 OCC = 128
@@ -44,6 +45,21 @@
     lax.fori_loop(0, PAIRS, step, 0)
 
 
+def find(table_ref, row_irrep_ref, cols_ref, out_ref):
+    def step(row, carry):
+        irrep = row_irrep_ref[row]
+        for n in range(NZ * PER_Z):
+            entry = table_ref[cols_ref[row, n]]
+            out_ref[row, n] = jnp.where(
+                jnp.bitwise_and(entry, NIRR - 1) == irrep,
+                lax.shift_right_logical(entry, 3),
+                BLK,
+            )
+        return carry
+
+    lax.fori_loop(0, ROWS, step, 0)
+
+
 def pick(where_ref, *refs):
     pieces, out_ref, amp, sem = refs[:-3], *refs[-3:]
     size = BLK // len(pieces)
@@ -105,15 +121,13 @@
     core, z = lax.axis_index("core"), lax.axis_index("z")
 
     part = lax.dynamic_slice_in_dim(amplitudes, z * SUB, SUB, 1)
-    to_y = jnp.broadcast_to(part, (NY, ROWS, SUB, OCC))
-    along_y = lax.all_to_all(to_y, "y", 0, 0, tiled=False)
-    own = [along_y.reshape(NY * ROWS, SUB, OCC)]
+    along_y = lax.all_gather(part, "y", axis=0, tiled=True)
+    pieces = [along_y]
     for k in (1, 2, 3):
         shift = [((i + k) % NX, i) for i in range(NX)]
-        own.append(lax.ppermute(own[0], "x", shift))
-    other = []
-    for piece in own:
-        other.append(lax.ppermute(piece, "core", [(0, 1), (1, 0)]))
+        pieces.append(lax.ppermute(along_y, "x", shift))
+    own = jnp.concatenate(pieces, axis=0)
+    other = lax.ppermute(own, "core", [(0, 1), (1, 0)])
 
     split = pl.pallas_call(
         split_tiles,
@@ -126,31 +140,36 @@
     )(integrals)
     tiles = lax.all_to_all(split, "z", 0, 0, tiled=False)
 
-    table = block_slot * 8 + irreps
+    holder = block_slot // ROWS
+    holder_x, holder_y = holder // (NY * NC), (holder // NC) % NY
+    place = ((holder_x - x) % NX) * NY + holder_y + (holder + core) % NC * (NX * NY)
+    table = (place * ROWS + block_slot % ROWS) * NIRR + irreps
     first_row = ((x * NY + y) * NC + core) * ROWS
     row_irrep = lax.dynamic_slice_in_dim(irreps, first_row, ROWS, 0)
-    found = table[tile_cols]
-    slot, labels = found // 8, found % 8
-    allowed = labels == row_irrep[:, None]
-    holder = slot // ROWS
-    holder_x, holder_y = holder // (NY * NC), (holder // NC) % NY
-    place = ((holder_x - x) % NX) * NY + holder_y + (holder + core) % NC * (NX * NY)
-    where = jnp.where(allowed, place * ROWS + slot % ROWS, BLK)
+    where = pl.pallas_call(
+        find,
+        out_shape=jax.ShapeDtypeStruct((ROWS, NZ * PER_Z), jnp.int32),
+        in_specs=[pl.BlockSpec(memory_space=pltpu.SMEM)] * 3,
+        out_specs=pl.BlockSpec(memory_space=pltpu.SMEM),
+        compiler_params=pltpu.CompilerParams(vmem_limit_bytes=VMEM),
+        cost_estimate=cost(1),
+        name="find",
+    )(table, row_irrep, tile_cols)
 
     picked = pl.pallas_call(
         pick,
         out_shape=jax.ShapeDtypeStruct((PAIRS, CONTR, 2 * OCC), bf16),
         in_specs=[pl.BlockSpec(memory_space=pltpu.SMEM)]
-        + [pl.BlockSpec(memory_space=pl.ANY)] * (NX * NC),
+        + [pl.BlockSpec(memory_space=pl.ANY)] * NC,
         out_specs=in_vmem(1)[0],
         scratch_shapes=[
             pltpu.VMEM((BLK + 8, SUB, OCC), bf16),
-            pltpu.SemaphoreType.DMA((NX * NC,)),
+            pltpu.SemaphoreType.DMA((NC,)),
         ],
         compiler_params=pltpu.CompilerParams(vmem_limit_bytes=VMEM),
         cost_estimate=cost(6),
         name="pick",
-    )(where, *own, *other)
+    )(where, own, other)
     sums = pl.pallas_call(
         contract,
         out_shape=jax.ShapeDtypeStruct((NZ, PAIRS, OCC // NZ, OCC), f32),

time: 95.9 us -> 99.6 us (1.039)
  the two profiles are of different devices: /device:TPU:2 before, /device:TPU:1 now
where the time goes in v3:
time: 99.6 us; the launch traced here: 99.1 us
  blocking collectives  46 us (46%)
  starting transfers between devices  29.6 us (30%)
  Pallas kernels  10.7 us (11%)
  waiting for transfers between devices  6.36 us (6%)
  local copies, waits for them, and re-layouts  6.26 us (6%)
    all_to_all x1, blocking collectives, local(): parts = lax.all_to_all(sums, 'z', 0, 0, tiled=False)  24.6 us
    all_gather x1, blocking collectives, local(): along_y = lax.all_gather(part, 'y', axis=0, tiled=True)  21.5 us
    all_to_all x1, starting transfers between devices, local(): tiles = lax.all_to_all(split, 'z', 0, 0, tiled=False)  11 us
    ppermute x1, starting transfers between devices, local(): other = lax.ppermute(own, 'core', [(0, 1), (1, 0)])  9.32 us
    ppermute x3, starting transfers between devices, local(): pieces.append(lax.ppermute(along_y, 'x', shift))  9.32 us
    ppermute x3, waiting for transfers between devices, local(): pieces.append(lax.ppermute(along_y, 'x', shift))  6.35 us
    unnamed x21, local copies, waits for them, and re-layouts  6.14 us
    pallas_call x1, Pallas kernels, local(): pl.pallas_call(find, out_shape=jax.ShapeDtypeStruct((ROWS, NZ * PER_Z), j...  3.97 us
  transfers between devices with their start and end apart: 5, of which 2 were waited for; matrix products, arithmetic and copies ran while one was open for 0% of the time, Pallas kernels for 6%

profile of v3, /device:TPU:1, one launch (start us, length us, event | category | flops | bytes accessed | tf_op | source)
XLA Modules:
  0.0 99.1 jit_solution(5426091955198634315)
XLA Ops:
  0.0 1.6 %copy-done.1 = bf16[16,8,64,64]{3,2,1,0:T(8,128)(2,1)S(1)} copy-done((bf16[16,8,64,64]{3,2,1,0:T(8,128)(2,1)S(1)}, bf16[16,8,64,64]{3,2,1,0:T(8,128)(2,1)}, u32[]{:S(2)}) %copy-start.1) | copy-done | bytes 1048600
  1.6 3.3 %split_tiles.1 = bf16[8,8,64,128]{3,2,1,0:T(8,128)(2,1)} custom-call(bf16[16,8,64,64]{3,2,1,0:T(8,128)(2,1)S(1)} %copy-done.1), custom_call_target="tpu_custom_call" | custom-call | flops 268435456 | bytes 3145728 | tf_op jit(solution)/shard_map/split_tiles/pallas_call | solution.py:132
  4.9 11.0 %all-to-all-start = ((bf16[8,8,64,128]{3,2,1,0:T(8,128)(2,1)}), bf16[8,8,64,128]{3,2,1,0:T(8,128)(2,1)S(1)}, u32[]{:S(2)}, u32[]{:S(2)}) async-start(bf16[8,8,64,128]{3,2,1,0:T(8,128)(2,1)} %split_tiles.1), calls=%async_computation | async-start | bytes 2097152 | tf_op jit(solution)/shard_map/all_to_all | solution.py:141
  15.9 21.5 %all_gather.3 = bf16[128,8,128]{2,1,0:T(8,128)(2,1)S(1)} all-gather(bf16[16,8,128]{2,1,0:T(8,128)(2,1)S(1)} %constant_dynamic-slice_fusion), channel_id=1, replica_groups=mesh['x'=4,'y'=8,'core'=2,'z'=8] {'y'}, dimensions={0}, use_global_device_ids=true | all-gather | bytes 294912 | tf_op jit(solution)/shard_map/all_gather | solution.py:124
  37.4 4.4 %collective-permute-start = (bf16[128,8,128]{2,1,0:T(8,128)(2,1)S(1)}, bf16[128,8,128]{2,1,0:T(8,128)(2,1)S(1)}, u32[]{:S(2)}, u32[]{:S(2)}) collective-permute-start(bf16[128,8,128]{2,1,0:T(8,128)(2,1)S(1)} %all_gather.3), channel_id=1, source_target_pairs={{128,0},{256,128},{384,256},{0,384},{129,1},{257,129},{385,257},{1... | collective-permute-start | bytes 786440 | tf_op jit(solution)/shard_map/ppermute | solution.py:128
  41.8 2.4 %collective-permute-start.1 = (bf16[128,8,128]{2,1,0:T(8,128)(2,1)S(1)}, bf16[128,8,128]{2,1,0:T(8,128)(2,1)S(1)}, u32[]{:S(2)}, u32[]{:S(2)}) collective-permute-start(bf16[128,8,128]{2,1,0:T(8,128)(2,1)S(1)} %all_gather.3), channel_id=1, source_target_pairs={{256,0},{384,128},{0,256},{128,384},{257,1},{385,129},{1,257},{129... | collective-permute-start | bytes 786440 | tf_op jit(solution)/shard_map/ppermute | solution.py:128
  44.2 2.5 %collective-permute-start.2 = (bf16[128,8,128]{2,1,0:T(8,128)(2,1)S(1)}, bf16[128,8,128]{2,1,0:T(8,128)(2,1)S(1)}, u32[]{:S(2)}, u32[]{:S(2)}) collective-permute-start(bf16[128,8,128]{2,1,0:T(8,128)(2,1)S(1)} %all_gather.3), channel_id=1, source_target_pairs={{384,0},{0,128},{128,256},{256,384},{385,1},{1,129},{129,257},{257... | collective-permute-start | bytes 786440 | tf_op jit(solution)/shard_map/ppermute | solution.py:128
  46.8 0.0 collective-permute-done
  46.8 3.7 %collective-permute-done.1 = bf16[128,8,128]{2,1,0:T(8,128)(2,1)S(1)} collective-permute-done((bf16[128,8,128]{2,1,0:T(8,128)(2,1)S(1)}, bf16[128,8,128]{2,1,0:T(8,128)(2,1)S(1)}, u32[]{:S(2)}, u32[]{:S(2)}) %collective-permute-start.1) | collective-permute-done | bytes 262176 | tf_op jit(solution)/shard_map/ppermute | solution.py:128
  50.5 2.7 %collective-permute-done.2 = bf16[128,8,128]{2,1,0:T(8,128)(2,1)S(1)} collective-permute-done((bf16[128,8,128]{2,1,0:T(8,128)(2,1)S(1)}, bf16[128,8,128]{2,1,0:T(8,128)(2,1)S(1)}, u32[]{:S(2)}, u32[]{:S(2)}) %collective-permute-start.2) | collective-permute-done | bytes 262176 | tf_op jit(solution)/shard_map/ppermute | solution.py:128
  53.2 9.3 %collective-permute-start.3 = (bf16[512,8,128]{2,1,0:T(8,128)(2,1)S(1)}, bf16[512,8,128]{2,1,0:T(8,128)(2,1)S(1)}, u32[]{:S(2)}, u32[]{:S(2)}) collective-permute-start(bf16[512,8,128]{2,1,0:T(8,128)(2,1)S(1)} %constant_dynamic-update-slice_fusion.refs_0_), channel_id=1, source_target_pairs={{0,8},{8,0},{1,9},{9,1},{2,10},{10,2},{3,11},{11,3},{4,12},{12,4},... | collective-permute-start | bytes 3145736 | tf_op jit(solution)/shard_map/ppermute | solution.py:130
  62.6 1.0 copy-done.2
  63.6 0.1 dynamic_slice.6.row_irrep_ref
  63.7 0.0 copy-done.8
  63.7 4.0 %find.1.where_ref = s32[16,64]{1,0:T(8,128)S(1)} custom-call(s32[1024]{0:T(1024)S(1)} %fusion.9.table_ref, s32[16]{0:T(128)S(1)} %dynamic_slice.6.row_irrep_ref, s32[16,64]{1,0:T(8,128)S(1)} %copy-done.6), custom_call_target="tpu_custom_call" | custom-call | flops 268435456 | bytes 1048576 | tf_op jit(solution)/shard_map/find/pallas_call | solution.py:149
  67.7 0.0 collective-permute-done.3.refs_1_
  67.7 1.0 copy-done.4
  68.7 1.2 %copy-done.3 = bf16[512,8,128]{2,1,0:T(8,128)(2,1)S(1)} copy-done((bf16[512,8,128]{2,1,0:T(8,128)(2,1)S(1)}, bf16[512,8,128]{2,1,0:T(8,128)(2,1)}, u32[]{:S(2)}) %copy-start.3) | copy-done | bytes 1048600
  69.9 1.2 %copy-done.5 = bf16[512,8,128]{2,1,0:T(8,128)(2,1)S(1)} copy-done((bf16[512,8,128]{2,1,0:T(8,128)(2,1)S(1)}, bf16[512,8,128]{2,1,0:T(8,128)(2,1)}, u32[]{:S(2)}) %copy-start.5) | copy-done | bytes 1048600
  71.1 1.9 %pick.1.picked_ref = bf16[8,512,256]{2,1,0:T(8,128)(2,1)S(1)} custom-call(s32[16,64]{1,0:T(8,128)S(1)} %find.1.where_ref, bf16[512,8,128]{2,1,0:T(8,128)(2,1)S(1)} %copy-done.3, bf16[512,8,128]{2,1,0:T(8,128)(2,1)S(1)} %copy-done.5), custom_call_target="tpu_custom_call" | custom-call | flops 268435456 | bytes 6291456 | tf_op jit(solution)/shard_map/pick/pallas_call | solution.py:159
  73.1 0.0 all-to-all-done.tiles_ref
  73.1 0.8 contract.1
  73.8 24.6 %all_to_all.10.parts_ref = f32[8,8,16,128]{3,2,1,0:T(8,128)S(1)} all-to-all(f32[8,8,16,128]{3,2,1,0:T(8,128)S(1)} %contract.1), channel_id=1, replica_groups=mesh['x'=4,'y'=8,'core'=2,'z'=8] {'z'}, dimensions={0} | all-to-all | bytes 1048576 | tf_op jit(solution)/shard_map/all_to_all | solution.py:182
  98.4 0.8 add_up.1
  (18 shorter events, 0.2 us)
Async XLA Ops:
  0.0 15.9 %copy-start = (bf16[16,64,128]{2,1,0:T(8,128)(2,1)S(1)}, bf16[16,64,128]{2,1,0:T(8,128)(2,1)}, u32[]{:S(2)}) copy-start(bf16[16,64,128]{2,1,0:T(8,128)(2,1)} %param.5) | copy-start | bytes 786436
  0.0 1.6 %copy-start.1 = (bf16[16,8,64,64]{3,2,1,0:T(8,128)(2,1)S(1)}, bf16[16,8,64,64]{3,2,1,0:T(8,128)(2,1)}, u32[]{:S(2)}) copy-start(bf16[16,8,64,64]{3,2,1,0:T(8,128)(2,1)} %tiles_ref.1) | copy-start | bytes 3145732
  4.9 58.7 %copy-start.7 = (s32[1024]{0:T(1024)S(1)}, s32[1024]{0:T(1024)}, u32[]{:S(2)}) copy-start(s32[1024]{0:T(1024)} %param.9) | copy-start | bytes 12292
  4.9 58.8 %copy-start.8 = (s32[1024]{0:T(1024)S(1)}, s32[1024]{0:T(1024)}, u32[]{:S(2)}) copy-start(s32[1024]{0:T(1024)} %param.6) | copy-start | bytes 12292
  4.9 58.8 %copy-start.6 = (s32[16,64]{1,0:T(8,128)S(1)}, s32[16,64]{1,0:T(8,128)}, u32[]{:S(2)}) copy-start(s32[16,64]{1,0:T(8,128)} %cols_ref.1) | copy-start | bytes 12292
  4.9 68.2 %all-to-all-start = ((bf16[8,8,64,128]{3,2,1,0:T(8,128)(2,1)}), bf16[8,8,64,128]{3,2,1,0:T(8,128)(2,1)S(1)}, u32[]{:S(2)}, u32[]{:S(2)}) async-start(bf16[8,8,64,128]{3,2,1,0:T(8,128)(2,1)} %split_tiles.1), calls=%async_computation | async-start | bytes 2097152 | tf_op jit(solution)/shard_map/all_to_all | solution.py:141
  37.4 9.4 %collective-permute-start = (bf16[128,8,128]{2,1,0:T(8,128)(2,1)S(1)}, bf16[128,8,128]{2,1,0:T(8,128)(2,1)S(1)}, u32[]{:S(2)}, u32[]{:S(2)}) collective-permute-start(bf16[128,8,128]{2,1,0:T(8,128)(2,1)S(1)} %all_gather.3), channel_id=1, source_target_pairs={{128,0},{256,128},{384,256},{0,384},{129,1},{257,129},{385,257},{1... | collective-permute-start | bytes 786440 | tf_op jit(solution)/shard_map/ppermute | solution.py:128
  41.8 8.7 %collective-permute-start.1 = (bf16[128,8,128]{2,1,0:T(8,128)(2,1)S(1)}, bf16[128,8,128]{2,1,0:T(8,128)(2,1)S(1)}, u32[]{:S(2)}, u32[]{:S(2)}) collective-permute-start(bf16[128,8,128]{2,1,0:T(8,128)(2,1)S(1)} %all_gather.3), channel_id=1, source_target_pairs={{256,0},{384,128},{0,256},{128,384},{257,1},{385,129},{1,257},{129... | collective-permute-start | bytes 786440 | tf_op jit(solution)/shard_map/ppermute | solution.py:128
  44.2 9.0 %collective-permute-start.2 = (bf16[128,8,128]{2,1,0:T(8,128)(2,1)S(1)}, bf16[128,8,128]{2,1,0:T(8,128)(2,1)S(1)}, u32[]{:S(2)}, u32[]{:S(2)}) collective-permute-start(bf16[128,8,128]{2,1,0:T(8,128)(2,1)S(1)} %all_gather.3), channel_id=1, source_target_pairs={{384,0},{0,128},{128,256},{256,384},{385,1},{1,129},{129,257},{257... | collective-permute-start | bytes 786440 | tf_op jit(solution)/shard_map/ppermute | solution.py:128
  53.2 14.4 %collective-permute-start.3 = (bf16[512,8,128]{2,1,0:T(8,128)(2,1)S(1)}, bf16[512,8,128]{2,1,0:T(8,128)(2,1)S(1)}, u32[]{:S(2)}, u32[]{:S(2)}) collective-permute-start(bf16[512,8,128]{2,1,0:T(8,128)(2,1)S(1)} %constant_dynamic-update-slice_fusion.refs_0_), channel_id=1, source_target_pairs={{0,8},{8,0},{1,9},{9,1},{2,10},{10,2},{3,11},{11,3},{4,12},{12,4},... | collective-permute-start | bytes 3145736 | tf_op jit(solution)/shard_map/ppermute | solution.py:130
  62.6 1.0 %copy-start.2 = (bf16[512,8,128]{2,1,0:T(8,128)(2,1)}, bf16[512,8,128]{2,1,0:T(8,128)(2,1)S(1)}, u32[]{:S(2)}) copy-start(bf16[512,8,128]{2,1,0:T(8,128)(2,1)S(1)} %constant_dynamic-update-slice_fusion.refs_0_) | copy-start | bytes 3145732
  67.7 1.0 copy-start.4
  68.7 1.2 %copy-start.3 = (bf16[512,8,128]{2,1,0:T(8,128)(2,1)S(1)}, bf16[512,8,128]{2,1,0:T(8,128)(2,1)}, u32[]{:S(2)}) copy-start(bf16[512,8,128]{2,1,0:T(8,128)(2,1)} %copy-done.2) | copy-start | bytes 3145732
  69.9 1.2 %copy-start.5 = (bf16[512,8,128]{2,1,0:T(8,128)(2,1)S(1)}, bf16[512,8,128]{2,1,0:T(8,128)(2,1)}, u32[]{:S(2)}) copy-start(bf16[512,8,128]{2,1,0:T(8,128)(2,1)} %copy-done.4) | copy-start | bytes 3145732

commit v4 on v3

--- a/solution.py
+++ b/solution.py
@@ -15,6 +15,7 @@
 SUB = TILE // NZ
 PER_Z = 8
 OCC = 128
+BACKWARD = list(range(NZ))[::-1]
 VMEM = 16 << 20
 CONTR = NZ * PER_Z * SUB
 
@@ -92,9 +93,9 @@
         both = lax.dot_general(
             picked_ref[pair], tiles, (((0,), (0,)), ((), ())), preferred_element_type=f32
         )
-        out_ref[:, pair] = jnp.where(low, both[:OCC], both[OCC:]).reshape(
-            NZ, OCC // NZ, OCC
-        )
+        total = jnp.where(low, both[:OCC], both[OCC:])
+        for i, z in enumerate(BACKWARD):
+            out_ref[i, pair] = total[z * (OCC // NZ) : (z + 1) * (OCC // NZ)]
 
 
 def add_up(parts_ref, out_ref):
@@ -121,7 +122,9 @@
     core, z = lax.axis_index("core"), lax.axis_index("z")
 
     part = lax.dynamic_slice_in_dim(amplitudes, z * SUB, SUB, 1)
-    along_y = lax.all_gather(part, "y", axis=0, tiled=True)
+    to_y = jnp.broadcast_to(part, (NY, ROWS, SUB, OCC))
+    along_y = lax.all_to_all(to_y, "y", 0, 0, tiled=False)
+    along_y = along_y.reshape(NY * ROWS, SUB, OCC)
     pieces = [along_y]
     for k in (1, 2, 3):
         shift = [((i + k) % NX, i) for i in range(NX)]
@@ -179,7 +182,7 @@
         cost_estimate=cost(4),
         name="contract",
     )(picked, tiles)
-    parts = lax.all_to_all(sums, "z", 0, 0, tiled=False)
+    parts = lax.all_to_all(sums, "z", 0, 0, axis_index_groups=[BACKWARD], tiled=False)
 
     total = pl.pallas_call(
         add_up,

time: 99.6 us -> 85.8 us (0.86)
  the two profiles are of different devices: /device:TPU:1 before, /device:TPU:64 now
where the time goes in v4:
time: 85.8 us; the launch traced here: 85.3 us
  starting transfers between devices  29.1 us (34%)
  blocking collectives  21.3 us (25%)
  waiting for transfers between devices  16.1 us (19%)
  Pallas kernels  10.7 us (12%)
  local copies, waits for them, and re-layouts  7.78 us (9%)
    all_to_all x1, blocking collectives, local(): lax.all_to_all(sums, 'z', 0, 0, axis_index_groups=[BACKWARD], tiled=False)  21.3 us
    ppermute x3, starting transfers between devices, local(): pieces.append(lax.ppermute(along_y, 'x', shift))  10.2 us
    all_to_all x1, starting transfers between devices, local(): tiles = lax.all_to_all(split, 'z', 0, 0, tiled=False)  9.97 us
    ppermute x3, waiting for transfers between devices, local(): pieces.append(lax.ppermute(along_y, 'x', shift))  9.04 us
    all_to_all x1, starting transfers between devices, local(): along_y = lax.all_to_all(to_y, 'y', 0, 0, tiled=False)  7.1 us
    all_to_all x1, waiting for transfers between devices, local(): along_y = lax.all_to_all(to_y, 'y', 0, 0, tiled=False)  7.03 us
    unnamed x18, local copies, waits for them, and re-layouts  6.94 us
    pallas_call x1, Pallas kernels, local(): pl.pallas_call(find, out_shape=jax.ShapeDtypeStruct((ROWS, NZ * PER_Z), j...  3.97 us
  transfers between devices with their start and end apart: 6, of which 4 were waited for; matrix products, arithmetic and copies ran while one was open for 0% of the time, Pallas kernels for 11%

profile of v4, /device:TPU:64, one launch (start us, length us, event | category | flops | bytes accessed | tf_op | source)
XLA Modules:
  0.0 85.3 jit_solution(16620411776681694014)
XLA Ops:
  0.0 0.9 %copy-done = bf16[16,64,128]{2,1,0:T(8,128)(2,1)S(1)} copy-done((bf16[16,64,128]{2,1,0:T(8,128)(2,1)S(1)}, bf16[16,64,128]{2,1,0:T(8,128)(2,1)}, u32[]{:S(2)}) %copy-start) | copy-done | bytes 262168
  1.0 0.8 broadcast_in_dim.3
  1.7 7.1 %all-to-all-start = ((bf16[8,16,8,128]{3,2,1,0:T(8,128)(2,1)}), bf16[8,16,8,128]{3,2,1,0:T(8,128)(2,1)S(1)}, u32[]{:S(2)}, u32[]{:S(2)}) async-start(bf16[8,16,8,128]{3,2,1,0:T(8,128)(2,1)} %broadcast_in_dim.3), calls=%async_computation | async-start | bytes 524288 | tf_op jit(solution)/shard_map/all_to_all | solution.py:126
  8.8 1.6 %copy-done.3 = bf16[16,8,64,64]{3,2,1,0:T(8,128)(2,1)S(1)} copy-done((bf16[16,8,64,64]{3,2,1,0:T(8,128)(2,1)S(1)}, bf16[16,8,64,64]{3,2,1,0:T(8,128)(2,1)}, u32[]{:S(2)}) %copy-start.3) | copy-done | bytes 1048600
  10.4 3.2 %split_tiles.1 = bf16[8,8,64,128]{3,2,1,0:T(8,128)(2,1)} custom-call(bf16[16,8,64,64]{3,2,1,0:T(8,128)(2,1)S(1)} %copy-done.3), custom_call_target="tpu_custom_call" | custom-call | flops 268435456 | bytes 3145728 | tf_op jit(solution)/shard_map/split_tiles/pallas_call | solution.py:135
  13.7 7.0 %all-to-all-done = bf16[8,16,8,128]{3,2,1,0:T(8,128)(2,1)S(1)} async-done(((bf16[8,16,8,128]{3,2,1,0:T(8,128)(2,1)}), bf16[8,16,8,128]{3,2,1,0:T(8,128)(2,1)S(1)}, u32[]{:S(2)}, u32[]{:S(2)}) %all-to-all-start) | async-done | bytes 262176 | tf_op jit(solution)/shard_map/all_to_all | solution.py:126
  20.7 10.0 %all-to-all-start.1 = ((bf16[8,8,64,128]{3,2,1,0:T(8,128)(2,1)}), bf16[8,8,64,128]{3,2,1,0:T(8,128)(2,1)S(1)}, u32[]{:S(2)}, u32[]{:S(2)}) async-start(bf16[8,8,64,128]{3,2,1,0:T(8,128)(2,1)} %split_tiles.1), calls=%async_computation.1 | async-start | bytes 2097152 | tf_op jit(solution)/shard_map/all_to_all | solution.py:144
  30.7 4.7 %collective-permute-start = (bf16[128,8,128]{2,1,0:T(8,128)(2,1)S(1)}, bf16[128,8,128]{2,1,0:T(8,128)(2,1)S(1)}, u32[]{:S(2)}, u32[]{:S(2)}) collective-permute-start(bf16[128,8,128]{2,1,0:T(8,128)(2,1)S(1)} %bitcast.2), channel_id=1, source_target_pairs={{128,0},{256,128},{384,256},{0,384},{129,1},{257,129},{385,257},{1... | collective-permute-start | bytes 786440 | tf_op jit(solution)/shard_map/ppermute | solution.py:131
  35.3 2.7 %collective-permute-start.1 = (bf16[128,8,128]{2,1,0:T(8,128)(2,1)S(1)}, bf16[128,8,128]{2,1,0:T(8,128)(2,1)S(1)}, u32[]{:S(2)}, u32[]{:S(2)}) collective-permute-start(bf16[128,8,128]{2,1,0:T(8,128)(2,1)S(1)} %bitcast.3), channel_id=1, source_target_pairs={{256,0},{384,128},{0,256},{128,384},{257,1},{385,129},{1,257},{129... | collective-permute-start | bytes 786440 | tf_op jit(solution)/shard_map/ppermute | solution.py:131
  38.0 2.8 %collective-permute-start.2 = (bf16[128,8,128]{2,1,0:T(8,128)(2,1)S(1)}, bf16[128,8,128]{2,1,0:T(8,128)(2,1)S(1)}, u32[]{:S(2)}, u32[]{:S(2)}) collective-permute-start(bf16[128,8,128]{2,1,0:T(8,128)(2,1)S(1)} %bitcast.4), channel_id=1, source_target_pairs={{384,0},{0,128},{128,256},{256,384},{385,1},{1,129},{129,257},{257... | collective-permute-start | bytes 786440 | tf_op jit(solution)/shard_map/ppermute | solution.py:131
  40.9 3.7 %collective-permute-done = bf16[128,8,128]{2,1,0:T(8,128)(2,1)S(1)} collective-permute-done((bf16[128,8,128]{2,1,0:T(8,128)(2,1)S(1)}, bf16[128,8,128]{2,1,0:T(8,128)(2,1)S(1)}, u32[]{:S(2)}, u32[]{:S(2)}) %collective-permute-start) | collective-permute-done | bytes 262176 | tf_op jit(solution)/shard_map/ppermute | solution.py:131
  44.6 2.5 %collective-permute-done.1 = bf16[128,8,128]{2,1,0:T(8,128)(2,1)S(1)} collective-permute-done((bf16[128,8,128]{2,1,0:T(8,128)(2,1)S(1)}, bf16[128,8,128]{2,1,0:T(8,128)(2,1)S(1)}, u32[]{:S(2)}, u32[]{:S(2)}) %collective-permute-start.1) | collective-permute-done | bytes 262176 | tf_op jit(solution)/shard_map/ppermute | solution.py:131
  47.1 2.8 %collective-permute-done.2 = bf16[128,8,128]{2,1,0:T(8,128)(2,1)S(1)} collective-permute-done((bf16[128,8,128]{2,1,0:T(8,128)(2,1)S(1)}, bf16[128,8,128]{2,1,0:T(8,128)(2,1)S(1)}, u32[]{:S(2)}, u32[]{:S(2)}) %collective-permute-start.2) | collective-permute-done | bytes 262176 | tf_op jit(solution)/shard_map/ppermute | solution.py:131
  49.9 0.1 pad_maximum_fusion.refs_0_
  50.0 1.9 %collective-permute-start.3 = (bf16[512,8,128]{2,1,0:T(8,128)(2,1)S(1)}, bf16[512,8,128]{2,1,0:T(8,128)(2,1)S(1)}, u32[]{:S(2)}, u32[]{:S(2)}) collective-permute-start(bf16[512,8,128]{2,1,0:T(8,128)(2,1)S(1)} %pad_maximum_fusion.refs_0_), channel_id=1, source_target_pairs={{0,8},{8,0},{1,9},{9,1},{2,10},{10,2},{3,11},{11,3},{4,12},{12,4},... | collective-permute-start | bytes 3145736 | tf_op jit(solution)/shard_map/ppermute | solution.py:133
  52.0 1.0 %copy-done.1 = bf16[512,8,128]{2,1,0:T(8,128)(2,1)} copy-done((bf16[512,8,128]{2,1,0:T(8,128)(2,1)}, bf16[512,8,128]{2,1,0:T(8,128)(2,1)S(1)}, u32[]{:S(2)}) %copy-start.1) | copy-done | bytes 1048600
  53.1 4.0 %find.1.where_ref = s32[16,64]{1,0:T(8,128)S(1)} custom-call(s32[1024]{0:T(1024)S(1)} %fusion.9.table_ref, s32[16]{0:T(128)S(1)} %dynamic_slice.6.row_irrep_ref, s32[16,64]{1,0:T(8,128)S(1)} %copy-done.6), custom_call_target="tpu_custom_call" | custom-call | flops 268435456 | bytes 1048576 | tf_op jit(solution)/shard_map/find/pallas_call | solution.py:152
  57.1 1.0 %copy-done.4 = bf16[512,8,128]{2,1,0:T(8,128)(2,1)} copy-done((bf16[512,8,128]{2,1,0:T(8,128)(2,1)}, bf16[512,8,128]{2,1,0:T(8,128)(2,1)S(1)}, u32[]{:S(2)}) %copy-start.4) | copy-done | bytes 1048600
  58.0 1.2 %copy-done.2 = bf16[512,8,128]{2,1,0:T(8,128)(2,1)S(1)} copy-done((bf16[512,8,128]{2,1,0:T(8,128)(2,1)S(1)}, bf16[512,8,128]{2,1,0:T(8,128)(2,1)}, u32[]{:S(2)}) %copy-start.2) | copy-done | bytes 1048600
  59.2 1.2 %copy-done.5 = bf16[512,8,128]{2,1,0:T(8,128)(2,1)S(1)} copy-done((bf16[512,8,128]{2,1,0:T(8,128)(2,1)S(1)}, bf16[512,8,128]{2,1,0:T(8,128)(2,1)}, u32[]{:S(2)}) %copy-start.5) | copy-done | bytes 1048600
  60.5 1.9 %pick.1.picked_ref = bf16[8,512,256]{2,1,0:T(8,128)(2,1)S(1)} custom-call(s32[16,64]{1,0:T(8,128)S(1)} %find.1.where_ref, bf16[512,8,128]{2,1,0:T(8,128)(2,1)S(1)} %copy-done.2, bf16[512,8,128]{2,1,0:T(8,128)(2,1)S(1)} %copy-done.5), custom_call_target="tpu_custom_call" | custom-call | flops 268435456 | bytes 6291456 | tf_op jit(solution)/shard_map/pick/pallas_call | solution.py:162
  62.4 0.8 contract.1
  63.2 21.3 %all_to_all.15.parts_ref = f32[8,8,16,128]{3,2,1,0:T(8,128)S(1)} all-to-all(f32[8,8,16,128]{3,2,1,0:T(8,128)S(1)} %contract.1), channel_id=1, replica_groups={{7,6,5,4,3,2,1,0},{15,14,13,12,11,10,9,8},{23,22,21,20,19,18,17,16},{31..., dimensions={0} | all-to-all | bytes 1048576 | tf_op jit(solution)/shard_map/all_to_all | solution.py:185
  84.5 0.8 add_up.1
  (17 shorter events, 0.1 us)
Async XLA Ops:
  0.0 1.0 %copy-start = (bf16[16,64,128]{2,1,0:T(8,128)(2,1)S(1)}, bf16[16,64,128]{2,1,0:T(8,128)(2,1)}, u32[]{:S(2)}) copy-start(bf16[16,64,128]{2,1,0:T(8,128)(2,1)} %param.5) | copy-start | bytes 786436
  1.7 19.0 %all-to-all-start = ((bf16[8,16,8,128]{3,2,1,0:T(8,128)(2,1)}), bf16[8,16,8,128]{3,2,1,0:T(8,128)(2,1)S(1)}, u32[]{:S(2)}, u32[]{:S(2)}) async-start(bf16[8,16,8,128]{3,2,1,0:T(8,128)(2,1)} %broadcast_in_dim.3), calls=%async_computation | async-start | bytes 524288 | tf_op jit(solution)/shard_map/all_to_all | solution.py:126
  8.8 1.6 %copy-start.3 = (bf16[16,8,64,64]{3,2,1,0:T(8,128)(2,1)S(1)}, bf16[16,8,64,64]{3,2,1,0:T(8,128)(2,1)}, u32[]{:S(2)}) copy-start(bf16[16,8,64,64]{3,2,1,0:T(8,128)(2,1)} %tiles_ref.1) | copy-start | bytes 3145732
  13.7 39.3 %copy-start.7 = (s32[1024]{0:T(1024)S(1)}, s32[1024]{0:T(1024)}, u32[]{:S(2)}) copy-start(s32[1024]{0:T(1024)} %param.9) | copy-start | bytes 12292
  13.7 39.4 %copy-start.8 = (s32[1024]{0:T(1024)S(1)}, s32[1024]{0:T(1024)}, u32[]{:S(2)}) copy-start(s32[1024]{0:T(1024)} %param.6) | copy-start | bytes 12292
  13.7 39.4 %copy-start.6 = (s32[16,64]{1,0:T(8,128)S(1)}, s32[16,64]{1,0:T(8,128)}, u32[]{:S(2)}) copy-start(s32[16,64]{1,0:T(8,128)} %cols_ref.1) | copy-start | bytes 12292
  20.7 41.7 %all-to-all-start.1 = ((bf16[8,8,64,128]{3,2,1,0:T(8,128)(2,1)}), bf16[8,8,64,128]{3,2,1,0:T(8,128)(2,1)S(1)}, u32[]{:S(2)}, u32[]{:S(2)}) async-start(bf16[8,8,64,128]{3,2,1,0:T(8,128)(2,1)} %split_tiles.1), calls=%async_computation.1 | async-start | bytes 2097152 | tf_op jit(solution)/shard_map/all_to_all | solution.py:144
  30.7 13.9 %collective-permute-start = (bf16[128,8,128]{2,1,0:T(8,128)(2,1)S(1)}, bf16[128,8,128]{2,1,0:T(8,128)(2,1)S(1)}, u32[]{:S(2)}, u32[]{:S(2)}) collective-permute-start(bf16[128,8,128]{2,1,0:T(8,128)(2,1)S(1)} %bitcast.2), channel_id=1, source_target_pairs={{128,0},{256,128},{384,256},{0,384},{129,1},{257,129},{385,257},{1... | collective-permute-start | bytes 786440 | tf_op jit(solution)/shard_map/ppermute | solution.py:131
  35.3 11.8 %collective-permute-start.1 = (bf16[128,8,128]{2,1,0:T(8,128)(2,1)S(1)}, bf16[128,8,128]{2,1,0:T(8,128)(2,1)S(1)}, u32[]{:S(2)}, u32[]{:S(2)}) collective-permute-start(bf16[128,8,128]{2,1,0:T(8,128)(2,1)S(1)} %bitcast.3), channel_id=1, source_target_pairs={{256,0},{384,128},{0,256},{128,384},{257,1},{385,129},{1,257},{129... | collective-permute-start | bytes 786440 | tf_op jit(solution)/shard_map/ppermute | solution.py:131
  38.0 11.8 %collective-permute-start.2 = (bf16[128,8,128]{2,1,0:T(8,128)(2,1)S(1)}, bf16[128,8,128]{2,1,0:T(8,128)(2,1)S(1)}, u32[]{:S(2)}, u32[]{:S(2)}) collective-permute-start(bf16[128,8,128]{2,1,0:T(8,128)(2,1)S(1)} %bitcast.4), channel_id=1, source_target_pairs={{384,0},{0,128},{128,256},{256,384},{385,1},{1,129},{129,257},{257... | collective-permute-start | bytes 786440 | tf_op jit(solution)/shard_map/ppermute | solution.py:131
  50.0 7.0 %collective-permute-start.3 = (bf16[512,8,128]{2,1,0:T(8,128)(2,1)S(1)}, bf16[512,8,128]{2,1,0:T(8,128)(2,1)S(1)}, u32[]{:S(2)}, u32[]{:S(2)}) collective-permute-start(bf16[512,8,128]{2,1,0:T(8,128)(2,1)S(1)} %pad_maximum_fusion.refs_0_), channel_id=1, source_target_pairs={{0,8},{8,0},{1,9},{9,1},{2,10},{10,2},{3,11},{11,3},{4,12},{12,4},... | collective-permute-start | bytes 3145736 | tf_op jit(solution)/shard_map/ppermute | solution.py:133
  52.0 1.0 %copy-start.1 = (bf16[512,8,128]{2,1,0:T(8,128)(2,1)}, bf16[512,8,128]{2,1,0:T(8,128)(2,1)S(1)}, u32[]{:S(2)}) copy-start(bf16[512,8,128]{2,1,0:T(8,128)(2,1)S(1)} %pad_maximum_fusion.refs_0_) | copy-start | bytes 3145732
  57.1 1.0 %copy-start.4 = (bf16[512,8,128]{2,1,0:T(8,128)(2,1)}, bf16[512,8,128]{2,1,0:T(8,128)(2,1)S(1)}, u32[]{:S(2)}) copy-start(bf16[512,8,128]{2,1,0:T(8,128)(2,1)S(1)} %collective-permute-done.3.refs_1_) | copy-start | bytes 3145732
  58.0 1.2 %copy-start.2 = (bf16[512,8,128]{2,1,0:T(8,128)(2,1)S(1)}, bf16[512,8,128]{2,1,0:T(8,128)(2,1)}, u32[]{:S(2)}) copy-start(bf16[512,8,128]{2,1,0:T(8,128)(2,1)} %copy-done.1) | copy-start | bytes 3145732
  59.2 1.2 %copy-start.5 = (bf16[512,8,128]{2,1,0:T(8,128)(2,1)S(1)}, bf16[512,8,128]{2,1,0:T(8,128)(2,1)}, u32[]{:S(2)}) copy-start(bf16[512,8,128]{2,1,0:T(8,128)(2,1)} %copy-done.4) | copy-start | bytes 3145732

commit v5 on v4

--- a/solution.py
+++ b/solution.py
@@ -122,15 +122,20 @@
     core, z = lax.axis_index("core"), lax.axis_index("z")
 
     part = lax.dynamic_slice_in_dim(amplitudes, z * SUB, SUB, 1)
-    to_y = jnp.broadcast_to(part, (NY, ROWS, SUB, OCC))
-    along_y = lax.all_to_all(to_y, "y", 0, 0, tiled=False)
-    along_y = along_y.reshape(NY * ROWS, SUB, OCC)
+    to_y = jnp.broadcast_to(part, (NY // 2, ROWS, SUB, OCC))
+    same = lax.all_to_all(
+        to_y, "y", 0, 0, axis_index_groups=[[0, 2, 4, 6], [1, 3, 5, 7]], tiled=False
+    ).reshape(NY // 2 * ROWS, SUB, OCC)
+    near = lax.ppermute(same, "y", [(i, i ^ 1) for i in range(NY)])
+    along_y = jnp.concatenate([same, near], axis=0)
     pieces = [along_y]
     for k in (1, 2, 3):
         shift = [((i + k) % NX, i) for i in range(NX)]
         pieces.append(lax.ppermute(along_y, "x", shift))
-    own = jnp.concatenate(pieces, axis=0)
-    other = lax.ppermute(own, "core", [(0, 1), (1, 0)])
+    owns, others = [], []
+    for two in (pieces[:2], pieces[2:]):
+        owns.append(jnp.concatenate(two, axis=0))
+        others.append(lax.ppermute(owns[-1], "core", [(0, 1), (1, 0)]))
 
     split = pl.pallas_call(
         split_tiles,
@@ -145,7 +150,8 @@
 
     holder = block_slot // ROWS
     holder_x, holder_y = holder // (NY * NC), (holder // NC) % NY
-    place = ((holder_x - x) % NX) * NY + holder_y + (holder + core) % NC * (NX * NY)
+    near = (holder_y + y) % 2 * (NY // 2) + holder_y // 2
+    place = ((holder_x - x) % NX) * NY + near + (holder + core) % NC * (NX * NY)
     table = (place * ROWS + block_slot % ROWS) * NIRR + irreps
     first_row = ((x * NY + y) * NC + core) * ROWS
     row_irrep = lax.dynamic_slice_in_dim(irreps, first_row, ROWS, 0)
@@ -163,16 +169,16 @@
         pick,
         out_shape=jax.ShapeDtypeStruct((PAIRS, CONTR, 2 * OCC), bf16),
         in_specs=[pl.BlockSpec(memory_space=pltpu.SMEM)]
-        + [pl.BlockSpec(memory_space=pl.ANY)] * NC,
+        + [pl.BlockSpec(memory_space=pl.ANY)] * (2 * NC),
         out_specs=in_vmem(1)[0],
         scratch_shapes=[
             pltpu.VMEM((BLK + 8, SUB, OCC), bf16),
-            pltpu.SemaphoreType.DMA((NC,)),
+            pltpu.SemaphoreType.DMA((2 * NC,)),
         ],
         compiler_params=pltpu.CompilerParams(vmem_limit_bytes=VMEM),
         cost_estimate=cost(6),
         name="pick",
-    )(where, own, other)
+    )(where, *owns, *others)
     sums = pl.pallas_call(
         contract,
         out_shape=jax.ShapeDtypeStruct((NZ, PAIRS, OCC // NZ, OCC), f32),

time: 85.8 us -> 90.1 us (1.050)
  starting transfers between devices: 29.1 us -> 33.9 us
  waiting for transfers between devices: 16.1 us -> 13.8 us
  local copies, waits for them, and re-layouts: 7.78 us -> 9.12 us
    ppermute x1 -> x3, starting transfers between devices: 1.92 us -> 6.66 us  [the longest x2 3.84 us: local(): others.append(lax.ppermute(owns[-1], 'core', [(0, 1), (1, 0)]))]
    ppermute x1 -> x3, waiting for transfers between devices: 0.01 us -> 4.03 us  [the longest x1 4.02 us: local(): near = lax.ppermute(same, 'y', [(i, i ^ 1) for i in range(NY)])]
    ppermute x3, waiting for transfers between devices: 9.04 us -> 5.66 us  [local(): pieces.append(lax.ppermute(along_y, 'x', shift))]
    all_to_all x1, waiting for transfers between devices: 7.03 us -> 4.06 us  [local(): lax.all_to_all(to_y, 'y', 0, 0, axis_index_groups=[[0, 2, 4, 6], [1, 3, 5...]
    unnamed x18 -> x27, local copies, waits for them, and re-layouts: 6.94 us -> 8.32 us
  transfers between devices with their start and end apart: 6 -> 8, of which waited for: 4 -> 5; matrix products, arithmetic and copies ran while one was open for 0% -> 0% of each run, Pallas kernels for 11% -> 10%
where the time goes in v5:
time: 90.1 us; the launch traced here: 89.4 us
  starting transfers between devices  33.9 us (38%)
  blocking collectives  21.6 us (24%)
  waiting for transfers between devices  13.8 us (15%)
  Pallas kernels  10.7 us (12%)
  local copies, waits for them, and re-layouts  9.12 us (10%)
    all_to_all x1, blocking collectives, local(): lax.all_to_all(sums, 'z', 0, 0, axis_index_groups=[BACKWARD], tiled=False)  21.6 us
    ppermute x3, starting transfers between devices, local(): pieces.append(lax.ppermute(along_y, 'x', shift))  10.2 us
    all_to_all x1, starting transfers between devices, local(): tiles = lax.all_to_all(split, 'z', 0, 0, tiled=False)  9.97 us
    unnamed x27, local copies, waits for them, and re-layouts  8.32 us
    all_to_all x1, starting transfers between devices, local(): lax.all_to_all(to_y, 'y', 0, 0, axis_index_groups=[[0, 2, 4, 6], [1, 3, 5...  7.09 us
    ppermute x3, waiting for transfers between devices, local(): pieces.append(lax.ppermute(along_y, 'x', shift))  5.66 us
    all_to_all x1, waiting for transfers between devices, local(): lax.all_to_all(to_y, 'y', 0, 0, axis_index_groups=[[0, 2, 4, 6], [1, 3, 5...  4.06 us
    ppermute x1, waiting for transfers between devices, local(): near = lax.ppermute(same, 'y', [(i, i ^ 1) for i in range(NY)])  4.02 us
  transfers between devices with their start and end apart: 8, of which 5 were waited for; matrix products, arithmetic and copies ran while one was open for 0% of the time, Pallas kernels for 10%

profile of v5, /device:TPU:64, one launch (start us, length us, event | category | flops | bytes accessed | tf_op | source)
XLA Modules:
  0.0 89.4 jit_solution(5690373834682025446)
XLA Ops:
  0.0 0.9 %copy-done = bf16[16,64,128]{2,1,0:T(8,128)(2,1)S(1)} copy-done((bf16[16,64,128]{2,1,0:T(8,128)(2,1)S(1)}, bf16[16,64,128]{2,1,0:T(8,128)(2,1)}, u32[]{:S(2)}) %copy-start) | copy-done | bytes 262168
  1.6 7.1 %all-to-all-start = ((bf16[4,16,8,128]{3,2,1,0:T(8,128)(2,1)}), bf16[4,16,8,128]{3,2,1,0:T(8,128)(2,1)S(1)}, u32[]{:S(2)}, u32[]{:S(2)}) async-start(bf16[4,16,8,128]{3,2,1,0:T(8,128)(2,1)} %broadcast_in_dim.3), calls=%async_computation | async-start | bytes 262144 | tf_op jit(solution)/shard_map/all_to_all | solution.py:126
  8.7 1.6 %copy-done.1 = bf16[16,8,64,64]{3,2,1,0:T(8,128)(2,1)S(1)} copy-done((bf16[16,8,64,64]{3,2,1,0:T(8,128)(2,1)S(1)}, bf16[16,8,64,64]{3,2,1,0:T(8,128)(2,1)}, u32[]{:S(2)}) %copy-start.1) | copy-done | bytes 1048600
  10.3 3.3 %split_tiles.1 = bf16[8,8,64,128]{3,2,1,0:T(8,128)(2,1)} custom-call(bf16[16,8,64,64]{3,2,1,0:T(8,128)(2,1)S(1)} %copy-done.1), custom_call_target="tpu_custom_call" | custom-call | flops 268435456 | bytes 3145728 | tf_op jit(solution)/shard_map/split_tiles/pallas_call | solution.py:140
  13.6 4.1 %all-to-all-done = bf16[4,16,8,128]{3,2,1,0:T(8,128)(2,1)S(1)} async-done(((bf16[4,16,8,128]{3,2,1,0:T(8,128)(2,1)}), bf16[4,16,8,128]{3,2,1,0:T(8,128)(2,1)S(1)}, u32[]{:S(2)}, u32[]{:S(2)}) %all-to-all-start) | async-done | bytes 131104 | tf_op jit(solution)/shard_map/all_to_all | solution.py:126
  17.7 10.0 %all-to-all-start.1 = ((bf16[8,8,64,128]{3,2,1,0:T(8,128)(2,1)}), bf16[8,8,64,128]{3,2,1,0:T(8,128)(2,1)S(1)}, u32[]{:S(2)}, u32[]{:S(2)}) async-start(bf16[8,8,64,128]{3,2,1,0:T(8,128)(2,1)} %split_tiles.1), calls=%async_computation.1 | async-start | bytes 2097152 | tf_op jit(solution)/shard_map/all_to_all | solution.py:149
  27.6 2.8 %collective-permute-start = (bf16[64,8,128]{2,1,0:T(8,128)(2,1)S(1)}, bf16[64,8,128]{2,1,0:T(8,128)(2,1)S(1)}, u32[]{:S(2)}, u32[]{:S(2)}) collective-permute-start(bf16[64,8,128]{2,1,0:T(8,128)(2,1)S(1)} %bitcast.2), channel_id=1, source_target_pairs={{0,16},{16,0},{32,48},{48,32},{64,80},{80,64},{96,112},{112,96},{1... | collective-permute-start | bytes 393224 | tf_op jit(solution)/shard_map/ppermute | solution.py:129
  30.5 4.0 %collective-permute-done = bf16[64,8,128]{2,1,0:T(8,128)(2,1)S(1)} collective-permute-done((bf16[64,8,128]{2,1,0:T(8,128)(2,1)S(1)}, bf16[64,8,128]{2,1,0:T(8,128)(2,1)S(1)}, u32[]{:S(2)}, u32[]{:S(2)}) %collective-permute-start) | collective-permute-done | bytes 131104 | tf_op jit(solution)/shard_map/ppermute | solution.py:129
  34.5 4.7 %collective-permute-start.1 = (bf16[128,8,128]{2,1,0:T(8,128)(2,1)S(1)}, bf16[128,8,128]{2,1,0:T(8,128)(2,1)S(1)}, u32[]{:S(2)}, u32[]{:S(2)}) collective-permute-start(bf16[128,8,128]{2,1,0:T(8,128)(2,1)S(1)} %pad_maximum_fusion.1), channel_id=1, source_target_pairs={{128,0},{256,128},{384,256},{0,384},{129,1},{257,129},{385,257},{1... | collective-permute-start | bytes 786440 | tf_op jit(solution)/shard_map/ppermute | solution.py:134
  39.2 2.7 %collective-permute-start.2 = (bf16[128,8,128]{2,1,0:T(8,128)(2,1)S(1)}, bf16[128,8,128]{2,1,0:T(8,128)(2,1)S(1)}, u32[]{:S(2)}, u32[]{:S(2)}) collective-permute-start(bf16[128,8,128]{2,1,0:T(8,128)(2,1)S(1)} %pad_maximum_fusion.1), channel_id=1, source_target_pairs={{256,0},{384,128},{0,256},{128,384},{257,1},{385,129},{1,257},{129... | collective-permute-start | bytes 786440 | tf_op jit(solution)/shard_map/ppermute | solution.py:134
  41.9 2.8 %collective-permute-start.3 = (bf16[128,8,128]{2,1,0:T(8,128)(2,1)S(1)}, bf16[128,8,128]{2,1,0:T(8,128)(2,1)S(1)}, u32[]{:S(2)}, u32[]{:S(2)}) collective-permute-start(bf16[128,8,128]{2,1,0:T(8,128)(2,1)S(1)} %pad_maximum_fusion.1), channel_id=1, source_target_pairs={{384,0},{0,128},{128,256},{256,384},{385,1},{1,129},{129,257},{257... | collective-permute-start | bytes 786440 | tf_op jit(solution)/shard_map/ppermute | solution.py:134
  44.7 2.7 %collective-permute-done.1 = bf16[128,8,128]{2,1,0:T(8,128)(2,1)S(1)} collective-permute-done((bf16[128,8,128]{2,1,0:T(8,128)(2,1)S(1)}, bf16[128,8,128]{2,1,0:T(8,128)(2,1)S(1)}, u32[]{:S(2)}, u32[]{:S(2)}) %collective-permute-start.1) | collective-permute-done | bytes 262176 | tf_op jit(solution)/shard_map/ppermute | solution.py:134
  47.5 1.9 %collective-permute-start.4 = (bf16[256,8,128]{2,1,0:T(8,128)(2,1)S(1)}, bf16[256,8,128]{2,1,0:T(8,128)(2,1)S(1)}, u32[]{:S(2)}, u32[]{:S(2)}) collective-permute-start(bf16[256,8,128]{2,1,0:T(8,128)(2,1)S(1)} %pad_maximum_fusion.refs_0_), channel_id=1, source_target_pairs={{0,8},{8,0},{1,9},{9,1},{2,10},{10,2},{3,11},{11,3},{4,12},{12,4},... | collective-permute-start | bytes 1572872 | tf_op jit(solution)/shard_map/ppermute | solution.py:138
  49.7 2.7 %collective-permute-done.3 = bf16[128,8,128]{2,1,0:T(8,128)(2,1)S(1)} collective-permute-done((bf16[128,8,128]{2,1,0:T(8,128)(2,1)S(1)}, bf16[128,8,128]{2,1,0:T(8,128)(2,1)S(1)}, u32[]{:S(2)}, u32[]{:S(2)}) %collective-permute-start.3) | collective-permute-done | bytes 262176 | tf_op jit(solution)/shard_map/ppermute | solution.py:134
  52.4 1.9 %collective-permute-start.5 = (bf16[256,8,128]{2,1,0:T(8,128)(2,1)S(1)}, bf16[256,8,128]{2,1,0:T(8,128)(2,1)S(1)}, u32[]{:S(2)}, u32[]{:S(2)}) collective-permute-start(bf16[256,8,128]{2,1,0:T(8,128)(2,1)S(1)} %constant_dynamic-update-slice_fusion.refs_1_), channel_id=1, source_target_pairs={{0,8},{8,0},{1,9},{9,1},{2,10},{10,2},{3,11},{11,3},{4,12},{12,4},... | collective-permute-start | bytes 1572872 | tf_op jit(solution)/shard_map/ppermute | solution.py:138
  54.5 4.0 %find.1.where_ref = s32[16,64]{1,0:T(8,128)S(1)} custom-call(s32[1024]{0:T(1024)S(1)} %fusion.9.table_ref, s32[16]{0:T(128)S(1)} %dynamic_slice.6.row_irrep_ref, s32[16,64]{1,0:T(8,128)S(1)} %copy-done.10), custom_call_target="tpu_custom_call" | custom-call | flops 268435456 | bytes 1048576 | tf_op jit(solution)/shard_map/find/pallas_call | solution.py:158
  58.5 0.8 copy-done.6
  59.3 0.8 copy-done.8
  60.1 1.0 %copy-done.3 = bf16[256,8,128]{2,1,0:T(8,128)(2,1)S(1)} copy-done((bf16[256,8,128]{2,1,0:T(8,128)(2,1)S(1)}, bf16[256,8,128]{2,1,0:T(8,128)(2,1)}, u32[]{:S(2)}) %copy-start.3) | copy-done | bytes 524312
  61.2 1.0 %copy-done.5 = bf16[256,8,128]{2,1,0:T(8,128)(2,1)S(1)} copy-done((bf16[256,8,128]{2,1,0:T(8,128)(2,1)S(1)}, bf16[256,8,128]{2,1,0:T(8,128)(2,1)}, u32[]{:S(2)}) %copy-start.5) | copy-done | bytes 524312
  62.2 1.0 %copy-done.7 = bf16[256,8,128]{2,1,0:T(8,128)(2,1)S(1)} copy-done((bf16[256,8,128]{2,1,0:T(8,128)(2,1)S(1)}, bf16[256,8,128]{2,1,0:T(8,128)(2,1)}, u32[]{:S(2)}) %copy-start.7) | copy-done | bytes 524312
  63.2 1.0 %copy-done.9 = bf16[256,8,128]{2,1,0:T(8,128)(2,1)S(1)} copy-done((bf16[256,8,128]{2,1,0:T(8,128)(2,1)S(1)}, bf16[256,8,128]{2,1,0:T(8,128)(2,1)}, u32[]{:S(2)}) %copy-start.9) | copy-done | bytes 524312
  64.3 2.0 %pick.1.picked_ref = bf16[8,512,256]{2,1,0:T(8,128)(2,1)S(1)} custom-call(s32[16,64]{1,0:T(8,128)S(1)} %find.1.where_ref, bf16[256,8,128]{2,1,0:T(8,128)(2,1)S(1)} %copy-done.3, bf16[256,8,128]{2,1,0:T(8,128)(2,1)S(1)} %copy-done.5, bf16[256,8,128]{2,1,0:T(8,128)(2,1)S(1)} %copy-done.7, bf16[256,8,128]{2,1,0:T(8,128)(2,1)S(1)} %copy-done.9), custom_call_target="tpu_custom_call" | custom-call | flops 268435456 | bytes 6291456 | tf_op jit(solution)/shard_map/pick/pallas_call | solution.py:168
  67.0 21.6 %all_to_all.15.parts_ref = f32[8,8,16,128]{3,2,1,0:T(8,128)S(1)} all-to-all(f32[8,8,16,128]{3,2,1,0:T(8,128)S(1)} %contract.1), channel_id=1, replica_groups={{7,6,5,4,3,2,1,0},{15,14,13,12,11,10,9,8},{23,22,21,20,19,18,17,16},{31..., dimensions={0} | all-to-all | bytes 1048576 | tf_op jit(solution)/shard_map/all_to_all | solution.py:191
  (32 shorter events, 2.8 us)
Async XLA Ops:
  0.0 1.0 %copy-start = (bf16[16,64,128]{2,1,0:T(8,128)(2,1)S(1)}, bf16[16,64,128]{2,1,0:T(8,128)(2,1)}, u32[]{:S(2)}) copy-start(bf16[16,64,128]{2,1,0:T(8,128)(2,1)} %param.5) | copy-start | bytes 786436
  1.6 16.0 %all-to-all-start = ((bf16[4,16,8,128]{3,2,1,0:T(8,128)(2,1)}), bf16[4,16,8,128]{3,2,1,0:T(8,128)(2,1)S(1)}, u32[]{:S(2)}, u32[]{:S(2)}) async-start(bf16[4,16,8,128]{3,2,1,0:T(8,128)(2,1)} %broadcast_in_dim.3), calls=%async_computation | async-start | bytes 262144 | tf_op jit(solution)/shard_map/all_to_all | solution.py:126
  8.7 1.6 %copy-start.1 = (bf16[16,8,64,64]{3,2,1,0:T(8,128)(2,1)S(1)}, bf16[16,8,64,64]{3,2,1,0:T(8,128)(2,1)}, u32[]{:S(2)}) copy-start(bf16[16,8,64,64]{3,2,1,0:T(8,128)(2,1)} %tiles_ref.1) | copy-start | bytes 3145732
  13.6 40.8 %copy-start.11 = (s32[1024]{0:T(1024)S(1)}, s32[1024]{0:T(1024)}, u32[]{:S(2)}) copy-start(s32[1024]{0:T(1024)} %param.9) | copy-start | bytes 12292
  13.6 40.9 %copy-start.12 = (s32[1024]{0:T(1024)S(1)}, s32[1024]{0:T(1024)}, u32[]{:S(2)}) copy-start(s32[1024]{0:T(1024)} %param.6) | copy-start | bytes 12292
  13.6 40.9 %copy-start.10 = (s32[16,64]{1,0:T(8,128)S(1)}, s32[16,64]{1,0:T(8,128)}, u32[]{:S(2)}) copy-start(s32[16,64]{1,0:T(8,128)} %cols_ref.1) | copy-start | bytes 12292
  17.7 48.6 %all-to-all-start.1 = ((bf16[8,8,64,128]{3,2,1,0:T(8,128)(2,1)}), bf16[8,8,64,128]{3,2,1,0:T(8,128)(2,1)S(1)}, u32[]{:S(2)}, u32[]{:S(2)}) async-start(bf16[8,8,64,128]{3,2,1,0:T(8,128)(2,1)} %split_tiles.1), calls=%async_computation.1 | async-start | bytes 2097152 | tf_op jit(solution)/shard_map/all_to_all | solution.py:149
  27.6 6.8 %collective-permute-start = (bf16[64,8,128]{2,1,0:T(8,128)(2,1)S(1)}, bf16[64,8,128]{2,1,0:T(8,128)(2,1)S(1)}, u32[]{:S(2)}, u32[]{:S(2)}) collective-permute-start(bf16[64,8,128]{2,1,0:T(8,128)(2,1)S(1)} %bitcast.2), channel_id=1, source_target_pairs={{0,16},{16,0},{32,48},{48,32},{64,80},{80,64},{96,112},{112,96},{1... | collective-permute-start | bytes 393224 | tf_op jit(solution)/shard_map/ppermute | solution.py:129
  34.5 12.9 %collective-permute-start.1 = (bf16[128,8,128]{2,1,0:T(8,128)(2,1)S(1)}, bf16[128,8,128]{2,1,0:T(8,128)(2,1)S(1)}, u32[]{:S(2)}, u32[]{:S(2)}) collective-permute-start(bf16[128,8,128]{2,1,0:T(8,128)(2,1)S(1)} %pad_maximum_fusion.1), channel_id=1, source_target_pairs={{128,0},{256,128},{384,256},{0,384},{129,1},{257,129},{385,257},{1... | collective-permute-start | bytes 786440 | tf_op jit(solution)/shard_map/ppermute | solution.py:134
  39.2 10.5 %collective-permute-start.2 = (bf16[128,8,128]{2,1,0:T(8,128)(2,1)S(1)}, bf16[128,8,128]{2,1,0:T(8,128)(2,1)S(1)}, u32[]{:S(2)}, u32[]{:S(2)}) collective-permute-start(bf16[128,8,128]{2,1,0:T(8,128)(2,1)S(1)} %pad_maximum_fusion.1), channel_id=1, source_target_pairs={{256,0},{384,128},{0,256},{128,384},{257,1},{385,129},{1,257},{129... | collective-permute-start | bytes 786440 | tf_op jit(solution)/shard_map/ppermute | solution.py:134
  41.9 10.5 %collective-permute-start.3 = (bf16[128,8,128]{2,1,0:T(8,128)(2,1)S(1)}, bf16[128,8,128]{2,1,0:T(8,128)(2,1)S(1)}, u32[]{:S(2)}, u32[]{:S(2)}) collective-permute-start(bf16[128,8,128]{2,1,0:T(8,128)(2,1)S(1)} %pad_maximum_fusion.1), channel_id=1, source_target_pairs={{384,0},{0,128},{128,256},{256,384},{385,1},{1,129},{129,257},{257... | collective-permute-start | bytes 786440 | tf_op jit(solution)/shard_map/ppermute | solution.py:134
  47.5 11.1 %copy-start.2 = (bf16[256,8,128]{2,1,0:T(8,128)(2,1)}, bf16[256,8,128]{2,1,0:T(8,128)(2,1)S(1)}, u32[]{:S(2)}) copy-start(bf16[256,8,128]{2,1,0:T(8,128)(2,1)S(1)} %pad_maximum_fusion.refs_0_) | copy-start | bytes 1572868
  47.5 11.0 %collective-permute-start.4 = (bf16[256,8,128]{2,1,0:T(8,128)(2,1)S(1)}, bf16[256,8,128]{2,1,0:T(8,128)(2,1)S(1)}, u32[]{:S(2)}, u32[]{:S(2)}) collective-permute-start(bf16[256,8,128]{2,1,0:T(8,128)(2,1)S(1)} %pad_maximum_fusion.refs_0_), channel_id=1, source_target_pairs={{0,8},{8,0},{1,9},{9,1},{2,10},{10,2},{3,11},{11,3},{4,12},{12,4},... | collective-permute-start | bytes 1572872 | tf_op jit(solution)/shard_map/ppermute | solution.py:138
  52.4 6.1 %copy-start.4 = (bf16[256,8,128]{2,1,0:T(8,128)(2,1)}, bf16[256,8,128]{2,1,0:T(8,128)(2,1)S(1)}, u32[]{:S(2)}) copy-start(bf16[256,8,128]{2,1,0:T(8,128)(2,1)S(1)} %constant_dynamic-update-slice_fusion.refs_1_) | copy-start | bytes 1572868
  52.4 6.9 %collective-permute-start.5 = (bf16[256,8,128]{2,1,0:T(8,128)(2,1)S(1)}, bf16[256,8,128]{2,1,0:T(8,128)(2,1)S(1)}, u32[]{:S(2)}, u32[]{:S(2)}) collective-permute-start(bf16[256,8,128]{2,1,0:T(8,128)(2,1)S(1)} %constant_dynamic-update-slice_fusion.refs_1_), channel_id=1, source_target_pairs={{0,8},{8,0},{1,9},{9,1},{2,10},{10,2},{3,11},{11,3},{4,12},{12,4},... | collective-permute-start | bytes 1572872 | tf_op jit(solution)/shard_map/ppermute | solution.py:138
  58.5 0.8 copy-start.6
  59.3 0.8 copy-start.8
  60.1 1.0 %copy-start.3 = (bf16[256,8,128]{2,1,0:T(8,128)(2,1)S(1)}, bf16[256,8,128]{2,1,0:T(8,128)(2,1)}, u32[]{:S(2)}) copy-start(bf16[256,8,128]{2,1,0:T(8,128)(2,1)} %copy-done.2) | copy-start | bytes 1572868
  61.2 1.0 %copy-start.5 = (bf16[256,8,128]{2,1,0:T(8,128)(2,1)S(1)}, bf16[256,8,128]{2,1,0:T(8,128)(2,1)}, u32[]{:S(2)}) copy-start(bf16[256,8,128]{2,1,0:T(8,128)(2,1)} %copy-done.4) | copy-start | bytes 1572868
  62.2 1.0 %copy-start.7 = (bf16[256,8,128]{2,1,0:T(8,128)(2,1)S(1)}, bf16[256,8,128]{2,1,0:T(8,128)(2,1)}, u32[]{:S(2)}) copy-start(bf16[256,8,128]{2,1,0:T(8,128)(2,1)} %copy-done.6) | copy-start | bytes 1572868
  63.2 1.0 %copy-start.9 = (bf16[256,8,128]{2,1,0:T(8,128)(2,1)S(1)}, bf16[256,8,128]{2,1,0:T(8,128)(2,1)}, u32[]{:S(2)}) copy-start(bf16[256,8,128]{2,1,0:T(8,128)(2,1)} %copy-done.8) | copy-start | bytes 1572868

commit v6 on v5

--- a/solution.py
+++ b/solution.py
@@ -16,6 +16,8 @@
 PER_Z = 8
 OCC = 128
 BACKWARD = list(range(NZ))[::-1]
+STEPS = 32000.0
+SMALLEST = 2.0**-100
 VMEM = 16 << 20
 CONTR = NZ * PER_Z * SUB
 
@@ -86,25 +88,38 @@
     lax.fori_loop(0, PAIRS, step, 0)
 
 
-def contract(picked_ref, tiles_ref, out_ref):
+def contract(picked_ref, tiles_ref, out_ref, powers_ref):
     low = lax.broadcasted_iota(jnp.int32, (OCC, OCC), 1) < TILE
+    powers_ref[...] = jnp.zeros_like(powers_ref)
     for pair in range(PAIRS):
         tiles = tiles_ref[:, pair].reshape(CONTR, OCC)
         both = lax.dot_general(
             picked_ref[pair], tiles, (((0,), (0,)), ((), ())), preferred_element_type=f32
         )
-        total = jnp.where(low, both[:OCC], both[OCC:])
+        total = jnp.where(low, both[:OCC], both[OCC:]).reshape(NZ, OCC // NZ, OCC)
+        top = jnp.max(jnp.abs(total), axis=1)
+        power = jnp.ceil(jnp.log2(jnp.maximum(top, SMALLEST)))
+        scale = jnp.exp2(-power) * STEPS
         for i, z in enumerate(BACKWARD):
-            out_ref[i, pair] = total[z * (OCC // NZ) : (z + 1) * (OCC // NZ)]
+            fixed = jnp.round(total[z] * scale[z : z + 1])
+            out_ref[i, pair] = fixed.astype(jnp.int32).astype(jnp.int16)
+            powers_ref[i, pair : pair + 1, :] = power[z : z + 1]
+    for i in range(NZ):
+        out_ref[i, PAIRS] = powers_ref[i].astype(jnp.int32).astype(jnp.int16)
 
 
 def add_up(parts_ref, out_ref):
-    total = parts_ref[0]
-    for z in range(1, NZ):
-        total = total + parts_ref[z]
+    scales = [
+        jnp.exp2(parts_ref[z, PAIRS].astype(jnp.int32).astype(f32)) * (1.0 / STEPS)
+        for z in range(NZ)
+    ]
     for pair in range(PAIRS):
-        out_ref[2 * pair] = total[pair, :, :TILE]
-        out_ref[2 * pair + 1] = total[pair, :, TILE:]
+        total = jnp.zeros((OCC // NZ, OCC), f32)
+        for z in range(NZ):
+            fixed = parts_ref[z, pair].astype(jnp.int32).astype(f32)
+            total = total + fixed * scales[z][pair : pair + 1]
+        out_ref[2 * pair] = total[:, :TILE]
+        out_ref[2 * pair + 1] = total[:, TILE:]
 
 
 def in_vmem(n):
@@ -181,9 +196,10 @@
     )(where, *owns, *others)
     sums = pl.pallas_call(
         contract,
-        out_shape=jax.ShapeDtypeStruct((NZ, PAIRS, OCC // NZ, OCC), f32),
+        out_shape=jax.ShapeDtypeStruct((NZ, PAIRS + 1, OCC // NZ, OCC), jnp.int16),
         in_specs=in_vmem(2),
         out_specs=in_vmem(1)[0],
+        scratch_shapes=[pltpu.VMEM((NZ, OCC // NZ, OCC), f32)],
         compiler_params=pltpu.CompilerParams(vmem_limit_bytes=VMEM),
         cost_estimate=cost(4),
         name="contract",

time: 90.1 us -> 87.4 us (0.970)
  the two profiles are of different devices: /device:TPU:64 before, /device:TPU:1 now
where the time goes in v6:
time: 87.4 us; the launch traced here: 86.6 us
  starting transfers between devices  43.8 us (50%)
  blocking collectives  16.6 us (19%)
  Pallas kernels  10.8 us (12%)
  local copies, waits for them, and re-layouts  9.12 us (10%)
  waiting for transfers between devices  5.87 us (7%)
    all_to_all x1, blocking collectives, local(): lax.all_to_all(sums, 'z', 0, 0, axis_index_groups=[BACKWARD], tiled=False)  16.6 us
    ppermute x2, starting transfers between devices, local(): others.append(lax.ppermute(owns[-1], 'core', [(0, 1), (1, 0)]))  14.5 us
    all_to_all x1, starting transfers between devices, local(): tiles = lax.all_to_all(split, 'z', 0, 0, tiled=False)  10 us
    ppermute x3, starting transfers between devices, local(): pieces.append(lax.ppermute(along_y, 'x', shift))  9.33 us
    unnamed x27, local copies, waits for them, and re-layouts  8.32 us
    all_to_all x1, starting transfers between devices, local(): lax.all_to_all(to_y, 'y', 0, 0, axis_index_groups=[[0, 2, 4, 6], [1, 3, 5...  7.63 us
    pallas_call x1, Pallas kernels, local(): pl.pallas_call(find, out_shape=jax.ShapeDtypeStruct((ROWS, NZ * PER_Z), j...  3.97 us
    ppermute x1, waiting for transfers between devices, local(): near = lax.ppermute(same, 'y', [(i, i ^ 1) for i in range(NY)])  3.39 us
  transfers between devices with their start and end apart: 8, of which 2 were waited for; matrix products, arithmetic and copies ran while one was open for 0% of the time, Pallas kernels for 11%

profile of v6, /device:TPU:1, one launch (start us, length us, event | category | flops | bytes accessed | tf_op | source)
XLA Modules:
  0.0 86.6 jit_solution(12852144171998052928)
XLA Ops:
  0.0 0.9 %copy-done = bf16[16,64,128]{2,1,0:T(8,128)(2,1)S(1)} copy-done((bf16[16,64,128]{2,1,0:T(8,128)(2,1)S(1)}, bf16[16,64,128]{2,1,0:T(8,128)(2,1)}, u32[]{:S(2)}) %copy-start) | copy-done | bytes 262168
  1.6 7.6 %all-to-all-start = ((bf16[4,16,8,128]{3,2,1,0:T(8,128)(2,1)}), bf16[4,16,8,128]{3,2,1,0:T(8,128)(2,1)S(1)}, u32[]{:S(2)}, u32[]{:S(2)}) async-start(bf16[4,16,8,128]{3,2,1,0:T(8,128)(2,1)} %broadcast_in_dim.3), calls=%async_computation | async-start | bytes 262144 | tf_op jit(solution)/shard_map/all_to_all | solution.py:141
  9.3 1.6 %copy-done.1 = bf16[16,8,64,64]{3,2,1,0:T(8,128)(2,1)S(1)} copy-done((bf16[16,8,64,64]{3,2,1,0:T(8,128)(2,1)S(1)}, bf16[16,8,64,64]{3,2,1,0:T(8,128)(2,1)}, u32[]{:S(2)}) %copy-start.1) | copy-done | bytes 1048600
  10.9 3.3 %split_tiles.1 = bf16[8,8,64,128]{3,2,1,0:T(8,128)(2,1)} custom-call(bf16[16,8,64,64]{3,2,1,0:T(8,128)(2,1)S(1)} %copy-done.1), custom_call_target="tpu_custom_call" | custom-call | flops 268435456 | bytes 3145728 | tf_op jit(solution)/shard_map/split_tiles/pallas_call | solution.py:155
  14.1 2.5 %all-to-all-done = bf16[4,16,8,128]{3,2,1,0:T(8,128)(2,1)S(1)} async-done(((bf16[4,16,8,128]{3,2,1,0:T(8,128)(2,1)}), bf16[4,16,8,128]{3,2,1,0:T(8,128)(2,1)S(1)}, u32[]{:S(2)}, u32[]{:S(2)}) %all-to-all-start) | async-done | bytes 131104 | tf_op jit(solution)/shard_map/all_to_all | solution.py:141
  16.6 10.0 %all-to-all-start.1 = ((bf16[8,8,64,128]{3,2,1,0:T(8,128)(2,1)}), bf16[8,8,64,128]{3,2,1,0:T(8,128)(2,1)S(1)}, u32[]{:S(2)}, u32[]{:S(2)}) async-start(bf16[8,8,64,128]{3,2,1,0:T(8,128)(2,1)} %split_tiles.1), calls=%async_computation.1 | async-start | bytes 2097152 | tf_op jit(solution)/shard_map/all_to_all | solution.py:164
  26.6 2.3 %collective-permute-start = (bf16[64,8,128]{2,1,0:T(8,128)(2,1)S(1)}, bf16[64,8,128]{2,1,0:T(8,128)(2,1)S(1)}, u32[]{:S(2)}, u32[]{:S(2)}) collective-permute-start(bf16[64,8,128]{2,1,0:T(8,128)(2,1)S(1)} %bitcast.2), channel_id=1, source_target_pairs={{0,16},{16,0},{32,48},{48,32},{64,80},{80,64},{96,112},{112,96},{1... | collective-permute-start | bytes 393224 | tf_op jit(solution)/shard_map/ppermute | solution.py:144
  29.0 3.4 %collective-permute-done = bf16[64,8,128]{2,1,0:T(8,128)(2,1)S(1)} collective-permute-done((bf16[64,8,128]{2,1,0:T(8,128)(2,1)S(1)}, bf16[64,8,128]{2,1,0:T(8,128)(2,1)S(1)}, u32[]{:S(2)}, u32[]{:S(2)}) %collective-permute-start) | collective-permute-done | bytes 131104 | tf_op jit(solution)/shard_map/ppermute | solution.py:144
  32.4 4.4 %collective-permute-start.1 = (bf16[128,8,128]{2,1,0:T(8,128)(2,1)S(1)}, bf16[128,8,128]{2,1,0:T(8,128)(2,1)S(1)}, u32[]{:S(2)}, u32[]{:S(2)}) collective-permute-start(bf16[128,8,128]{2,1,0:T(8,128)(2,1)S(1)} %pad_maximum_fusion.1), channel_id=1, source_target_pairs={{128,0},{256,128},{384,256},{0,384},{129,1},{257,129},{385,257},{1... | collective-permute-start | bytes 786440 | tf_op jit(solution)/shard_map/ppermute | solution.py:149
  36.8 2.4 %collective-permute-start.2 = (bf16[128,8,128]{2,1,0:T(8,128)(2,1)S(1)}, bf16[128,8,128]{2,1,0:T(8,128)(2,1)S(1)}, u32[]{:S(2)}, u32[]{:S(2)}) collective-permute-start(bf16[128,8,128]{2,1,0:T(8,128)(2,1)S(1)} %pad_maximum_fusion.1), channel_id=1, source_target_pairs={{256,0},{384,128},{0,256},{128,384},{257,1},{385,129},{1,257},{129... | collective-permute-start | bytes 786440 | tf_op jit(solution)/shard_map/ppermute | solution.py:149
  39.2 2.5 %collective-permute-start.3 = (bf16[128,8,128]{2,1,0:T(8,128)(2,1)S(1)}, bf16[128,8,128]{2,1,0:T(8,128)(2,1)S(1)}, u32[]{:S(2)}, u32[]{:S(2)}) collective-permute-start(bf16[128,8,128]{2,1,0:T(8,128)(2,1)S(1)} %pad_maximum_fusion.1), channel_id=1, source_target_pairs={{384,0},{0,128},{128,256},{256,384},{385,1},{1,129},{129,257},{257... | collective-permute-start | bytes 786440 | tf_op jit(solution)/shard_map/ppermute | solution.py:149
  41.8 9.7 %collective-permute-start.4 = (bf16[256,8,128]{2,1,0:T(8,128)(2,1)S(1)}, bf16[256,8,128]{2,1,0:T(8,128)(2,1)S(1)}, u32[]{:S(2)}, u32[]{:S(2)}) collective-permute-start(bf16[256,8,128]{2,1,0:T(8,128)(2,1)S(1)} %pad_maximum_fusion.refs_0_), channel_id=1, source_target_pairs={{0,8},{8,0},{1,9},{9,1},{2,10},{10,2},{3,11},{11,3},{4,12},{12,4},... | collective-permute-start | bytes 1572872 | tf_op jit(solution)/shard_map/ppermute | solution.py:153
  51.6 4.9 %collective-permute-start.5 = (bf16[256,8,128]{2,1,0:T(8,128)(2,1)S(1)}, bf16[256,8,128]{2,1,0:T(8,128)(2,1)S(1)}, u32[]{:S(2)}, u32[]{:S(2)}) collective-permute-start(bf16[256,8,128]{2,1,0:T(8,128)(2,1)S(1)} %constant_dynamic-update-slice_fusion.refs_1_), channel_id=1, source_target_pairs={{0,8},{8,0},{1,9},{9,1},{2,10},{10,2},{3,11},{11,3},{4,12},{12,4},... | collective-permute-start | bytes 1572872 | tf_op jit(solution)/shard_map/ppermute | solution.py:153
  56.6 4.0 %find.1.where_ref = s32[16,64]{1,0:T(8,128)S(1)} custom-call(s32[1024]{0:T(1024)S(1)} %fusion.9.table_ref, s32[16]{0:T(128)S(1)} %dynamic_slice.6.row_irrep_ref, s32[16,64]{1,0:T(8,128)S(1)} %copy-done.10), custom_call_target="tpu_custom_call" | custom-call | flops 268435456 | bytes 1048576 | tf_op jit(solution)/shard_map/find/pallas_call | solution.py:173
  60.6 0.8 copy-done.6
  61.4 0.8 copy-done.8
  62.2 1.0 %copy-done.3 = bf16[256,8,128]{2,1,0:T(8,128)(2,1)S(1)} copy-done((bf16[256,8,128]{2,1,0:T(8,128)(2,1)S(1)}, bf16[256,8,128]{2,1,0:T(8,128)(2,1)}, u32[]{:S(2)}) %copy-start.3) | copy-done | bytes 524312
  63.3 1.0 %copy-done.5 = bf16[256,8,128]{2,1,0:T(8,128)(2,1)S(1)} copy-done((bf16[256,8,128]{2,1,0:T(8,128)(2,1)S(1)}, bf16[256,8,128]{2,1,0:T(8,128)(2,1)}, u32[]{:S(2)}) %copy-start.5) | copy-done | bytes 524312
  64.3 1.0 %copy-done.7 = bf16[256,8,128]{2,1,0:T(8,128)(2,1)S(1)} copy-done((bf16[256,8,128]{2,1,0:T(8,128)(2,1)S(1)}, bf16[256,8,128]{2,1,0:T(8,128)(2,1)}, u32[]{:S(2)}) %copy-start.7) | copy-done | bytes 524312
  65.4 1.0 %copy-done.9 = bf16[256,8,128]{2,1,0:T(8,128)(2,1)S(1)} copy-done((bf16[256,8,128]{2,1,0:T(8,128)(2,1)S(1)}, bf16[256,8,128]{2,1,0:T(8,128)(2,1)}, u32[]{:S(2)}) %copy-start.9) | copy-done | bytes 524312
  66.4 2.0 %pick.1.picked_ref = bf16[8,512,256]{2,1,0:T(8,128)(2,1)S(1)} custom-call(s32[16,64]{1,0:T(8,128)S(1)} %find.1.where_ref, bf16[256,8,128]{2,1,0:T(8,128)(2,1)S(1)} %copy-done.3, bf16[256,8,128]{2,1,0:T(8,128)(2,1)S(1)} %copy-done.5, bf16[256,8,128]{2,1,0:T(8,128)(2,1)S(1)} %copy-done.7, bf16[256,8,128]{2,1,0:T(8,128)(2,1)S(1)} %copy-done.9), custom_call_target="tpu_custom_call" | custom-call | flops 268435456 | bytes 6291456 | tf_op jit(solution)/shard_map/pick/pallas_call | solution.py:183
  68.4 0.8 contract.1
  69.2 16.6 %all_to_all.15.parts_ref = s16[8,9,16,128]{3,2,1,0:T(8,128)(2,1)S(1)} all-to-all(s16[8,9,16,128]{3,2,1,0:T(8,128)(2,1)S(1)} %contract.1), channel_id=1, replica_groups={{7,6,5,4,3,2,1,0},{15,14,13,12,11,10,9,8},{23,22,21,20,19,18,17,16},{31..., dimensions={0} | all-to-all | bytes 589824 | tf_op jit(solution)/shard_map/all_to_all | solution.py:207
  85.8 0.8 add_up.1
  (32 shorter events, 1.0 us)
Async XLA Ops:
  0.0 1.0 %copy-start = (bf16[16,64,128]{2,1,0:T(8,128)(2,1)S(1)}, bf16[16,64,128]{2,1,0:T(8,128)(2,1)}, u32[]{:S(2)}) copy-start(bf16[16,64,128]{2,1,0:T(8,128)(2,1)} %param.5) | copy-start | bytes 786436
  1.6 15.0 %all-to-all-start = ((bf16[4,16,8,128]{3,2,1,0:T(8,128)(2,1)}), bf16[4,16,8,128]{3,2,1,0:T(8,128)(2,1)S(1)}, u32[]{:S(2)}, u32[]{:S(2)}) async-start(bf16[4,16,8,128]{3,2,1,0:T(8,128)(2,1)} %broadcast_in_dim.3), calls=%async_computation | async-start | bytes 262144 | tf_op jit(solution)/shard_map/all_to_all | solution.py:141
  9.3 1.6 %copy-start.1 = (bf16[16,8,64,64]{3,2,1,0:T(8,128)(2,1)S(1)}, bf16[16,8,64,64]{3,2,1,0:T(8,128)(2,1)}, u32[]{:S(2)}) copy-start(bf16[16,8,64,64]{3,2,1,0:T(8,128)(2,1)} %tiles_ref.1) | copy-start | bytes 3145732
  14.1 42.4 %copy-start.11 = (s32[1024]{0:T(1024)S(1)}, s32[1024]{0:T(1024)}, u32[]{:S(2)}) copy-start(s32[1024]{0:T(1024)} %param.9) | copy-start | bytes 12292
  14.1 42.4 %copy-start.12 = (s32[1024]{0:T(1024)S(1)}, s32[1024]{0:T(1024)}, u32[]{:S(2)}) copy-start(s32[1024]{0:T(1024)} %param.6) | copy-start | bytes 12292
  14.1 42.5 %copy-start.10 = (s32[16,64]{1,0:T(8,128)S(1)}, s32[16,64]{1,0:T(8,128)}, u32[]{:S(2)}) copy-start(s32[16,64]{1,0:T(8,128)} %cols_ref.1) | copy-start | bytes 12292
  16.6 51.8 %all-to-all-start.1 = ((bf16[8,8,64,128]{3,2,1,0:T(8,128)(2,1)}), bf16[8,8,64,128]{3,2,1,0:T(8,128)(2,1)S(1)}, u32[]{:S(2)}, u32[]{:S(2)}) async-start(bf16[8,8,64,128]{3,2,1,0:T(8,128)(2,1)} %split_tiles.1), calls=%async_computation.1 | async-start | bytes 2097152 | tf_op jit(solution)/shard_map/all_to_all | solution.py:164
  26.6 5.7 %collective-permute-start = (bf16[64,8,128]{2,1,0:T(8,128)(2,1)S(1)}, bf16[64,8,128]{2,1,0:T(8,128)(2,1)S(1)}, u32[]{:S(2)}, u32[]{:S(2)}) collective-permute-start(bf16[64,8,128]{2,1,0:T(8,128)(2,1)S(1)} %bitcast.2), channel_id=1, source_target_pairs={{0,16},{16,0},{32,48},{48,32},{64,80},{80,64},{96,112},{112,96},{1... | collective-permute-start | bytes 393224 | tf_op jit(solution)/shard_map/ppermute | solution.py:144
  32.4 9.4 %collective-permute-start.1 = (bf16[128,8,128]{2,1,0:T(8,128)(2,1)S(1)}, bf16[128,8,128]{2,1,0:T(8,128)(2,1)S(1)}, u32[]{:S(2)}, u32[]{:S(2)}) collective-permute-start(bf16[128,8,128]{2,1,0:T(8,128)(2,1)S(1)} %pad_maximum_fusion.1), channel_id=1, source_target_pairs={{128,0},{256,128},{384,256},{0,384},{129,1},{257,129},{385,257},{1... | collective-permute-start | bytes 786440 | tf_op jit(solution)/shard_map/ppermute | solution.py:149
  36.8 14.7 %collective-permute-start.2 = (bf16[128,8,128]{2,1,0:T(8,128)(2,1)S(1)}, bf16[128,8,128]{2,1,0:T(8,128)(2,1)S(1)}, u32[]{:S(2)}, u32[]{:S(2)}) collective-permute-start(bf16[128,8,128]{2,1,0:T(8,128)(2,1)S(1)} %pad_maximum_fusion.1), channel_id=1, source_target_pairs={{256,0},{384,128},{0,256},{128,384},{257,1},{385,129},{1,257},{129... | collective-permute-start | bytes 786440 | tf_op jit(solution)/shard_map/ppermute | solution.py:149
  39.2 12.3 %collective-permute-start.3 = (bf16[128,8,128]{2,1,0:T(8,128)(2,1)S(1)}, bf16[128,8,128]{2,1,0:T(8,128)(2,1)S(1)}, u32[]{:S(2)}, u32[]{:S(2)}) collective-permute-start(bf16[128,8,128]{2,1,0:T(8,128)(2,1)S(1)} %pad_maximum_fusion.1), channel_id=1, source_target_pairs={{384,0},{0,128},{128,256},{256,384},{385,1},{1,129},{129,257},{257... | collective-permute-start | bytes 786440 | tf_op jit(solution)/shard_map/ppermute | solution.py:149
  41.8 18.8 %copy-start.2 = (bf16[256,8,128]{2,1,0:T(8,128)(2,1)}, bf16[256,8,128]{2,1,0:T(8,128)(2,1)S(1)}, u32[]{:S(2)}) copy-start(bf16[256,8,128]{2,1,0:T(8,128)(2,1)S(1)} %pad_maximum_fusion.refs_0_) | copy-start | bytes 1572868
  41.8 18.8 %collective-permute-start.4 = (bf16[256,8,128]{2,1,0:T(8,128)(2,1)S(1)}, bf16[256,8,128]{2,1,0:T(8,128)(2,1)S(1)}, u32[]{:S(2)}, u32[]{:S(2)}) collective-permute-start(bf16[256,8,128]{2,1,0:T(8,128)(2,1)S(1)} %pad_maximum_fusion.refs_0_), channel_id=1, source_target_pairs={{0,8},{8,0},{1,9},{9,1},{2,10},{10,2},{3,11},{11,3},{4,12},{12,4},... | collective-permute-start | bytes 1572872 | tf_op jit(solution)/shard_map/ppermute | solution.py:153
  51.6 9.0 %copy-start.4 = (bf16[256,8,128]{2,1,0:T(8,128)(2,1)}, bf16[256,8,128]{2,1,0:T(8,128)(2,1)S(1)}, u32[]{:S(2)}) copy-start(bf16[256,8,128]{2,1,0:T(8,128)(2,1)S(1)} %constant_dynamic-update-slice_fusion.refs_1_) | copy-start | bytes 1572868
  51.6 9.8 %collective-permute-start.5 = (bf16[256,8,128]{2,1,0:T(8,128)(2,1)S(1)}, bf16[256,8,128]{2,1,0:T(8,128)(2,1)S(1)}, u32[]{:S(2)}, u32[]{:S(2)}) collective-permute-start(bf16[256,8,128]{2,1,0:T(8,128)(2,1)S(1)} %constant_dynamic-update-slice_fusion.refs_1_), channel_id=1, source_target_pairs={{0,8},{8,0},{1,9},{9,1},{2,10},{10,2},{3,11},{11,3},{4,12},{12,4},... | collective-permute-start | bytes 1572872 | tf_op jit(solution)/shard_map/ppermute | solution.py:153
  60.6 0.8 copy-start.6
  61.4 0.8 copy-start.8
  62.2 1.0 %copy-start.3 = (bf16[256,8,128]{2,1,0:T(8,128)(2,1)S(1)}, bf16[256,8,128]{2,1,0:T(8,128)(2,1)}, u32[]{:S(2)}) copy-start(bf16[256,8,128]{2,1,0:T(8,128)(2,1)} %copy-done.2) | copy-start | bytes 1572868
  63.3 1.0 %copy-start.5 = (bf16[256,8,128]{2,1,0:T(8,128)(2,1)S(1)}, bf16[256,8,128]{2,1,0:T(8,128)(2,1)}, u32[]{:S(2)}) copy-start(bf16[256,8,128]{2,1,0:T(8,128)(2,1)} %copy-done.4) | copy-start | bytes 1572868
  64.3 1.0 %copy-start.7 = (bf16[256,8,128]{2,1,0:T(8,128)(2,1)S(1)}, bf16[256,8,128]{2,1,0:T(8,128)(2,1)}, u32[]{:S(2)}) copy-start(bf16[256,8,128]{2,1,0:T(8,128)(2,1)} %copy-done.6) | copy-start | bytes 1572868
  65.3 1.0 %copy-start.9 = (bf16[256,8,128]{2,1,0:T(8,128)(2,1)S(1)}, bf16[256,8,128]{2,1,0:T(8,128)(2,1)}, u32[]{:S(2)}) copy-start(bf16[256,8,128]{2,1,0:T(8,128)(2,1)} %copy-done.8) | copy-start | bytes 1572868

commit v7 on v6

--- a/solution.py
+++ b/solution.py
@@ -15,7 +15,8 @@
 SUB = TILE // NZ
 PER_Z = 8
 OCC = 128
-BACKWARD = list(range(NZ))[::-1]
+TILES_ORDER = [0, 1, 2, 3, 4, 5, 6, 7]
+SUMS_ORDER = [4, 5, 6, 7, 0, 1, 2, 3]
 STEPS = 32000.0
 SMALLEST = 2.0**-100
 VMEM = 16 << 20
@@ -39,8 +40,8 @@
             turned = lax.dot_general(
                 eye, both, (((1,), (1,)), ((), ())), preferred_element_type=f32
             ).astype(bf16)
-            for z in range(NZ):
-                out_ref[z, pair, n * SUB : (n + 1) * SUB, :] = turned[
+            for i, z in enumerate(TILES_ORDER):
+                out_ref[i, pair, n * SUB : (n + 1) * SUB, :] = turned[
                     z * SUB : (z + 1) * SUB, :
                 ]
         return carry
@@ -52,7 +53,9 @@
     def step(row, carry):
         irrep = row_irrep_ref[row]
         for n in range(NZ * PER_Z):
-            entry = table_ref[cols_ref[row, n]]
+            entry = table_ref[
+                cols_ref[row, TILES_ORDER[n // PER_Z] * PER_Z + n % PER_Z]
+            ]
             out_ref[row, n] = jnp.where(
                 jnp.bitwise_and(entry, NIRR - 1) == irrep,
                 lax.shift_right_logical(entry, 3),
@@ -100,7 +103,7 @@
         top = jnp.max(jnp.abs(total), axis=1)
         power = jnp.ceil(jnp.log2(jnp.maximum(top, SMALLEST)))
         scale = jnp.exp2(-power) * STEPS
-        for i, z in enumerate(BACKWARD):
+        for i, z in enumerate(SUMS_ORDER):
             fixed = jnp.round(total[z] * scale[z : z + 1])
             out_ref[i, pair] = fixed.astype(jnp.int32).astype(jnp.int16)
             powers_ref[i, pair : pair + 1, :] = power[z : z + 1]
@@ -204,7 +207,7 @@
         cost_estimate=cost(4),
         name="contract",
     )(picked, tiles)
-    parts = lax.all_to_all(sums, "z", 0, 0, axis_index_groups=[BACKWARD], tiled=False)
+    parts = lax.all_to_all(sums, "z", 0, 0, axis_index_groups=[SUMS_ORDER], tiled=False)
 
     total = pl.pallas_call(
         add_up,

time: 87.4 us -> 86.1 us (0.985)
  blocking collectives: 16.6 us -> 15.4 us
    all_to_all x1, blocking collectives: 16.6 us -> 15.4 us  [local(): lax.all_to_all(sums, 'z', 0, 0, axis_index_groups=[SUMS_ORDER], tiled=False)]
where the time goes in v7:
time: 86.1 us; the launch traced here: 85.4 us
  starting transfers between devices  43.8 us (51%)
  blocking collectives  15.4 us (18%)
  Pallas kernels  10.8 us (13%)
  local copies, waits for them, and re-layouts  9.12 us (11%)
  waiting for transfers between devices  5.87 us (7%)
    all_to_all x1, blocking collectives, local(): lax.all_to_all(sums, 'z', 0, 0, axis_index_groups=[SUMS_ORDER], tiled=False)  15.4 us
    ppermute x2, starting transfers between devices, local(): others.append(lax.ppermute(owns[-1], 'core', [(0, 1), (1, 0)]))  14.5 us
    all_to_all x1, starting transfers between devices, local(): tiles = lax.all_to_all(split, 'z', 0, 0, tiled=False)  10 us
    ppermute x3, starting transfers between devices, local(): pieces.append(lax.ppermute(along_y, 'x', shift))  9.33 us
    unnamed x27, local copies, waits for them, and re-layouts  8.32 us
    all_to_all x1, starting transfers between devices, local(): lax.all_to_all(to_y, 'y', 0, 0, axis_index_groups=[[0, 2, 4, 6], [1, 3, 5...  7.63 us
    pallas_call x1, Pallas kernels, local(): pl.pallas_call(find, out_shape=jax.ShapeDtypeStruct((ROWS, NZ * PER_Z), j...  3.97 us
    ppermute x1, waiting for transfers between devices, local(): near = lax.ppermute(same, 'y', [(i, i ^ 1) for i in range(NY)])  3.39 us
  transfers between devices with their start and end apart: 8, of which 2 were waited for; matrix products, arithmetic and copies ran while one was open for 0% of the time, Pallas kernels for 11%

profile of v7, /device:TPU:1, one launch (start us, length us, event | category | flops | bytes accessed | tf_op | source)
XLA Modules:
  0.0 85.4 jit_solution(11153751051319238770)
XLA Ops:
  0.0 0.9 %copy-done = bf16[16,64,128]{2,1,0:T(8,128)(2,1)S(1)} copy-done((bf16[16,64,128]{2,1,0:T(8,128)(2,1)S(1)}, bf16[16,64,128]{2,1,0:T(8,128)(2,1)}, u32[]{:S(2)}) %copy-start) | copy-done | bytes 262168
  1.6 7.6 %all-to-all-start = ((bf16[4,16,8,128]{3,2,1,0:T(8,128)(2,1)}), bf16[4,16,8,128]{3,2,1,0:T(8,128)(2,1)S(1)}, u32[]{:S(2)}, u32[]{:S(2)}) async-start(bf16[4,16,8,128]{3,2,1,0:T(8,128)(2,1)} %broadcast_in_dim.3), calls=%async_computation | async-start | bytes 262144 | tf_op jit(solution)/shard_map/all_to_all | solution.py:144
  9.3 1.6 %copy-done.1 = bf16[16,8,64,64]{3,2,1,0:T(8,128)(2,1)S(1)} copy-done((bf16[16,8,64,64]{3,2,1,0:T(8,128)(2,1)S(1)}, bf16[16,8,64,64]{3,2,1,0:T(8,128)(2,1)}, u32[]{:S(2)}) %copy-start.1) | copy-done | bytes 1048600
  10.9 3.3 %split_tiles.1 = bf16[8,8,64,128]{3,2,1,0:T(8,128)(2,1)} custom-call(bf16[16,8,64,64]{3,2,1,0:T(8,128)(2,1)S(1)} %copy-done.1), custom_call_target="tpu_custom_call" | custom-call | flops 268435456 | bytes 3145728 | tf_op jit(solution)/shard_map/split_tiles/pallas_call | solution.py:158
  14.1 2.5 %all-to-all-done = bf16[4,16,8,128]{3,2,1,0:T(8,128)(2,1)S(1)} async-done(((bf16[4,16,8,128]{3,2,1,0:T(8,128)(2,1)}), bf16[4,16,8,128]{3,2,1,0:T(8,128)(2,1)S(1)}, u32[]{:S(2)}, u32[]{:S(2)}) %all-to-all-start) | async-done | bytes 131104 | tf_op jit(solution)/shard_map/all_to_all | solution.py:144
  16.6 10.0 %all-to-all-start.1 = ((bf16[8,8,64,128]{3,2,1,0:T(8,128)(2,1)}), bf16[8,8,64,128]{3,2,1,0:T(8,128)(2,1)S(1)}, u32[]{:S(2)}, u32[]{:S(2)}) async-start(bf16[8,8,64,128]{3,2,1,0:T(8,128)(2,1)} %split_tiles.1), calls=%async_computation.1 | async-start | bytes 2097152 | tf_op jit(solution)/shard_map/all_to_all | solution.py:167
  26.6 2.3 %collective-permute-start = (bf16[64,8,128]{2,1,0:T(8,128)(2,1)S(1)}, bf16[64,8,128]{2,1,0:T(8,128)(2,1)S(1)}, u32[]{:S(2)}, u32[]{:S(2)}) collective-permute-start(bf16[64,8,128]{2,1,0:T(8,128)(2,1)S(1)} %bitcast.2), channel_id=1, source_target_pairs={{0,16},{16,0},{32,48},{48,32},{64,80},{80,64},{96,112},{112,96},{1... | collective-permute-start | bytes 393224 | tf_op jit(solution)/shard_map/ppermute | solution.py:147
  29.0 3.4 %collective-permute-done = bf16[64,8,128]{2,1,0:T(8,128)(2,1)S(1)} collective-permute-done((bf16[64,8,128]{2,1,0:T(8,128)(2,1)S(1)}, bf16[64,8,128]{2,1,0:T(8,128)(2,1)S(1)}, u32[]{:S(2)}, u32[]{:S(2)}) %collective-permute-start) | collective-permute-done | bytes 131104 | tf_op jit(solution)/shard_map/ppermute | solution.py:147
  32.4 4.4 %collective-permute-start.1 = (bf16[128,8,128]{2,1,0:T(8,128)(2,1)S(1)}, bf16[128,8,128]{2,1,0:T(8,128)(2,1)S(1)}, u32[]{:S(2)}, u32[]{:S(2)}) collective-permute-start(bf16[128,8,128]{2,1,0:T(8,128)(2,1)S(1)} %pad_maximum_fusion.1), channel_id=1, source_target_pairs={{128,0},{256,128},{384,256},{0,384},{129,1},{257,129},{385,257},{1... | collective-permute-start | bytes 786440 | tf_op jit(solution)/shard_map/ppermute | solution.py:152
  36.8 2.4 %collective-permute-start.2 = (bf16[128,8,128]{2,1,0:T(8,128)(2,1)S(1)}, bf16[128,8,128]{2,1,0:T(8,128)(2,1)S(1)}, u32[]{:S(2)}, u32[]{:S(2)}) collective-permute-start(bf16[128,8,128]{2,1,0:T(8,128)(2,1)S(1)} %pad_maximum_fusion.1), channel_id=1, source_target_pairs={{256,0},{384,128},{0,256},{128,384},{257,1},{385,129},{1,257},{129... | collective-permute-start | bytes 786440 | tf_op jit(solution)/shard_map/ppermute | solution.py:152
  39.2 2.5 %collective-permute-start.3 = (bf16[128,8,128]{2,1,0:T(8,128)(2,1)S(1)}, bf16[128,8,128]{2,1,0:T(8,128)(2,1)S(1)}, u32[]{:S(2)}, u32[]{:S(2)}) collective-permute-start(bf16[128,8,128]{2,1,0:T(8,128)(2,1)S(1)} %pad_maximum_fusion.1), channel_id=1, source_target_pairs={{384,0},{0,128},{128,256},{256,384},{385,1},{1,129},{129,257},{257... | collective-permute-start | bytes 786440 | tf_op jit(solution)/shard_map/ppermute | solution.py:152
  41.8 9.7 %collective-permute-start.4 = (bf16[256,8,128]{2,1,0:T(8,128)(2,1)S(1)}, bf16[256,8,128]{2,1,0:T(8,128)(2,1)S(1)}, u32[]{:S(2)}, u32[]{:S(2)}) collective-permute-start(bf16[256,8,128]{2,1,0:T(8,128)(2,1)S(1)} %pad_maximum_fusion.refs_0_), channel_id=1, source_target_pairs={{0,8},{8,0},{1,9},{9,1},{2,10},{10,2},{3,11},{11,3},{4,12},{12,4},... | collective-permute-start | bytes 1572872 | tf_op jit(solution)/shard_map/ppermute | solution.py:156
  51.6 4.9 %collective-permute-start.5 = (bf16[256,8,128]{2,1,0:T(8,128)(2,1)S(1)}, bf16[256,8,128]{2,1,0:T(8,128)(2,1)S(1)}, u32[]{:S(2)}, u32[]{:S(2)}) collective-permute-start(bf16[256,8,128]{2,1,0:T(8,128)(2,1)S(1)} %constant_dynamic-update-slice_fusion.refs_1_), channel_id=1, source_target_pairs={{0,8},{8,0},{1,9},{9,1},{2,10},{10,2},{3,11},{11,3},{4,12},{12,4},... | collective-permute-start | bytes 1572872 | tf_op jit(solution)/shard_map/ppermute | solution.py:156
  56.6 4.0 %find.1.where_ref = s32[16,64]{1,0:T(8,128)S(1)} custom-call(s32[1024]{0:T(1024)S(1)} %fusion.9.table_ref, s32[16]{0:T(128)S(1)} %dynamic_slice.6.row_irrep_ref, s32[16,64]{1,0:T(8,128)S(1)} %copy-done.10), custom_call_target="tpu_custom_call" | custom-call | flops 268435456 | bytes 1048576 | tf_op jit(solution)/shard_map/find/pallas_call | solution.py:176
  60.6 0.8 copy-done.6
  61.4 0.8 copy-done.8
  62.2 1.0 %copy-done.3 = bf16[256,8,128]{2,1,0:T(8,128)(2,1)S(1)} copy-done((bf16[256,8,128]{2,1,0:T(8,128)(2,1)S(1)}, bf16[256,8,128]{2,1,0:T(8,128)(2,1)}, u32[]{:S(2)}) %copy-start.3) | copy-done | bytes 524312
  63.3 1.0 %copy-done.5 = bf16[256,8,128]{2,1,0:T(8,128)(2,1)S(1)} copy-done((bf16[256,8,128]{2,1,0:T(8,128)(2,1)S(1)}, bf16[256,8,128]{2,1,0:T(8,128)(2,1)}, u32[]{:S(2)}) %copy-start.5) | copy-done | bytes 524312
  64.3 1.0 %copy-done.7 = bf16[256,8,128]{2,1,0:T(8,128)(2,1)S(1)} copy-done((bf16[256,8,128]{2,1,0:T(8,128)(2,1)S(1)}, bf16[256,8,128]{2,1,0:T(8,128)(2,1)}, u32[]{:S(2)}) %copy-start.7) | copy-done | bytes 524312
  65.4 1.0 %copy-done.9 = bf16[256,8,128]{2,1,0:T(8,128)(2,1)S(1)} copy-done((bf16[256,8,128]{2,1,0:T(8,128)(2,1)S(1)}, bf16[256,8,128]{2,1,0:T(8,128)(2,1)}, u32[]{:S(2)}) %copy-start.9) | copy-done | bytes 524312
  66.4 2.0 %pick.1.picked_ref = bf16[8,512,256]{2,1,0:T(8,128)(2,1)S(1)} custom-call(s32[16,64]{1,0:T(8,128)S(1)} %find.1.where_ref, bf16[256,8,128]{2,1,0:T(8,128)(2,1)S(1)} %copy-done.3, bf16[256,8,128]{2,1,0:T(8,128)(2,1)S(1)} %copy-done.5, bf16[256,8,128]{2,1,0:T(8,128)(2,1)S(1)} %copy-done.7, bf16[256,8,128]{2,1,0:T(8,128)(2,1)S(1)} %copy-done.9), custom_call_target="tpu_custom_call" | custom-call | flops 268435456 | bytes 6291456 | tf_op jit(solution)/shard_map/pick/pallas_call | solution.py:186
  68.4 0.8 contract.1
  69.2 15.4 %all_to_all.15.parts_ref = s16[8,9,16,128]{3,2,1,0:T(8,128)(2,1)S(1)} all-to-all(s16[8,9,16,128]{3,2,1,0:T(8,128)(2,1)S(1)} %contract.1), channel_id=1, replica_groups={{4,5,6,7,0,1,2,3},{12,13,14,15,8,9,10,11},{20,21,22,23,16,17,18,19},{28..., dimensions={0} | all-to-all | bytes 589824 | tf_op jit(solution)/shard_map/all_to_all | solution.py:210
  84.6 0.8 add_up.1
  (32 shorter events, 1.0 us)
Async XLA Ops:
  0.0 1.0 %copy-start = (bf16[16,64,128]{2,1,0:T(8,128)(2,1)S(1)}, bf16[16,64,128]{2,1,0:T(8,128)(2,1)}, u32[]{:S(2)}) copy-start(bf16[16,64,128]{2,1,0:T(8,128)(2,1)} %param.5) | copy-start | bytes 786436
  1.6 15.0 %all-to-all-start = ((bf16[4,16,8,128]{3,2,1,0:T(8,128)(2,1)}), bf16[4,16,8,128]{3,2,1,0:T(8,128)(2,1)S(1)}, u32[]{:S(2)}, u32[]{:S(2)}) async-start(bf16[4,16,8,128]{3,2,1,0:T(8,128)(2,1)} %broadcast_in_dim.3), calls=%async_computation | async-start | bytes 262144 | tf_op jit(solution)/shard_map/all_to_all | solution.py:144
  9.3 1.6 %copy-start.1 = (bf16[16,8,64,64]{3,2,1,0:T(8,128)(2,1)S(1)}, bf16[16,8,64,64]{3,2,1,0:T(8,128)(2,1)}, u32[]{:S(2)}) copy-start(bf16[16,8,64,64]{3,2,1,0:T(8,128)(2,1)} %tiles_ref.1) | copy-start | bytes 3145732
  14.1 42.4 %copy-start.11 = (s32[1024]{0:T(1024)S(1)}, s32[1024]{0:T(1024)}, u32[]{:S(2)}) copy-start(s32[1024]{0:T(1024)} %param.9) | copy-start | bytes 12292
  14.1 42.4 %copy-start.12 = (s32[1024]{0:T(1024)S(1)}, s32[1024]{0:T(1024)}, u32[]{:S(2)}) copy-start(s32[1024]{0:T(1024)} %param.6) | copy-start | bytes 12292
  14.1 42.5 %copy-start.10 = (s32[16,64]{1,0:T(8,128)S(1)}, s32[16,64]{1,0:T(8,128)}, u32[]{:S(2)}) copy-start(s32[16,64]{1,0:T(8,128)} %cols_ref.1) | copy-start | bytes 12292
  16.6 51.8 %all-to-all-start.1 = ((bf16[8,8,64,128]{3,2,1,0:T(8,128)(2,1)}), bf16[8,8,64,128]{3,2,1,0:T(8,128)(2,1)S(1)}, u32[]{:S(2)}, u32[]{:S(2)}) async-start(bf16[8,8,64,128]{3,2,1,0:T(8,128)(2,1)} %split_tiles.1), calls=%async_computation.1 | async-start | bytes 2097152 | tf_op jit(solution)/shard_map/all_to_all | solution.py:167
  26.6 5.7 %collective-permute-start = (bf16[64,8,128]{2,1,0:T(8,128)(2,1)S(1)}, bf16[64,8,128]{2,1,0:T(8,128)(2,1)S(1)}, u32[]{:S(2)}, u32[]{:S(2)}) collective-permute-start(bf16[64,8,128]{2,1,0:T(8,128)(2,1)S(1)} %bitcast.2), channel_id=1, source_target_pairs={{0,16},{16,0},{32,48},{48,32},{64,80},{80,64},{96,112},{112,96},{1... | collective-permute-start | bytes 393224 | tf_op jit(solution)/shard_map/ppermute | solution.py:147
  32.4 9.4 %collective-permute-start.1 = (bf16[128,8,128]{2,1,0:T(8,128)(2,1)S(1)}, bf16[128,8,128]{2,1,0:T(8,128)(2,1)S(1)}, u32[]{:S(2)}, u32[]{:S(2)}) collective-permute-start(bf16[128,8,128]{2,1,0:T(8,128)(2,1)S(1)} %pad_maximum_fusion.1), channel_id=1, source_target_pairs={{128,0},{256,128},{384,256},{0,384},{129,1},{257,129},{385,257},{1... | collective-permute-start | bytes 786440 | tf_op jit(solution)/shard_map/ppermute | solution.py:152
  36.8 14.7 %collective-permute-start.2 = (bf16[128,8,128]{2,1,0:T(8,128)(2,1)S(1)}, bf16[128,8,128]{2,1,0:T(8,128)(2,1)S(1)}, u32[]{:S(2)}, u32[]{:S(2)}) collective-permute-start(bf16[128,8,128]{2,1,0:T(8,128)(2,1)S(1)} %pad_maximum_fusion.1), channel_id=1, source_target_pairs={{256,0},{384,128},{0,256},{128,384},{257,1},{385,129},{1,257},{129... | collective-permute-start | bytes 786440 | tf_op jit(solution)/shard_map/ppermute | solution.py:152
  39.2 12.3 %collective-permute-start.3 = (bf16[128,8,128]{2,1,0:T(8,128)(2,1)S(1)}, bf16[128,8,128]{2,1,0:T(8,128)(2,1)S(1)}, u32[]{:S(2)}, u32[]{:S(2)}) collective-permute-start(bf16[128,8,128]{2,1,0:T(8,128)(2,1)S(1)} %pad_maximum_fusion.1), channel_id=1, source_target_pairs={{384,0},{0,128},{128,256},{256,384},{385,1},{1,129},{129,257},{257... | collective-permute-start | bytes 786440 | tf_op jit(solution)/shard_map/ppermute | solution.py:152
  41.8 18.8 %copy-start.2 = (bf16[256,8,128]{2,1,0:T(8,128)(2,1)}, bf16[256,8,128]{2,1,0:T(8,128)(2,1)S(1)}, u32[]{:S(2)}) copy-start(bf16[256,8,128]{2,1,0:T(8,128)(2,1)S(1)} %pad_maximum_fusion.refs_0_) | copy-start | bytes 1572868
  41.8 18.8 %collective-permute-start.4 = (bf16[256,8,128]{2,1,0:T(8,128)(2,1)S(1)}, bf16[256,8,128]{2,1,0:T(8,128)(2,1)S(1)}, u32[]{:S(2)}, u32[]{:S(2)}) collective-permute-start(bf16[256,8,128]{2,1,0:T(8,128)(2,1)S(1)} %pad_maximum_fusion.refs_0_), channel_id=1, source_target_pairs={{0,8},{8,0},{1,9},{9,1},{2,10},{10,2},{3,11},{11,3},{4,12},{12,4},... | collective-permute-start | bytes 1572872 | tf_op jit(solution)/shard_map/ppermute | solution.py:156
  51.6 9.0 %copy-start.4 = (bf16[256,8,128]{2,1,0:T(8,128)(2,1)}, bf16[256,8,128]{2,1,0:T(8,128)(2,1)S(1)}, u32[]{:S(2)}) copy-start(bf16[256,8,128]{2,1,0:T(8,128)(2,1)S(1)} %constant_dynamic-update-slice_fusion.refs_1_) | copy-start | bytes 1572868
  51.6 9.8 %collective-permute-start.5 = (bf16[256,8,128]{2,1,0:T(8,128)(2,1)S(1)}, bf16[256,8,128]{2,1,0:T(8,128)(2,1)S(1)}, u32[]{:S(2)}, u32[]{:S(2)}) collective-permute-start(bf16[256,8,128]{2,1,0:T(8,128)(2,1)S(1)} %constant_dynamic-update-slice_fusion.refs_1_), channel_id=1, source_target_pairs={{0,8},{8,0},{1,9},{9,1},{2,10},{10,2},{3,11},{11,3},{4,12},{12,4},... | collective-permute-start | bytes 1572872 | tf_op jit(solution)/shard_map/ppermute | solution.py:156
  60.6 0.8 copy-start.6
  61.4 0.8 copy-start.8
  62.2 1.0 %copy-start.3 = (bf16[256,8,128]{2,1,0:T(8,128)(2,1)S(1)}, bf16[256,8,128]{2,1,0:T(8,128)(2,1)}, u32[]{:S(2)}) copy-start(bf16[256,8,128]{2,1,0:T(8,128)(2,1)} %copy-done.2) | copy-start | bytes 1572868
  63.3 1.0 %copy-start.5 = (bf16[256,8,128]{2,1,0:T(8,128)(2,1)S(1)}, bf16[256,8,128]{2,1,0:T(8,128)(2,1)}, u32[]{:S(2)}) copy-start(bf16[256,8,128]{2,1,0:T(8,128)(2,1)} %copy-done.4) | copy-start | bytes 1572868
  64.3 1.0 %copy-start.7 = (bf16[256,8,128]{2,1,0:T(8,128)(2,1)S(1)}, bf16[256,8,128]{2,1,0:T(8,128)(2,1)}, u32[]{:S(2)}) copy-start(bf16[256,8,128]{2,1,0:T(8,128)(2,1)} %copy-done.6) | copy-start | bytes 1572868
  65.3 1.0 %copy-start.9 = (bf16[256,8,128]{2,1,0:T(8,128)(2,1)S(1)}, bf16[256,8,128]{2,1,0:T(8,128)(2,1)}, u32[]{:S(2)}) copy-start(bf16[256,8,128]{2,1,0:T(8,128)(2,1)} %copy-done.8) | copy-start | bytes 1572868

commit v8 on v7

--- a/solution.py
+++ b/solution.py
@@ -151,7 +151,7 @@
         shift = [((i + k) % NX, i) for i in range(NX)]
         pieces.append(lax.ppermute(along_y, "x", shift))
     owns, others = [], []
-    for two in (pieces[:2], pieces[2:]):
+    for two in (pieces[::2], pieces[1::2]):
         owns.append(jnp.concatenate(two, axis=0))
         others.append(lax.ppermute(owns[-1], "core", [(0, 1), (1, 0)]))
 
@@ -169,7 +169,8 @@
     holder = block_slot // ROWS
     holder_x, holder_y = holder // (NY * NC), (holder // NC) % NY
     near = (holder_y + y) % 2 * (NY // 2) + holder_y // 2
-    place = ((holder_x - x) % NX) * NY + near + (holder + core) % NC * (NX * NY)
+    apart = (holder_x - x) % NX
+    place = (apart % 2 * 2 + apart // 2) * NY + near + (holder + core) % NC * (NX * NY)
     table = (place * ROWS + block_slot % ROWS) * NIRR + irreps
     first_row = ((x * NY + y) * NC + core) * ROWS
     row_irrep = lax.dynamic_slice_in_dim(irreps, first_row, ROWS, 0)

time: 86.1 us -> 85.5 us (level)
    ppermute x2, starting transfers between devices: 14.5 us -> 13.3 us  [local(): others.append(lax.ppermute(owns[-1], 'core', [(0, 1), (1, 0)]))]
where the time goes in v8:
time: 85.5 us; the launch traced here: 84.7 us
  starting transfers between devices  43.2 us (51%)
  blocking collectives  15.4 us (18%)
  Pallas kernels  10.8 us (13%)
  local copies, waits for them, and re-layouts  9.12 us (11%)
  waiting for transfers between devices  5.87 us (7%)
    all_to_all x1, blocking collectives, local(): lax.all_to_all(sums, 'z', 0, 0, axis_index_groups=[SUMS_ORDER], tiled=False)  15.4 us
    ppermute x2, starting transfers between devices, local(): others.append(lax.ppermute(owns[-1], 'core', [(0, 1), (1, 0)]))  13.3 us
    all_to_all x1, starting transfers between devices, local(): tiles = lax.all_to_all(split, 'z', 0, 0, tiled=False)  10 us
    ppermute x3, starting transfers between devices, local(): pieces.append(lax.ppermute(along_y, 'x', shift))  9.93 us
    unnamed x27, local copies, waits for them, and re-layouts  8.32 us
    all_to_all x1, starting transfers between devices, local(): lax.all_to_all(to_y, 'y', 0, 0, axis_index_groups=[[0, 2, 4, 6], [1, 3, 5...  7.63 us
    pallas_call x1, Pallas kernels, local(): pl.pallas_call(find, out_shape=jax.ShapeDtypeStruct((ROWS, NZ * PER_Z), j...  3.97 us
    ppermute x1, waiting for transfers between devices, local(): near = lax.ppermute(same, 'y', [(i, i ^ 1) for i in range(NY)])  3.39 us
  transfers between devices with their start and end apart: 8, of which 2 were waited for; matrix products, arithmetic and copies ran while one was open for 0% of the time, Pallas kernels for 11%

profile of v8, /device:TPU:1, one launch (start us, length us, event | category | flops | bytes accessed | tf_op | source)
XLA Modules:
  0.0 84.7 jit_solution(983688119329894900)
XLA Ops:
  0.0 0.9 %copy-done = bf16[16,64,128]{2,1,0:T(8,128)(2,1)S(1)} copy-done((bf16[16,64,128]{2,1,0:T(8,128)(2,1)S(1)}, bf16[16,64,128]{2,1,0:T(8,128)(2,1)}, u32[]{:S(2)}) %copy-start) | copy-done | bytes 262168
  1.6 7.6 %all-to-all-start = ((bf16[4,16,8,128]{3,2,1,0:T(8,128)(2,1)}), bf16[4,16,8,128]{3,2,1,0:T(8,128)(2,1)S(1)}, u32[]{:S(2)}, u32[]{:S(2)}) async-start(bf16[4,16,8,128]{3,2,1,0:T(8,128)(2,1)} %broadcast_in_dim.3), calls=%async_computation | async-start | bytes 262144 | tf_op jit(solution)/shard_map/all_to_all | solution.py:144
  9.3 1.6 %copy-done.1 = bf16[16,8,64,64]{3,2,1,0:T(8,128)(2,1)S(1)} copy-done((bf16[16,8,64,64]{3,2,1,0:T(8,128)(2,1)S(1)}, bf16[16,8,64,64]{3,2,1,0:T(8,128)(2,1)}, u32[]{:S(2)}) %copy-start.1) | copy-done | bytes 1048600
  10.9 3.3 %split_tiles.1 = bf16[8,8,64,128]{3,2,1,0:T(8,128)(2,1)} custom-call(bf16[16,8,64,64]{3,2,1,0:T(8,128)(2,1)S(1)} %copy-done.1), custom_call_target="tpu_custom_call" | custom-call | flops 268435456 | bytes 3145728 | tf_op jit(solution)/shard_map/split_tiles/pallas_call | solution.py:158
  14.1 2.5 %all-to-all-done = bf16[4,16,8,128]{3,2,1,0:T(8,128)(2,1)S(1)} async-done(((bf16[4,16,8,128]{3,2,1,0:T(8,128)(2,1)}), bf16[4,16,8,128]{3,2,1,0:T(8,128)(2,1)S(1)}, u32[]{:S(2)}, u32[]{:S(2)}) %all-to-all-start) | async-done | bytes 131104 | tf_op jit(solution)/shard_map/all_to_all | solution.py:144
  16.6 10.0 %all-to-all-start.1 = ((bf16[8,8,64,128]{3,2,1,0:T(8,128)(2,1)}), bf16[8,8,64,128]{3,2,1,0:T(8,128)(2,1)S(1)}, u32[]{:S(2)}, u32[]{:S(2)}) async-start(bf16[8,8,64,128]{3,2,1,0:T(8,128)(2,1)} %split_tiles.1), calls=%async_computation.1 | async-start | bytes 2097152 | tf_op jit(solution)/shard_map/all_to_all | solution.py:167
  26.6 2.3 %collective-permute-start = (bf16[64,8,128]{2,1,0:T(8,128)(2,1)S(1)}, bf16[64,8,128]{2,1,0:T(8,128)(2,1)S(1)}, u32[]{:S(2)}, u32[]{:S(2)}) collective-permute-start(bf16[64,8,128]{2,1,0:T(8,128)(2,1)S(1)} %bitcast.2), channel_id=1, source_target_pairs={{0,16},{16,0},{32,48},{48,32},{64,80},{80,64},{96,112},{112,96},{1... | collective-permute-start | bytes 393224 | tf_op jit(solution)/shard_map/ppermute | solution.py:147
  29.0 3.4 %collective-permute-done = bf16[64,8,128]{2,1,0:T(8,128)(2,1)S(1)} collective-permute-done((bf16[64,8,128]{2,1,0:T(8,128)(2,1)S(1)}, bf16[64,8,128]{2,1,0:T(8,128)(2,1)S(1)}, u32[]{:S(2)}, u32[]{:S(2)}) %collective-permute-start) | collective-permute-done | bytes 131104 | tf_op jit(solution)/shard_map/ppermute | solution.py:147
  32.4 4.7 %collective-permute-start.1 = (bf16[128,8,128]{2,1,0:T(8,128)(2,1)S(1)}, bf16[128,8,128]{2,1,0:T(8,128)(2,1)S(1)}, u32[]{:S(2)}, u32[]{:S(2)}) collective-permute-start(bf16[128,8,128]{2,1,0:T(8,128)(2,1)S(1)} %pad_maximum_fusion.1), channel_id=1, source_target_pairs={{256,0},{384,128},{0,256},{128,384},{257,1},{385,129},{1,257},{129... | collective-permute-start | bytes 786440 | tf_op jit(solution)/shard_map/ppermute | solution.py:152
  37.0 2.8 %collective-permute-start.2 = (bf16[128,8,128]{2,1,0:T(8,128)(2,1)S(1)}, bf16[128,8,128]{2,1,0:T(8,128)(2,1)S(1)}, u32[]{:S(2)}, u32[]{:S(2)}) collective-permute-start(bf16[128,8,128]{2,1,0:T(8,128)(2,1)S(1)} %pad_maximum_fusion.1), channel_id=1, source_target_pairs={{128,0},{256,128},{384,256},{0,384},{129,1},{257,129},{385,257},{1... | collective-permute-start | bytes 786440 | tf_op jit(solution)/shard_map/ppermute | solution.py:152
  39.8 2.5 %collective-permute-start.3 = (bf16[128,8,128]{2,1,0:T(8,128)(2,1)S(1)}, bf16[128,8,128]{2,1,0:T(8,128)(2,1)S(1)}, u32[]{:S(2)}, u32[]{:S(2)}) collective-permute-start(bf16[128,8,128]{2,1,0:T(8,128)(2,1)S(1)} %pad_maximum_fusion.1), channel_id=1, source_target_pairs={{384,0},{0,128},{128,256},{256,384},{385,1},{1,129},{129,257},{257... | collective-permute-start | bytes 786440 | tf_op jit(solution)/shard_map/ppermute | solution.py:152
  42.4 7.2 %collective-permute-start.4 = (bf16[256,8,128]{2,1,0:T(8,128)(2,1)S(1)}, bf16[256,8,128]{2,1,0:T(8,128)(2,1)S(1)}, u32[]{:S(2)}, u32[]{:S(2)}) collective-permute-start(bf16[256,8,128]{2,1,0:T(8,128)(2,1)S(1)} %pad_maximum_fusion.refs_0_), channel_id=1, source_target_pairs={{0,8},{8,0},{1,9},{9,1},{2,10},{10,2},{3,11},{11,3},{4,12},{12,4},... | collective-permute-start | bytes 1572872 | tf_op jit(solution)/shard_map/ppermute | solution.py:156
  49.7 6.0 %collective-permute-start.5 = (bf16[256,8,128]{2,1,0:T(8,128)(2,1)S(1)}, bf16[256,8,128]{2,1,0:T(8,128)(2,1)S(1)}, u32[]{:S(2)}, u32[]{:S(2)}) collective-permute-start(bf16[256,8,128]{2,1,0:T(8,128)(2,1)S(1)} %constant_dynamic-update-slice_fusion.refs_1_), channel_id=1, source_target_pairs={{0,8},{8,0},{1,9},{9,1},{2,10},{10,2},{3,11},{11,3},{4,12},{12,4},... | collective-permute-start | bytes 1572872 | tf_op jit(solution)/shard_map/ppermute | solution.py:156
  56.0 4.0 %find.1.where_ref = s32[16,64]{1,0:T(8,128)S(1)} custom-call(s32[1024]{0:T(1024)S(1)} %fusion.11.table_ref, s32[16]{0:T(128)S(1)} %dynamic_slice.6.row_irrep_ref, s32[16,64]{1,0:T(8,128)S(1)} %copy-done.10), custom_call_target="tpu_custom_call" | custom-call | flops 268435456 | bytes 1048576 | tf_op jit(solution)/shard_map/find/pallas_call | solution.py:177
  60.0 0.8 copy-done.6
  60.7 0.8 copy-done.8
  61.5 1.0 %copy-done.3 = bf16[256,8,128]{2,1,0:T(8,128)(2,1)S(1)} copy-done((bf16[256,8,128]{2,1,0:T(8,128)(2,1)S(1)}, bf16[256,8,128]{2,1,0:T(8,128)(2,1)}, u32[]{:S(2)}) %copy-start.3) | copy-done | bytes 524312
  62.6 1.0 %copy-done.5 = bf16[256,8,128]{2,1,0:T(8,128)(2,1)S(1)} copy-done((bf16[256,8,128]{2,1,0:T(8,128)(2,1)S(1)}, bf16[256,8,128]{2,1,0:T(8,128)(2,1)}, u32[]{:S(2)}) %copy-start.5) | copy-done | bytes 524312
  63.6 1.0 %copy-done.7 = bf16[256,8,128]{2,1,0:T(8,128)(2,1)S(1)} copy-done((bf16[256,8,128]{2,1,0:T(8,128)(2,1)S(1)}, bf16[256,8,128]{2,1,0:T(8,128)(2,1)}, u32[]{:S(2)}) %copy-start.7) | copy-done | bytes 524312
  64.7 1.0 %copy-done.9 = bf16[256,8,128]{2,1,0:T(8,128)(2,1)S(1)} copy-done((bf16[256,8,128]{2,1,0:T(8,128)(2,1)S(1)}, bf16[256,8,128]{2,1,0:T(8,128)(2,1)}, u32[]{:S(2)}) %copy-start.9) | copy-done | bytes 524312
  65.7 2.0 %pick.1.picked_ref = bf16[8,512,256]{2,1,0:T(8,128)(2,1)S(1)} custom-call(s32[16,64]{1,0:T(8,128)S(1)} %find.1.where_ref, bf16[256,8,128]{2,1,0:T(8,128)(2,1)S(1)} %copy-done.3, bf16[256,8,128]{2,1,0:T(8,128)(2,1)S(1)} %copy-done.5, bf16[256,8,128]{2,1,0:T(8,128)(2,1)S(1)} %copy-done.7, bf16[256,8,128]{2,1,0:T(8,128)(2,1)S(1)} %copy-done.9), custom_call_target="tpu_custom_call" | custom-call | flops 268435456 | bytes 6291456 | tf_op jit(solution)/shard_map/pick/pallas_call | solution.py:187
  67.7 0.8 contract.1
  68.5 15.4 %all_to_all.15.parts_ref = s16[8,9,16,128]{3,2,1,0:T(8,128)(2,1)S(1)} all-to-all(s16[8,9,16,128]{3,2,1,0:T(8,128)(2,1)S(1)} %contract.1), channel_id=1, replica_groups={{4,5,6,7,0,1,2,3},{12,13,14,15,8,9,10,11},{20,21,22,23,16,17,18,19},{28..., dimensions={0} | all-to-all | bytes 589824 | tf_op jit(solution)/shard_map/all_to_all | solution.py:211
  83.9 0.8 add_up.1
  (32 shorter events, 1.0 us)
Async XLA Ops:
  0.0 1.0 %copy-start = (bf16[16,64,128]{2,1,0:T(8,128)(2,1)S(1)}, bf16[16,64,128]{2,1,0:T(8,128)(2,1)}, u32[]{:S(2)}) copy-start(bf16[16,64,128]{2,1,0:T(8,128)(2,1)} %param.5) | copy-start | bytes 786436
  1.6 15.0 %all-to-all-start = ((bf16[4,16,8,128]{3,2,1,0:T(8,128)(2,1)}), bf16[4,16,8,128]{3,2,1,0:T(8,128)(2,1)S(1)}, u32[]{:S(2)}, u32[]{:S(2)}) async-start(bf16[4,16,8,128]{3,2,1,0:T(8,128)(2,1)} %broadcast_in_dim.3), calls=%async_computation | async-start | bytes 262144 | tf_op jit(solution)/shard_map/all_to_all | solution.py:144
  9.3 1.6 %copy-start.1 = (bf16[16,8,64,64]{3,2,1,0:T(8,128)(2,1)S(1)}, bf16[16,8,64,64]{3,2,1,0:T(8,128)(2,1)}, u32[]{:S(2)}) copy-start(bf16[16,8,64,64]{3,2,1,0:T(8,128)(2,1)} %tiles_ref.1) | copy-start | bytes 3145732
  14.1 41.7 %copy-start.11 = (s32[1024]{0:T(1024)S(1)}, s32[1024]{0:T(1024)}, u32[]{:S(2)}) copy-start(s32[1024]{0:T(1024)} %param.9) | copy-start | bytes 12292
  14.1 41.8 %copy-start.12 = (s32[1024]{0:T(1024)S(1)}, s32[1024]{0:T(1024)}, u32[]{:S(2)}) copy-start(s32[1024]{0:T(1024)} %param.6) | copy-start | bytes 12292
  14.1 41.8 %copy-start.10 = (s32[16,64]{1,0:T(8,128)S(1)}, s32[16,64]{1,0:T(8,128)}, u32[]{:S(2)}) copy-start(s32[16,64]{1,0:T(8,128)} %cols_ref.1) | copy-start | bytes 12292
  16.6 51.1 %all-to-all-start.1 = ((bf16[8,8,64,128]{3,2,1,0:T(8,128)(2,1)}), bf16[8,8,64,128]{3,2,1,0:T(8,128)(2,1)S(1)}, u32[]{:S(2)}, u32[]{:S(2)}) async-start(bf16[8,8,64,128]{3,2,1,0:T(8,128)(2,1)} %split_tiles.1), calls=%async_computation.1 | async-start | bytes 2097152 | tf_op jit(solution)/shard_map/all_to_all | solution.py:167
  26.6 5.7 %collective-permute-start = (bf16[64,8,128]{2,1,0:T(8,128)(2,1)S(1)}, bf16[64,8,128]{2,1,0:T(8,128)(2,1)S(1)}, u32[]{:S(2)}, u32[]{:S(2)}) collective-permute-start(bf16[64,8,128]{2,1,0:T(8,128)(2,1)S(1)} %bitcast.2), channel_id=1, source_target_pairs={{0,16},{16,0},{32,48},{48,32},{64,80},{80,64},{96,112},{112,96},{1... | collective-permute-start | bytes 393224 | tf_op jit(solution)/shard_map/ppermute | solution.py:147
  32.4 10.0 %collective-permute-start.1 = (bf16[128,8,128]{2,1,0:T(8,128)(2,1)S(1)}, bf16[128,8,128]{2,1,0:T(8,128)(2,1)S(1)}, u32[]{:S(2)}, u32[]{:S(2)}) collective-permute-start(bf16[128,8,128]{2,1,0:T(8,128)(2,1)S(1)} %pad_maximum_fusion.1), channel_id=1, source_target_pairs={{256,0},{384,128},{0,256},{128,384},{257,1},{385,129},{1,257},{129... | collective-permute-start | bytes 786440 | tf_op jit(solution)/shard_map/ppermute | solution.py:152
  37.0 12.6 %collective-permute-start.2 = (bf16[128,8,128]{2,1,0:T(8,128)(2,1)S(1)}, bf16[128,8,128]{2,1,0:T(8,128)(2,1)S(1)}, u32[]{:S(2)}, u32[]{:S(2)}) collective-permute-start(bf16[128,8,128]{2,1,0:T(8,128)(2,1)S(1)} %pad_maximum_fusion.1), channel_id=1, source_target_pairs={{128,0},{256,128},{384,256},{0,384},{129,1},{257,129},{385,257},{1... | collective-permute-start | bytes 786440 | tf_op jit(solution)/shard_map/ppermute | solution.py:152
  39.8 9.9 %collective-permute-start.3 = (bf16[128,8,128]{2,1,0:T(8,128)(2,1)S(1)}, bf16[128,8,128]{2,1,0:T(8,128)(2,1)S(1)}, u32[]{:S(2)}, u32[]{:S(2)}) collective-permute-start(bf16[128,8,128]{2,1,0:T(8,128)(2,1)S(1)} %pad_maximum_fusion.1), channel_id=1, source_target_pairs={{384,0},{0,128},{128,256},{256,384},{385,1},{1,129},{129,257},{257... | collective-permute-start | bytes 786440 | tf_op jit(solution)/shard_map/ppermute | solution.py:152
  42.4 17.5 %copy-start.2 = (bf16[256,8,128]{2,1,0:T(8,128)(2,1)}, bf16[256,8,128]{2,1,0:T(8,128)(2,1)S(1)}, u32[]{:S(2)}) copy-start(bf16[256,8,128]{2,1,0:T(8,128)(2,1)S(1)} %pad_maximum_fusion.refs_0_) | copy-start | bytes 1572868
  42.4 17.5 %collective-permute-start.4 = (bf16[256,8,128]{2,1,0:T(8,128)(2,1)S(1)}, bf16[256,8,128]{2,1,0:T(8,128)(2,1)S(1)}, u32[]{:S(2)}, u32[]{:S(2)}) collective-permute-start(bf16[256,8,128]{2,1,0:T(8,128)(2,1)S(1)} %pad_maximum_fusion.refs_0_), channel_id=1, source_target_pairs={{0,8},{8,0},{1,9},{9,1},{2,10},{10,2},{3,11},{11,3},{4,12},{12,4},... | collective-permute-start | bytes 1572872 | tf_op jit(solution)/shard_map/ppermute | solution.py:156
  49.7 10.2 %copy-start.4 = (bf16[256,8,128]{2,1,0:T(8,128)(2,1)}, bf16[256,8,128]{2,1,0:T(8,128)(2,1)S(1)}, u32[]{:S(2)}) copy-start(bf16[256,8,128]{2,1,0:T(8,128)(2,1)S(1)} %constant_dynamic-update-slice_fusion.refs_1_) | copy-start | bytes 1572868
  49.7 11.0 %collective-permute-start.5 = (bf16[256,8,128]{2,1,0:T(8,128)(2,1)S(1)}, bf16[256,8,128]{2,1,0:T(8,128)(2,1)S(1)}, u32[]{:S(2)}, u32[]{:S(2)}) collective-permute-start(bf16[256,8,128]{2,1,0:T(8,128)(2,1)S(1)} %constant_dynamic-update-slice_fusion.refs_1_), channel_id=1, source_target_pairs={{0,8},{8,0},{1,9},{9,1},{2,10},{10,2},{3,11},{11,3},{4,12},{12,4},... | collective-permute-start | bytes 1572872 | tf_op jit(solution)/shard_map/ppermute | solution.py:156
  60.0 0.8 copy-start.6
  60.7 0.8 copy-start.8
  61.5 1.0 %copy-start.3 = (bf16[256,8,128]{2,1,0:T(8,128)(2,1)S(1)}, bf16[256,8,128]{2,1,0:T(8,128)(2,1)}, u32[]{:S(2)}) copy-start(bf16[256,8,128]{2,1,0:T(8,128)(2,1)} %copy-done.2) | copy-start | bytes 1572868
  62.6 1.0 %copy-start.5 = (bf16[256,8,128]{2,1,0:T(8,128)(2,1)S(1)}, bf16[256,8,128]{2,1,0:T(8,128)(2,1)}, u32[]{:S(2)}) copy-start(bf16[256,8,128]{2,1,0:T(8,128)(2,1)} %copy-done.4) | copy-start | bytes 1572868
  63.6 1.0 %copy-start.7 = (bf16[256,8,128]{2,1,0:T(8,128)(2,1)S(1)}, bf16[256,8,128]{2,1,0:T(8,128)(2,1)}, u32[]{:S(2)}) copy-start(bf16[256,8,128]{2,1,0:T(8,128)(2,1)} %copy-done.6) | copy-start | bytes 1572868
  64.7 1.0 %copy-start.9 = (bf16[256,8,128]{2,1,0:T(8,128)(2,1)S(1)}, bf16[256,8,128]{2,1,0:T(8,128)(2,1)}, u32[]{:S(2)}) copy-start(bf16[256,8,128]{2,1,0:T(8,128)(2,1)} %copy-done.8) | copy-start | bytes 1572868

commit v9 on v8

--- a/solution.py
+++ b/solution.py
@@ -15,7 +15,7 @@
 SUB = TILE // NZ
 PER_Z = 8
 OCC = 128
-TILES_ORDER = [0, 1, 2, 3, 4, 5, 6, 7]
+TILES_ORDER = [7, 1, 2, 3, 4, 5, 6, 0]
 SUMS_ORDER = [4, 5, 6, 7, 0, 1, 2, 3]
 STEPS = 32000.0
 SMALLEST = 2.0**-100
@@ -164,7 +164,9 @@
         cost_estimate=cost(3),
         name="split_tiles",
     )(integrals)
-    tiles = lax.all_to_all(split, "z", 0, 0, tiled=False)
+    tiles = lax.all_to_all(
+        split, "z", 0, 0, axis_index_groups=[TILES_ORDER], tiled=False
+    )
 
     holder = block_slot // ROWS
     holder_x, holder_y = holder // (NY * NC), (holder // NC) % NY

time: 85.5 us -> 86 us (level)
  starting transfers between devices: 43.2 us -> 45.1 us
  blocking collectives: 15.4 us -> 13.8 us
    all_to_all x1, starting transfers between devices: 10 us -> 12.3 us  [local(): lax.all_to_all(split, 'z', 0, 0, axis_index_groups=[TILES_ORDER], tiled=F...]
    all_to_all x1, blocking collectives: 15.4 us -> 13.8 us  [local(): lax.all_to_all(sums, 'z', 0, 0, axis_index_groups=[SUMS_ORDER], tiled=False)]
where the time goes in v9:
time: 86 us; the launch traced here: 85.3 us
  starting transfers between devices  45.1 us (52%)
  blocking collectives  13.8 us (16%)
  Pallas kernels  10.8 us (13%)
  local copies, waits for them, and re-layouts  9.12 us (11%)
  waiting for transfers between devices  6.17 us (7%)
    all_to_all x1, blocking collectives, local(): lax.all_to_all(sums, 'z', 0, 0, axis_index_groups=[SUMS_ORDER], tiled=False)  13.8 us
    ppermute x2, starting transfers between devices, local(): others.append(lax.ppermute(owns[-1], 'core', [(0, 1), (1, 0)]))  13 us
    all_to_all x1, starting transfers between devices, local(): lax.all_to_all(split, 'z', 0, 0, axis_index_groups=[TILES_ORDER], tiled=F...  12.3 us
    ppermute x3, starting transfers between devices, local(): pieces.append(lax.ppermute(along_y, 'x', shift))  9.93 us
    unnamed x27, local copies, waits for them, and re-layouts  8.32 us
    all_to_all x1, starting transfers between devices, local(): lax.all_to_all(to_y, 'y', 0, 0, axis_index_groups=[[0, 2, 4, 6], [1, 3, 5...  7.63 us
    pallas_call x1, Pallas kernels, local(): pl.pallas_call(find, out_shape=jax.ShapeDtypeStruct((ROWS, NZ * PER_Z), j...  3.97 us
    ppermute x1, waiting for transfers between devices, local(): near = lax.ppermute(same, 'y', [(i, i ^ 1) for i in range(NY)])  3.69 us
  transfers between devices with their start and end apart: 8, of which 2 were waited for; matrix products, arithmetic and copies ran while one was open for 0% of the time, Pallas kernels for 11%

profile of v9, /device:TPU:1, one launch (start us, length us, event | category | flops | bytes accessed | tf_op | source)
XLA Modules:
  0.0 85.3 jit_solution(6637327465878740802)
XLA Ops:
  0.0 0.9 %copy-done = bf16[16,64,128]{2,1,0:T(8,128)(2,1)S(1)} copy-done((bf16[16,64,128]{2,1,0:T(8,128)(2,1)S(1)}, bf16[16,64,128]{2,1,0:T(8,128)(2,1)}, u32[]{:S(2)}) %copy-start) | copy-done | bytes 262168
  1.6 7.6 %all-to-all-start = ((bf16[4,16,8,128]{3,2,1,0:T(8,128)(2,1)}), bf16[4,16,8,128]{3,2,1,0:T(8,128)(2,1)S(1)}, u32[]{:S(2)}, u32[]{:S(2)}) async-start(bf16[4,16,8,128]{3,2,1,0:T(8,128)(2,1)} %broadcast_in_dim.3), calls=%async_computation | async-start | bytes 262144 | tf_op jit(solution)/shard_map/all_to_all | solution.py:144
  9.3 1.6 %copy-done.1 = bf16[16,8,64,64]{3,2,1,0:T(8,128)(2,1)S(1)} copy-done((bf16[16,8,64,64]{3,2,1,0:T(8,128)(2,1)S(1)}, bf16[16,8,64,64]{3,2,1,0:T(8,128)(2,1)}, u32[]{:S(2)}) %copy-start.1) | copy-done | bytes 1048600
  10.9 3.3 %split_tiles.1 = bf16[8,8,64,128]{3,2,1,0:T(8,128)(2,1)} custom-call(bf16[16,8,64,64]{3,2,1,0:T(8,128)(2,1)S(1)} %copy-done.1), custom_call_target="tpu_custom_call" | custom-call | flops 268435456 | bytes 3145728 | tf_op jit(solution)/shard_map/split_tiles/pallas_call | solution.py:158
  14.1 2.5 %all-to-all-done = bf16[4,16,8,128]{3,2,1,0:T(8,128)(2,1)S(1)} async-done(((bf16[4,16,8,128]{3,2,1,0:T(8,128)(2,1)}), bf16[4,16,8,128]{3,2,1,0:T(8,128)(2,1)S(1)}, u32[]{:S(2)}, u32[]{:S(2)}) %all-to-all-start) | async-done | bytes 131104 | tf_op jit(solution)/shard_map/all_to_all | solution.py:144
  16.6 12.3 %all-to-all-start.1 = ((bf16[8,8,64,128]{3,2,1,0:T(8,128)(2,1)}), bf16[8,8,64,128]{3,2,1,0:T(8,128)(2,1)S(1)}, u32[]{:S(2)}, u32[]{:S(2)}) async-start(bf16[8,8,64,128]{3,2,1,0:T(8,128)(2,1)} %split_tiles.1), calls=%async_computation.1 | async-start | bytes 2097152 | tf_op jit(solution)/shard_map/all_to_all | solution.py:167
  28.9 2.3 %collective-permute-start = (bf16[64,8,128]{2,1,0:T(8,128)(2,1)S(1)}, bf16[64,8,128]{2,1,0:T(8,128)(2,1)S(1)}, u32[]{:S(2)}, u32[]{:S(2)}) collective-permute-start(bf16[64,8,128]{2,1,0:T(8,128)(2,1)S(1)} %bitcast.2), channel_id=1, source_target_pairs={{0,16},{16,0},{32,48},{48,32},{64,80},{80,64},{96,112},{112,96},{1... | collective-permute-start | bytes 393224 | tf_op jit(solution)/shard_map/ppermute | solution.py:147
  31.2 3.7 %collective-permute-done = bf16[64,8,128]{2,1,0:T(8,128)(2,1)S(1)} collective-permute-done((bf16[64,8,128]{2,1,0:T(8,128)(2,1)S(1)}, bf16[64,8,128]{2,1,0:T(8,128)(2,1)S(1)}, u32[]{:S(2)}, u32[]{:S(2)}) %collective-permute-start) | collective-permute-done | bytes 131104 | tf_op jit(solution)/shard_map/ppermute | solution.py:147
  34.9 4.7 %collective-permute-start.1 = (bf16[128,8,128]{2,1,0:T(8,128)(2,1)S(1)}, bf16[128,8,128]{2,1,0:T(8,128)(2,1)S(1)}, u32[]{:S(2)}, u32[]{:S(2)}) collective-permute-start(bf16[128,8,128]{2,1,0:T(8,128)(2,1)S(1)} %pad_maximum_fusion.1), channel_id=1, source_target_pairs={{256,0},{384,128},{0,256},{128,384},{257,1},{385,129},{1,257},{129... | collective-permute-start | bytes 786440 | tf_op jit(solution)/shard_map/ppermute | solution.py:152
  39.6 2.8 %collective-permute-start.2 = (bf16[128,8,128]{2,1,0:T(8,128)(2,1)S(1)}, bf16[128,8,128]{2,1,0:T(8,128)(2,1)S(1)}, u32[]{:S(2)}, u32[]{:S(2)}) collective-permute-start(bf16[128,8,128]{2,1,0:T(8,128)(2,1)S(1)} %pad_maximum_fusion.1), channel_id=1, source_target_pairs={{128,0},{256,128},{384,256},{0,384},{129,1},{257,129},{385,257},{1... | collective-permute-start | bytes 786440 | tf_op jit(solution)/shard_map/ppermute | solution.py:152
  42.3 2.5 %collective-permute-start.3 = (bf16[128,8,128]{2,1,0:T(8,128)(2,1)S(1)}, bf16[128,8,128]{2,1,0:T(8,128)(2,1)S(1)}, u32[]{:S(2)}, u32[]{:S(2)}) collective-permute-start(bf16[128,8,128]{2,1,0:T(8,128)(2,1)S(1)} %pad_maximum_fusion.1), channel_id=1, source_target_pairs={{384,0},{0,128},{128,256},{256,384},{385,1},{1,129},{129,257},{257... | collective-permute-start | bytes 786440 | tf_op jit(solution)/shard_map/ppermute | solution.py:152
  44.9 6.6 %collective-permute-start.4 = (bf16[256,8,128]{2,1,0:T(8,128)(2,1)S(1)}, bf16[256,8,128]{2,1,0:T(8,128)(2,1)S(1)}, u32[]{:S(2)}, u32[]{:S(2)}) collective-permute-start(bf16[256,8,128]{2,1,0:T(8,128)(2,1)S(1)} %pad_maximum_fusion.refs_0_), channel_id=1, source_target_pairs={{0,8},{8,0},{1,9},{9,1},{2,10},{10,2},{3,11},{11,3},{4,12},{12,4},... | collective-permute-start | bytes 1572872 | tf_op jit(solution)/shard_map/ppermute | solution.py:156
  51.7 6.3 %collective-permute-start.5 = (bf16[256,8,128]{2,1,0:T(8,128)(2,1)S(1)}, bf16[256,8,128]{2,1,0:T(8,128)(2,1)S(1)}, u32[]{:S(2)}, u32[]{:S(2)}) collective-permute-start(bf16[256,8,128]{2,1,0:T(8,128)(2,1)S(1)} %constant_dynamic-update-slice_fusion.refs_1_), channel_id=1, source_target_pairs={{0,8},{8,0},{1,9},{9,1},{2,10},{10,2},{3,11},{11,3},{4,12},{12,4},... | collective-permute-start | bytes 1572872 | tf_op jit(solution)/shard_map/ppermute | solution.py:156
  58.2 4.0 %find.1.where_ref = s32[16,64]{1,0:T(8,128)S(1)} custom-call(s32[1024]{0:T(1024)S(1)} %fusion.11.table_ref, s32[16]{0:T(128)S(1)} %dynamic_slice.6.row_irrep_ref, s32[16,64]{1,0:T(8,128)S(1)} %copy-done.10), custom_call_target="tpu_custom_call" | custom-call | flops 268435456 | bytes 1048576 | tf_op jit(solution)/shard_map/find/pallas_call | solution.py:179
  62.2 0.8 copy-done.6
  63.0 0.8 copy-done.8
  63.8 1.0 %copy-done.3 = bf16[256,8,128]{2,1,0:T(8,128)(2,1)S(1)} copy-done((bf16[256,8,128]{2,1,0:T(8,128)(2,1)S(1)}, bf16[256,8,128]{2,1,0:T(8,128)(2,1)}, u32[]{:S(2)}) %copy-start.3) | copy-done | bytes 524312
  64.8 1.0 %copy-done.5 = bf16[256,8,128]{2,1,0:T(8,128)(2,1)S(1)} copy-done((bf16[256,8,128]{2,1,0:T(8,128)(2,1)S(1)}, bf16[256,8,128]{2,1,0:T(8,128)(2,1)}, u32[]{:S(2)}) %copy-start.5) | copy-done | bytes 524312
  65.9 1.0 %copy-done.7 = bf16[256,8,128]{2,1,0:T(8,128)(2,1)S(1)} copy-done((bf16[256,8,128]{2,1,0:T(8,128)(2,1)S(1)}, bf16[256,8,128]{2,1,0:T(8,128)(2,1)}, u32[]{:S(2)}) %copy-start.7) | copy-done | bytes 524312
  66.9 1.0 %copy-done.9 = bf16[256,8,128]{2,1,0:T(8,128)(2,1)S(1)} copy-done((bf16[256,8,128]{2,1,0:T(8,128)(2,1)S(1)}, bf16[256,8,128]{2,1,0:T(8,128)(2,1)}, u32[]{:S(2)}) %copy-start.9) | copy-done | bytes 524312
  67.9 2.0 %pick.1.picked_ref = bf16[8,512,256]{2,1,0:T(8,128)(2,1)S(1)} custom-call(s32[16,64]{1,0:T(8,128)S(1)} %find.1.where_ref, bf16[256,8,128]{2,1,0:T(8,128)(2,1)S(1)} %copy-done.3, bf16[256,8,128]{2,1,0:T(8,128)(2,1)S(1)} %copy-done.5, bf16[256,8,128]{2,1,0:T(8,128)(2,1)S(1)} %copy-done.7, bf16[256,8,128]{2,1,0:T(8,128)(2,1)S(1)} %copy-done.9), custom_call_target="tpu_custom_call" | custom-call | flops 268435456 | bytes 6291456 | tf_op jit(solution)/shard_map/pick/pallas_call | solution.py:189
  69.9 0.8 contract.1
  70.7 13.8 %all_to_all.15.parts_ref = s16[8,9,16,128]{3,2,1,0:T(8,128)(2,1)S(1)} all-to-all(s16[8,9,16,128]{3,2,1,0:T(8,128)(2,1)S(1)} %contract.1), channel_id=1, replica_groups={{4,5,6,7,0,1,2,3},{12,13,14,15,8,9,10,11},{20,21,22,23,16,17,18,19},{28..., dimensions={0} | all-to-all | bytes 589824 | tf_op jit(solution)/shard_map/all_to_all | solution.py:213
  84.5 0.8 add_up.1
  (32 shorter events, 1.0 us)
Async XLA Ops:
  0.0 1.0 %copy-start = (bf16[16,64,128]{2,1,0:T(8,128)(2,1)S(1)}, bf16[16,64,128]{2,1,0:T(8,128)(2,1)}, u32[]{:S(2)}) copy-start(bf16[16,64,128]{2,1,0:T(8,128)(2,1)} %param.5) | copy-start | bytes 786436
  1.6 15.0 %all-to-all-start = ((bf16[4,16,8,128]{3,2,1,0:T(8,128)(2,1)}), bf16[4,16,8,128]{3,2,1,0:T(8,128)(2,1)S(1)}, u32[]{:S(2)}, u32[]{:S(2)}) async-start(bf16[4,16,8,128]{3,2,1,0:T(8,128)(2,1)} %broadcast_in_dim.3), calls=%async_computation | async-start | bytes 262144 | tf_op jit(solution)/shard_map/all_to_all | solution.py:144
  9.3 1.6 %copy-start.1 = (bf16[16,8,64,64]{3,2,1,0:T(8,128)(2,1)S(1)}, bf16[16,8,64,64]{3,2,1,0:T(8,128)(2,1)}, u32[]{:S(2)}) copy-start(bf16[16,8,64,64]{3,2,1,0:T(8,128)(2,1)} %tiles_ref.1) | copy-start | bytes 3145732
  14.1 43.9 %copy-start.11 = (s32[1024]{0:T(1024)S(1)}, s32[1024]{0:T(1024)}, u32[]{:S(2)}) copy-start(s32[1024]{0:T(1024)} %param.9) | copy-start | bytes 12292
  14.1 44.0 %copy-start.12 = (s32[1024]{0:T(1024)S(1)}, s32[1024]{0:T(1024)}, u32[]{:S(2)}) copy-start(s32[1024]{0:T(1024)} %param.6) | copy-start | bytes 12292
  14.1 44.0 %copy-start.10 = (s32[16,64]{1,0:T(8,128)S(1)}, s32[16,64]{1,0:T(8,128)}, u32[]{:S(2)}) copy-start(s32[16,64]{1,0:T(8,128)} %cols_ref.1) | copy-start | bytes 12292
  16.6 53.3 %all-to-all-start.1 = ((bf16[8,8,64,128]{3,2,1,0:T(8,128)(2,1)}), bf16[8,8,64,128]{3,2,1,0:T(8,128)(2,1)S(1)}, u32[]{:S(2)}, u32[]{:S(2)}) async-start(bf16[8,8,64,128]{3,2,1,0:T(8,128)(2,1)} %split_tiles.1), calls=%async_computation.1 | async-start | bytes 2097152 | tf_op jit(solution)/shard_map/all_to_all | solution.py:167
  28.9 6.0 %collective-permute-start = (bf16[64,8,128]{2,1,0:T(8,128)(2,1)S(1)}, bf16[64,8,128]{2,1,0:T(8,128)(2,1)S(1)}, u32[]{:S(2)}, u32[]{:S(2)}) collective-permute-start(bf16[64,8,128]{2,1,0:T(8,128)(2,1)S(1)} %bitcast.2), channel_id=1, source_target_pairs={{0,16},{16,0},{32,48},{48,32},{64,80},{80,64},{96,112},{112,96},{1... | collective-permute-start | bytes 393224 | tf_op jit(solution)/shard_map/ppermute | solution.py:147
  34.9 10.0 %collective-permute-start.1 = (bf16[128,8,128]{2,1,0:T(8,128)(2,1)S(1)}, bf16[128,8,128]{2,1,0:T(8,128)(2,1)S(1)}, u32[]{:S(2)}, u32[]{:S(2)}) collective-permute-start(bf16[128,8,128]{2,1,0:T(8,128)(2,1)S(1)} %pad_maximum_fusion.1), channel_id=1, source_target_pairs={{256,0},{384,128},{0,256},{128,384},{257,1},{385,129},{1,257},{129... | collective-permute-start | bytes 786440 | tf_op jit(solution)/shard_map/ppermute | solution.py:152
  39.6 12.0 %collective-permute-start.2 = (bf16[128,8,128]{2,1,0:T(8,128)(2,1)S(1)}, bf16[128,8,128]{2,1,0:T(8,128)(2,1)S(1)}, u32[]{:S(2)}, u32[]{:S(2)}) collective-permute-start(bf16[128,8,128]{2,1,0:T(8,128)(2,1)S(1)} %pad_maximum_fusion.1), channel_id=1, source_target_pairs={{128,0},{256,128},{384,256},{0,384},{129,1},{257,129},{385,257},{1... | collective-permute-start | bytes 786440 | tf_op jit(solution)/shard_map/ppermute | solution.py:152
  42.3 9.3 %collective-permute-start.3 = (bf16[128,8,128]{2,1,0:T(8,128)(2,1)S(1)}, bf16[128,8,128]{2,1,0:T(8,128)(2,1)S(1)}, u32[]{:S(2)}, u32[]{:S(2)}) collective-permute-start(bf16[128,8,128]{2,1,0:T(8,128)(2,1)S(1)} %pad_maximum_fusion.1), channel_id=1, source_target_pairs={{384,0},{0,128},{128,256},{256,384},{385,1},{1,129},{129,257},{257... | collective-permute-start | bytes 786440 | tf_op jit(solution)/shard_map/ppermute | solution.py:152
  44.9 17.2 %copy-start.2 = (bf16[256,8,128]{2,1,0:T(8,128)(2,1)}, bf16[256,8,128]{2,1,0:T(8,128)(2,1)S(1)}, u32[]{:S(2)}) copy-start(bf16[256,8,128]{2,1,0:T(8,128)(2,1)S(1)} %pad_maximum_fusion.refs_0_) | copy-start | bytes 1572868
  44.9 17.2 %collective-permute-start.4 = (bf16[256,8,128]{2,1,0:T(8,128)(2,1)S(1)}, bf16[256,8,128]{2,1,0:T(8,128)(2,1)S(1)}, u32[]{:S(2)}, u32[]{:S(2)}) collective-permute-start(bf16[256,8,128]{2,1,0:T(8,128)(2,1)S(1)} %pad_maximum_fusion.refs_0_), channel_id=1, source_target_pairs={{0,8},{8,0},{1,9},{9,1},{2,10},{10,2},{3,11},{11,3},{4,12},{12,4},... | collective-permute-start | bytes 1572872 | tf_op jit(solution)/shard_map/ppermute | solution.py:156
  51.7 10.5 %copy-start.4 = (bf16[256,8,128]{2,1,0:T(8,128)(2,1)}, bf16[256,8,128]{2,1,0:T(8,128)(2,1)S(1)}, u32[]{:S(2)}) copy-start(bf16[256,8,128]{2,1,0:T(8,128)(2,1)S(1)} %constant_dynamic-update-slice_fusion.refs_1_) | copy-start | bytes 1572868
  51.7 11.3 %collective-permute-start.5 = (bf16[256,8,128]{2,1,0:T(8,128)(2,1)S(1)}, bf16[256,8,128]{2,1,0:T(8,128)(2,1)S(1)}, u32[]{:S(2)}, u32[]{:S(2)}) collective-permute-start(bf16[256,8,128]{2,1,0:T(8,128)(2,1)S(1)} %constant_dynamic-update-slice_fusion.refs_1_), channel_id=1, source_target_pairs={{0,8},{8,0},{1,9},{9,1},{2,10},{10,2},{3,11},{11,3},{4,12},{12,4},... | collective-permute-start | bytes 1572872 | tf_op jit(solution)/shard_map/ppermute | solution.py:156
  62.2 0.8 copy-start.6
  63.0 0.8 copy-start.8
  63.8 1.0 %copy-start.3 = (bf16[256,8,128]{2,1,0:T(8,128)(2,1)S(1)}, bf16[256,8,128]{2,1,0:T(8,128)(2,1)}, u32[]{:S(2)}) copy-start(bf16[256,8,128]{2,1,0:T(8,128)(2,1)} %copy-done.2) | copy-start | bytes 1572868
  64.8 1.0 %copy-start.5 = (bf16[256,8,128]{2,1,0:T(8,128)(2,1)S(1)}, bf16[256,8,128]{2,1,0:T(8,128)(2,1)}, u32[]{:S(2)}) copy-start(bf16[256,8,128]{2,1,0:T(8,128)(2,1)} %copy-done.4) | copy-start | bytes 1572868
  65.9 1.0 %copy-start.7 = (bf16[256,8,128]{2,1,0:T(8,128)(2,1)S(1)}, bf16[256,8,128]{2,1,0:T(8,128)(2,1)}, u32[]{:S(2)}) copy-start(bf16[256,8,128]{2,1,0:T(8,128)(2,1)} %copy-done.6) | copy-start | bytes 1572868
  66.9 1.0 %copy-start.9 = (bf16[256,8,128]{2,1,0:T(8,128)(2,1)S(1)}, bf16[256,8,128]{2,1,0:T(8,128)(2,1)}, u32[]{:S(2)}) copy-start(bf16[256,8,128]{2,1,0:T(8,128)(2,1)} %copy-done.8) | copy-start | bytes 1572868

commit v10 on v7

--- a/solution.py
+++ b/solution.py
@@ -49,7 +49,7 @@
     lax.fori_loop(0, PAIRS, step, 0)
 
 
-def find(table_ref, row_irrep_ref, cols_ref, out_ref):
+def find(table_ref, row_irrep_ref, cols_ref, raw_ref, out_ref):
     def step(row, carry):
         irrep = row_irrep_ref[row]
         for n in range(NZ * PER_Z):
@@ -176,12 +176,13 @@
     where = pl.pallas_call(
         find,
         out_shape=jax.ShapeDtypeStruct((ROWS, NZ * PER_Z), jnp.int32),
-        in_specs=[pl.BlockSpec(memory_space=pltpu.SMEM)] * 3,
+        in_specs=[pl.BlockSpec(memory_space=pltpu.SMEM)] * 3
+        + [pl.BlockSpec(memory_space=pl.ANY)],
         out_specs=pl.BlockSpec(memory_space=pltpu.SMEM),
         compiler_params=pltpu.CompilerParams(vmem_limit_bytes=VMEM),
         cost_estimate=cost(1),
         name="find",
-    )(table, row_irrep, tile_cols)
+    )(table, row_irrep, tile_cols, amplitudes)
 
     picked = pl.pallas_call(
         pick,

time: 86.1 us -> 86 us (level)
    unnamed x27, local copies, waits for them, and re-layouts: 8.32 us -> 7.38 us
where the time goes in v10:
time: 86 us; the launch traced here: 85.2 us
  starting transfers between devices  43.8 us (51%)
  blocking collectives  15.4 us (18%)
  Pallas kernels  10.8 us (13%)
  local copies, waits for them, and re-layouts  8.92 us (10%)
  waiting for transfers between devices  5.87 us (7%)
    all_to_all x1, blocking collectives, local(): lax.all_to_all(sums, 'z', 0, 0, axis_index_groups=[SUMS_ORDER], tiled=False)  15.4 us
    ppermute x2, starting transfers between devices, local(): others.append(lax.ppermute(owns[-1], 'core', [(0, 1), (1, 0)]))  14.5 us
    all_to_all x1, starting transfers between devices, local(): tiles = lax.all_to_all(split, 'z', 0, 0, tiled=False)  10 us
    ppermute x3, starting transfers between devices, local(): pieces.append(lax.ppermute(along_y, 'x', shift))  9.33 us
    all_to_all x1, starting transfers between devices, local(): lax.all_to_all(to_y, 'y', 0, 0, axis_index_groups=[[0, 2, 4, 6], [1, 3, 5...  7.63 us
    unnamed x27, local copies, waits for them, and re-layouts  7.38 us
    pallas_call x1, Pallas kernels, local(): pl.pallas_call(find, out_shape=jax.ShapeDtypeStruct((ROWS, NZ * PER_Z), j...  3.97 us
    ppermute x1, waiting for transfers between devices, local(): near = lax.ppermute(same, 'y', [(i, i ^ 1) for i in range(NY)])  3.39 us
  transfers between devices with their start and end apart: 8, of which 2 were waited for; matrix products, arithmetic and copies ran while one was open for 0% of the time, Pallas kernels for 11%

profile of v10, /device:TPU:1, one launch (start us, length us, event | category | flops | bytes accessed | tf_op | source)
XLA Modules:
  0.0 85.2 jit_solution(4170632226278398692)
XLA Ops:
  0.0 0.8 constant_dynamic-slice_fusion
  1.4 7.6 %all-to-all-start = ((bf16[4,16,8,128]{3,2,1,0:T(8,128)(2,1)}), bf16[4,16,8,128]{3,2,1,0:T(8,128)(2,1)S(1)}, u32[]{:S(2)}, u32[]{:S(2)}) async-start(bf16[4,16,8,128]{3,2,1,0:T(8,128)(2,1)} %broadcast_in_dim.3), calls=%async_computation | async-start | bytes 262144 | tf_op jit(solution)/shard_map/all_to_all | solution.py:144
  9.1 1.6 %copy-done = bf16[16,8,64,64]{3,2,1,0:T(8,128)(2,1)S(1)} copy-done((bf16[16,8,64,64]{3,2,1,0:T(8,128)(2,1)S(1)}, bf16[16,8,64,64]{3,2,1,0:T(8,128)(2,1)}, u32[]{:S(2)}) %copy-start) | copy-done | bytes 1048600
  10.7 3.3 %split_tiles.1 = bf16[8,8,64,128]{3,2,1,0:T(8,128)(2,1)} custom-call(bf16[16,8,64,64]{3,2,1,0:T(8,128)(2,1)S(1)} %copy-done), custom_call_target="tpu_custom_call" | custom-call | flops 268435456 | bytes 3145728 | tf_op jit(solution)/shard_map/split_tiles/pallas_call | solution.py:158
  13.9 2.5 %all-to-all-done = bf16[4,16,8,128]{3,2,1,0:T(8,128)(2,1)S(1)} async-done(((bf16[4,16,8,128]{3,2,1,0:T(8,128)(2,1)}), bf16[4,16,8,128]{3,2,1,0:T(8,128)(2,1)S(1)}, u32[]{:S(2)}, u32[]{:S(2)}) %all-to-all-start) | async-done | bytes 131104 | tf_op jit(solution)/shard_map/all_to_all | solution.py:144
  16.4 10.0 %all-to-all-start.1 = ((bf16[8,8,64,128]{3,2,1,0:T(8,128)(2,1)}), bf16[8,8,64,128]{3,2,1,0:T(8,128)(2,1)S(1)}, u32[]{:S(2)}, u32[]{:S(2)}) async-start(bf16[8,8,64,128]{3,2,1,0:T(8,128)(2,1)} %split_tiles.1), calls=%async_computation.1 | async-start | bytes 2097152 | tf_op jit(solution)/shard_map/all_to_all | solution.py:167
  26.4 2.3 %collective-permute-start = (bf16[64,8,128]{2,1,0:T(8,128)(2,1)S(1)}, bf16[64,8,128]{2,1,0:T(8,128)(2,1)S(1)}, u32[]{:S(2)}, u32[]{:S(2)}) collective-permute-start(bf16[64,8,128]{2,1,0:T(8,128)(2,1)S(1)} %bitcast.2), channel_id=1, source_target_pairs={{0,16},{16,0},{32,48},{48,32},{64,80},{80,64},{96,112},{112,96},{1... | collective-permute-start | bytes 393224 | tf_op jit(solution)/shard_map/ppermute | solution.py:147
  28.8 3.4 %collective-permute-done = bf16[64,8,128]{2,1,0:T(8,128)(2,1)S(1)} collective-permute-done((bf16[64,8,128]{2,1,0:T(8,128)(2,1)S(1)}, bf16[64,8,128]{2,1,0:T(8,128)(2,1)S(1)}, u32[]{:S(2)}, u32[]{:S(2)}) %collective-permute-start) | collective-permute-done | bytes 131104 | tf_op jit(solution)/shard_map/ppermute | solution.py:147
  32.2 4.4 %collective-permute-start.1 = (bf16[128,8,128]{2,1,0:T(8,128)(2,1)S(1)}, bf16[128,8,128]{2,1,0:T(8,128)(2,1)S(1)}, u32[]{:S(2)}, u32[]{:S(2)}) collective-permute-start(bf16[128,8,128]{2,1,0:T(8,128)(2,1)S(1)} %pad_maximum_fusion.1), channel_id=1, source_target_pairs={{128,0},{256,128},{384,256},{0,384},{129,1},{257,129},{385,257},{1... | collective-permute-start | bytes 786440 | tf_op jit(solution)/shard_map/ppermute | solution.py:152
  36.6 2.4 %collective-permute-start.2 = (bf16[128,8,128]{2,1,0:T(8,128)(2,1)S(1)}, bf16[128,8,128]{2,1,0:T(8,128)(2,1)S(1)}, u32[]{:S(2)}, u32[]{:S(2)}) collective-permute-start(bf16[128,8,128]{2,1,0:T(8,128)(2,1)S(1)} %pad_maximum_fusion.1), channel_id=1, source_target_pairs={{256,0},{384,128},{0,256},{128,384},{257,1},{385,129},{1,257},{129... | collective-permute-start | bytes 786440 | tf_op jit(solution)/shard_map/ppermute | solution.py:152
  39.0 2.5 %collective-permute-start.3 = (bf16[128,8,128]{2,1,0:T(8,128)(2,1)S(1)}, bf16[128,8,128]{2,1,0:T(8,128)(2,1)S(1)}, u32[]{:S(2)}, u32[]{:S(2)}) collective-permute-start(bf16[128,8,128]{2,1,0:T(8,128)(2,1)S(1)} %pad_maximum_fusion.1), channel_id=1, source_target_pairs={{384,0},{0,128},{128,256},{256,384},{385,1},{1,129},{129,257},{257... | collective-permute-start | bytes 786440 | tf_op jit(solution)/shard_map/ppermute | solution.py:152
  41.6 9.7 %collective-permute-start.4 = (bf16[256,8,128]{2,1,0:T(8,128)(2,1)S(1)}, bf16[256,8,128]{2,1,0:T(8,128)(2,1)S(1)}, u32[]{:S(2)}, u32[]{:S(2)}) collective-permute-start(bf16[256,8,128]{2,1,0:T(8,128)(2,1)S(1)} %pad_maximum_fusion.refs_0_), channel_id=1, source_target_pairs={{0,8},{8,0},{1,9},{9,1},{2,10},{10,2},{3,11},{11,3},{4,12},{12,4},... | collective-permute-start | bytes 1572872 | tf_op jit(solution)/shard_map/ppermute | solution.py:156
  51.4 4.9 %collective-permute-start.5 = (bf16[256,8,128]{2,1,0:T(8,128)(2,1)S(1)}, bf16[256,8,128]{2,1,0:T(8,128)(2,1)S(1)}, u32[]{:S(2)}, u32[]{:S(2)}) collective-permute-start(bf16[256,8,128]{2,1,0:T(8,128)(2,1)S(1)} %constant_dynamic-update-slice_fusion.refs_1_), channel_id=1, source_target_pairs={{0,8},{8,0},{1,9},{9,1},{2,10},{10,2},{3,11},{11,3},{4,12},{12,4},... | collective-permute-start | bytes 1572872 | tf_op jit(solution)/shard_map/ppermute | solution.py:156
  56.4 4.0 %find.1.where_ref = s32[16,64]{1,0:T(8,128)S(1)} custom-call(s32[1024]{0:T(1024)S(1)} %fusion.9.table_ref, s32[16]{0:T(128)S(1)} %dynamic_slice.6.row_irrep_ref, s32[16,64]{1,0:T(8,128)S(1)} %copy-done.10, bf16[16,64,128]{2,1,0:T(8,128)(2,1)S(1)} %copy-done.9), custom_call_target="tpu_custom_call" | custom-call | flops 268435456 | bytes 1048576 | tf_op jit(solution)/shard_map/find/pallas_call | solution.py:176
  60.4 0.8 copy-done.5
  61.2 0.8 copy-done.7
  62.0 1.0 %copy-done.2 = bf16[256,8,128]{2,1,0:T(8,128)(2,1)S(1)} copy-done((bf16[256,8,128]{2,1,0:T(8,128)(2,1)S(1)}, bf16[256,8,128]{2,1,0:T(8,128)(2,1)}, u32[]{:S(2)}) %copy-start.2) | copy-done | bytes 524312
  63.1 1.0 %copy-done.4 = bf16[256,8,128]{2,1,0:T(8,128)(2,1)S(1)} copy-done((bf16[256,8,128]{2,1,0:T(8,128)(2,1)S(1)}, bf16[256,8,128]{2,1,0:T(8,128)(2,1)}, u32[]{:S(2)}) %copy-start.4) | copy-done | bytes 524312
  64.1 1.0 %copy-done.6 = bf16[256,8,128]{2,1,0:T(8,128)(2,1)S(1)} copy-done((bf16[256,8,128]{2,1,0:T(8,128)(2,1)S(1)}, bf16[256,8,128]{2,1,0:T(8,128)(2,1)}, u32[]{:S(2)}) %copy-start.6) | copy-done | bytes 524312
  65.2 1.0 %copy-done.8 = bf16[256,8,128]{2,1,0:T(8,128)(2,1)S(1)} copy-done((bf16[256,8,128]{2,1,0:T(8,128)(2,1)S(1)}, bf16[256,8,128]{2,1,0:T(8,128)(2,1)}, u32[]{:S(2)}) %copy-start.8) | copy-done | bytes 524312
  66.2 2.0 %pick.1.picked_ref = bf16[8,512,256]{2,1,0:T(8,128)(2,1)S(1)} custom-call(s32[16,64]{1,0:T(8,128)S(1)} %find.1.where_ref, bf16[256,8,128]{2,1,0:T(8,128)(2,1)S(1)} %copy-done.2, bf16[256,8,128]{2,1,0:T(8,128)(2,1)S(1)} %copy-done.4, bf16[256,8,128]{2,1,0:T(8,128)(2,1)S(1)} %copy-done.6, bf16[256,8,128]{2,1,0:T(8,128)(2,1)S(1)} %copy-done.8), custom_call_target="tpu_custom_call" | custom-call | flops 268435456 | bytes 6291456 | tf_op jit(solution)/shard_map/pick/pallas_call | solution.py:187
  68.2 0.8 contract.1
  69.0 15.4 %all_to_all.15.parts_ref = s16[8,9,16,128]{3,2,1,0:T(8,128)(2,1)S(1)} all-to-all(s16[8,9,16,128]{3,2,1,0:T(8,128)(2,1)S(1)} %contract.1), channel_id=1, replica_groups={{4,5,6,7,0,1,2,3},{12,13,14,15,8,9,10,11},{20,21,22,23,16,17,18,19},{28..., dimensions={0} | all-to-all | bytes 589824 | tf_op jit(solution)/shard_map/all_to_all | solution.py:211
  84.4 0.8 add_up.1
  (32 shorter events, 1.0 us)
Async XLA Ops:
  1.4 15.0 %all-to-all-start = ((bf16[4,16,8,128]{3,2,1,0:T(8,128)(2,1)}), bf16[4,16,8,128]{3,2,1,0:T(8,128)(2,1)S(1)}, u32[]{:S(2)}, u32[]{:S(2)}) async-start(bf16[4,16,8,128]{3,2,1,0:T(8,128)(2,1)} %broadcast_in_dim.3), calls=%async_computation | async-start | bytes 262144 | tf_op jit(solution)/shard_map/all_to_all | solution.py:144
  9.1 1.6 %copy-start = (bf16[16,8,64,64]{3,2,1,0:T(8,128)(2,1)S(1)}, bf16[16,8,64,64]{3,2,1,0:T(8,128)(2,1)}, u32[]{:S(2)}) copy-start(bf16[16,8,64,64]{3,2,1,0:T(8,128)(2,1)} %tiles_ref.1) | copy-start | bytes 3145732
  13.9 42.4 %copy-start.11 = (s32[1024]{0:T(1024)S(1)}, s32[1024]{0:T(1024)}, u32[]{:S(2)}) copy-start(s32[1024]{0:T(1024)} %param.9) | copy-start | bytes 12292
  13.9 42.4 %copy-start.12 = (s32[1024]{0:T(1024)S(1)}, s32[1024]{0:T(1024)}, u32[]{:S(2)}) copy-start(s32[1024]{0:T(1024)} %param.6) | copy-start | bytes 12292
  13.9 42.5 %copy-start.9 = (bf16[16,64,128]{2,1,0:T(8,128)(2,1)S(1)}, bf16[16,64,128]{2,1,0:T(8,128)(2,1)}, u32[]{:S(2)}) copy-start(bf16[16,64,128]{2,1,0:T(8,128)(2,1)} %raw_ref.1) | copy-start | bytes 786436
  13.9 42.5 %copy-start.10 = (s32[16,64]{1,0:T(8,128)S(1)}, s32[16,64]{1,0:T(8,128)}, u32[]{:S(2)}) copy-start(s32[16,64]{1,0:T(8,128)} %cols_ref.1) | copy-start | bytes 12292
  16.4 51.8 %all-to-all-start.1 = ((bf16[8,8,64,128]{3,2,1,0:T(8,128)(2,1)}), bf16[8,8,64,128]{3,2,1,0:T(8,128)(2,1)S(1)}, u32[]{:S(2)}, u32[]{:S(2)}) async-start(bf16[8,8,64,128]{3,2,1,0:T(8,128)(2,1)} %split_tiles.1), calls=%async_computation.1 | async-start | bytes 2097152 | tf_op jit(solution)/shard_map/all_to_all | solution.py:167
  26.4 5.7 %collective-permute-start = (bf16[64,8,128]{2,1,0:T(8,128)(2,1)S(1)}, bf16[64,8,128]{2,1,0:T(8,128)(2,1)S(1)}, u32[]{:S(2)}, u32[]{:S(2)}) collective-permute-start(bf16[64,8,128]{2,1,0:T(8,128)(2,1)S(1)} %bitcast.2), channel_id=1, source_target_pairs={{0,16},{16,0},{32,48},{48,32},{64,80},{80,64},{96,112},{112,96},{1... | collective-permute-start | bytes 393224 | tf_op jit(solution)/shard_map/ppermute | solution.py:147
  32.2 9.4 %collective-permute-start.1 = (bf16[128,8,128]{2,1,0:T(8,128)(2,1)S(1)}, bf16[128,8,128]{2,1,0:T(8,128)(2,1)S(1)}, u32[]{:S(2)}, u32[]{:S(2)}) collective-permute-start(bf16[128,8,128]{2,1,0:T(8,128)(2,1)S(1)} %pad_maximum_fusion.1), channel_id=1, source_target_pairs={{128,0},{256,128},{384,256},{0,384},{129,1},{257,129},{385,257},{1... | collective-permute-start | bytes 786440 | tf_op jit(solution)/shard_map/ppermute | solution.py:152
  36.6 14.7 %collective-permute-start.2 = (bf16[128,8,128]{2,1,0:T(8,128)(2,1)S(1)}, bf16[128,8,128]{2,1,0:T(8,128)(2,1)S(1)}, u32[]{:S(2)}, u32[]{:S(2)}) collective-permute-start(bf16[128,8,128]{2,1,0:T(8,128)(2,1)S(1)} %pad_maximum_fusion.1), channel_id=1, source_target_pairs={{256,0},{384,128},{0,256},{128,384},{257,1},{385,129},{1,257},{129... | collective-permute-start | bytes 786440 | tf_op jit(solution)/shard_map/ppermute | solution.py:152
  39.0 12.3 %collective-permute-start.3 = (bf16[128,8,128]{2,1,0:T(8,128)(2,1)S(1)}, bf16[128,8,128]{2,1,0:T(8,128)(2,1)S(1)}, u32[]{:S(2)}, u32[]{:S(2)}) collective-permute-start(bf16[128,8,128]{2,1,0:T(8,128)(2,1)S(1)} %pad_maximum_fusion.1), channel_id=1, source_target_pairs={{384,0},{0,128},{128,256},{256,384},{385,1},{1,129},{129,257},{257... | collective-permute-start | bytes 786440 | tf_op jit(solution)/shard_map/ppermute | solution.py:152
  41.6 18.8 %copy-start.1 = (bf16[256,8,128]{2,1,0:T(8,128)(2,1)}, bf16[256,8,128]{2,1,0:T(8,128)(2,1)S(1)}, u32[]{:S(2)}) copy-start(bf16[256,8,128]{2,1,0:T(8,128)(2,1)S(1)} %pad_maximum_fusion.refs_0_) | copy-start | bytes 1572868
  41.6 18.8 %collective-permute-start.4 = (bf16[256,8,128]{2,1,0:T(8,128)(2,1)S(1)}, bf16[256,8,128]{2,1,0:T(8,128)(2,1)S(1)}, u32[]{:S(2)}, u32[]{:S(2)}) collective-permute-start(bf16[256,8,128]{2,1,0:T(8,128)(2,1)S(1)} %pad_maximum_fusion.refs_0_), channel_id=1, source_target_pairs={{0,8},{8,0},{1,9},{9,1},{2,10},{10,2},{3,11},{11,3},{4,12},{12,4},... | collective-permute-start | bytes 1572872 | tf_op jit(solution)/shard_map/ppermute | solution.py:156
  51.4 9.0 %copy-start.3 = (bf16[256,8,128]{2,1,0:T(8,128)(2,1)}, bf16[256,8,128]{2,1,0:T(8,128)(2,1)S(1)}, u32[]{:S(2)}) copy-start(bf16[256,8,128]{2,1,0:T(8,128)(2,1)S(1)} %constant_dynamic-update-slice_fusion.refs_1_) | copy-start | bytes 1572868
  51.4 9.8 %collective-permute-start.5 = (bf16[256,8,128]{2,1,0:T(8,128)(2,1)S(1)}, bf16[256,8,128]{2,1,0:T(8,128)(2,1)S(1)}, u32[]{:S(2)}, u32[]{:S(2)}) collective-permute-start(bf16[256,8,128]{2,1,0:T(8,128)(2,1)S(1)} %constant_dynamic-update-slice_fusion.refs_1_), channel_id=1, source_target_pairs={{0,8},{8,0},{1,9},{9,1},{2,10},{10,2},{3,11},{11,3},{4,12},{12,4},... | collective-permute-start | bytes 1572872 | tf_op jit(solution)/shard_map/ppermute | solution.py:156
  60.4 0.8 copy-start.5
  61.2 0.8 copy-start.7
  62.0 1.0 %copy-start.2 = (bf16[256,8,128]{2,1,0:T(8,128)(2,1)S(1)}, bf16[256,8,128]{2,1,0:T(8,128)(2,1)}, u32[]{:S(2)}) copy-start(bf16[256,8,128]{2,1,0:T(8,128)(2,1)} %copy-done.1) | copy-start | bytes 1572868
  63.1 1.0 %copy-start.4 = (bf16[256,8,128]{2,1,0:T(8,128)(2,1)S(1)}, bf16[256,8,128]{2,1,0:T(8,128)(2,1)}, u32[]{:S(2)}) copy-start(bf16[256,8,128]{2,1,0:T(8,128)(2,1)} %copy-done.3) | copy-start | bytes 1572868
  64.1 1.0 %copy-start.6 = (bf16[256,8,128]{2,1,0:T(8,128)(2,1)S(1)}, bf16[256,8,128]{2,1,0:T(8,128)(2,1)}, u32[]{:S(2)}) copy-start(bf16[256,8,128]{2,1,0:T(8,128)(2,1)} %copy-done.5) | copy-start | bytes 1572868
  65.2 1.0 %copy-start.8 = (bf16[256,8,128]{2,1,0:T(8,128)(2,1)S(1)}, bf16[256,8,128]{2,1,0:T(8,128)(2,1)}, u32[]{:S(2)}) copy-start(bf16[256,8,128]{2,1,0:T(8,128)(2,1)} %copy-done.7) | copy-start | bytes 1572868
